TPU v7x, 32 devices: a whole 2x2x4 slice. The times are simulated.
32 devices in a mesh: row: 4 (over y, x), col: 8 (over z, core).
Axes of the slice: x: 2, y: 2, z: 4, core: 2. Of those that a mesh axis runs over, the one named last changes fastest.
Arguments:
- features: bfloat16 [16384, 256], P(('col', 'row')), may hold values from -6 to 6
- weight: bfloat16 [256, 256], replicated, may hold values from -0.375 to 0.375
- cotangent: bfloat16 [16384, 256], P(('row', 'col')), may hold values from -6 to 6
- block_index: int32 [4, 8, 32], P('row', 'col'), may hold values from 0 to 511, as said below
- block_count: int32 [4, 8], P('row', 'col'), may hold values from 1 to 32, as said below
- block_values: bfloat16 [4, 8, 32, 128, 128], P('row', 'col'), may hold values from -0.25 to 0.25
Outputs:
- hidden_out: bfloat16 [16384, 256], P(('row', 'col'))
- input_grad: bfloat16 [16384, 256], P(('col', 'row'))
- weight_grad: float32 [256, 256], replicated
Inputs may be any that keep to these rules, and one draw needn't show every extreme that they name: `block_index`: the 32 entries of one tile are distinct; slots at or after the tile's count hold blocks that are not used. `block_count`: at least one tile holds exactly 32 blocks.
All inputs are finite; a program needn't handle non-finite values.
Results may differ from a plain program's by a relative error of at most 0.015.
Values may be sent and summed in bfloat16 or wider, within the bound.
No kernel may reach another device: no remote copies, remote signals or barrier semaphores. Data moves between devices by JAX's collectives and lax.ppermute only.
A program may use at most 64 MiB of HBM per device.

v0:
```python
import math

import jax
import jax.numpy as jnp
from jax import lax
from jax.sharding import PartitionSpec as P

GROUP = 32


def forward_tile(blocks_in, values, index, count, rows_out):
    ncols = blocks_in.shape[0]
    size = blocks_in.shape[1]
    width = blocks_in.shape[2]
    lanes = jnp.arange(GROUP, dtype=jnp.int32)
    targets = jnp.arange(rows_out, dtype=jnp.int32)

    def forward_advance(group_id, totals):
        start = (group_id * GROUP).astype(jnp.int32)
        live = start + lanes < count
        picked = jnp.take(blocks_in, index % ncols, axis=0)
        product = jnp.einsum("gij,gjd->gid", values, picked, preferred_element_type=jnp.float32)
        selector = ((index // ncols)[None, :] == targets[:, None]) & live[None, :]
        return totals + jnp.einsum(
            "rg,gid->rid", selector.astype(jnp.float32), product, precision=lax.Precision.HIGHEST
        )

    zeros = jnp.zeros((rows_out, size, width), jnp.float32)
    groups = (count + GROUP - 1) // GROUP
    return lax.fori_loop(jnp.int32(0), groups, forward_advance, zeros)


def backward_tile(blocks_grad, values, index, count, cols_out):
    size = blocks_grad.shape[1]
    width = blocks_grad.shape[2]
    lanes = jnp.arange(GROUP, dtype=jnp.int32)
    targets = jnp.arange(cols_out, dtype=jnp.int32)

    def backward_advance(group_id, totals):
        start = (group_id * GROUP).astype(jnp.int32)
        live = start + lanes < count
        picked = jnp.take(blocks_grad, index // cols_out, axis=0)
        product = jnp.einsum("gij,gid->gjd", values, picked, preferred_element_type=jnp.float32)
        selector = ((index % cols_out)[None, :] == targets[:, None]) & live[None, :]
        return totals + jnp.einsum(
            "cg,gjd->cjd", selector.astype(jnp.float32), product, precision=lax.Precision.HIGHEST
        )

    zeros = jnp.zeros((cols_out, size, width), jnp.float32)
    groups = (count + GROUP - 1) // GROUP
    return lax.fori_loop(jnp.int32(0), groups, backward_advance, zeros)


def body(features, weight, cotangent, block_index, block_count, block_values):
    row_total = lax.axis_size("row")
    col_total = lax.axis_size("col")
    rows = features.shape[0]
    width = features.shape[1]
    size = block_values.shape[-1]
    block_rows = rows * col_total // size
    block_cols = rows * row_total // size
    index = block_index[0, 0]
    count = block_count[0, 0]
    values = block_values[0, 0]
    gathered = lax.all_gather(features, "row", axis=0, tiled=True)
    projected = jnp.dot(gathered, weight, preferred_element_type=jnp.float32).astype(jnp.bfloat16)
    partial_out = forward_tile(
        projected.reshape(block_cols, size, width), values, index, count, block_rows
    )
    summed_out = lax.psum_scatter(
        partial_out.reshape(block_rows * size, width).astype(jnp.bfloat16),
        "col",
        scatter_dimension=0,
        tiled=True,
    )
    grad_rows = lax.all_gather(cotangent, "col", axis=0, tiled=True)
    partial_back = backward_tile(
        grad_rows.reshape(block_rows, size, width), values, index, count, block_cols
    )
    partial_back = partial_back.reshape(block_cols * size, width)
    grad_sum = lax.psum_scatter(
        partial_back.astype(jnp.bfloat16), "row", scatter_dimension=0, tiled=True
    ).astype(jnp.float32)
    input_grad = jnp.dot(
        grad_sum, weight.astype(jnp.float32).T, precision=lax.Precision.HIGHEST
    ).astype(jnp.bfloat16)
    term = jnp.einsum(
        "nd,ne->de", gathered, partial_back.astype(jnp.bfloat16), preferred_element_type=jnp.float32
    )
    total = lax.psum(term, ("row", "col"))
    nodes = rows * row_total * col_total
    weight_grad = total / math.sqrt(nodes)
    return (summed_out, input_grad, weight_grad)


def solution(mesh):
    in_specs = (
        P(("col", "row"), None),
        P(),
        P(("row", "col"), None),
        P("row", "col", None),
        P("row", "col"),
        P("row", "col", None, None, None),
    )
    out_specs = (P(("row", "col"), None), P(("col", "row"), None), P())
    return jax.shard_map(body, mesh=mesh, in_specs=in_specs, out_specs=out_specs, check_vma=False)
```

profile of v0, /device:TPU:0, one launch (start us, length us, event | category | flops | bytes accessed | tf_op | source)
XLA Modules:
  0.0 277.0 jit_solution(4447913578105518089)
XLA Ops:
  7.2 0.0 copy-start
  7.2 0.0 all-gather.5.cloned.1.call-start
  7.2 0.7 all-gather.5.cloned.1.call-update
  7.9 0.0 all-gather.3.cloned.1.call-start
  8.0 0.7 all-gather.3.cloned.1.call-update
  8.7 0.0 all-reduce.2.cloned.1.call-start
  9.4 0.7 fusion.42
  10.0 0.7 bitcast_sign_fusion.1
  10.7 0.7 negate_bitcast_fusion
  11.4 30.1 %all-gather.5.cloned.1.call-done = bf16[4096,256]{1,0:T(8,128)(2,1)} async-done(((bf16[512,256]{1,0:T(8,128)(2,1)}), bf16[4096,256]{1,0:T(8,128)(2,1)}) %all-gather.5.cloned.1.call-update) | async-done | bytes 2097168 | tf_op jit(solution)/shard_map/all_gather | solution.py:76
  41.5 3.6 %gather_fusion.1 = bf16[32,128,256]{2,1,0:T(8,128)(2,1)} fusion(bf16[32,128,256]{2,1,0:T(8,128)(2,1)} %bitcast.94, s32[1024]{0:T(1024)S(1)} %pad_clamp_fusion.1), kind=kCustom, calls=%fused_computation.1 | custom fusion | bytes 4194432 | tf_op jit(solution)/shard_map/while/body/jit(_take)/gather | solution.py:42
  45.1 0.0 copy-start.3
  45.1 0.2 broadcast_in_dim.63
  45.4 0.4 copy-done.3
  45.8 15.6 %while.34 = (s32[]{:T(128)}, f32[16,128,256]{2,0,1:T(8,128)S(1)}, s32[]{:T(128)}, s32[32]{0:T(128)S(1)}, s32[32]{0:T(128)S(1)}, /*index=5*/s32[]{:T(128)}, s32[3...) while((s32[]{:T(128)}, f32[16,128,256]{2,0,1:T(8,128)S(1)}, ...), condition=%wide.region_4.5_spmd.clone, body=%wide.region_3.4_spmd.clone.sunk | while | flops 471336928 | bytes 24118400 | solution.py:51
  45.8 0.7 compare_and_fusion.4
  46.5 4.6 %fusion.69 = f32[32,256,128]{2,1,0:T(8,128)} fusion(bf16[32,128,128]{2,1,0:T(8,128)(2,1)} %get-tuple-element.889, bf16[32,128,256]{2,1,0:T(8,128)(2,1)} %get-tuple-element.888, pred[32]{0:T(512)(128)(4,1)S(1)} %get-tuple-element.805), kind=kOutput, calls=%fused_computation.7.clone.1 | convolution fusion | flops 269484032 | bytes 7340064 | tf_op jit(solution)/shard_map/while/body/gij,gid->gjd/dot_general | solution.py:43
  51.1 5.5 %copy.20 = f32[32,256,128]{1,0,2:T(8,128)} copy(f32[32,256,128]{2,1,0:T(8,128)} %fusion.69) | data formatting | bytes 8388608 | tf_op jit(solution)/shard_map/while/body/gij,gid->gjd/dot_general | solution.py:43
  56.6 4.8 %fusion.70 = f32[16,128,256]{2,0,1:T(8,128)S(1)} fusion(f32[16,128,256]{2,0,1:T(8,128)S(1)} %get-tuple-element.871, f32[32,256,128]{1,0,2:T(8,128)} %copy.20, s32[32]{0:T(128)S(1)} %and_select_fusion.6, pred[32]{0:T(512)(128)(4,1)S(1)} %get-tuple-element.806), kind=kOutput, calls=%fused_computation.10.clone.1 | convolution fusion | flops 201851904 | bytes 8388768 | tf_op jit(solution)/shard_map/while/body/cg,gjd->cjd/dot_general | solution.py:45
  61.4 1.1 copy.17
  62.6 0.0 copy-start.1
  62.6 6.7 %all-gather.3.cloned.1.call-done = bf16[2048,256]{1,0:T(8,128)(2,1)} async-done(((bf16[512,256]{1,0:T(8,128)(2,1)}), bf16[2048,256]{1,0:T(8,128)(2,1)}) %all-gather.3.cloned.1.call-update) | async-done | bytes 1048592 | tf_op jit(solution)/shard_map/all_gather | solution.py:65
  69.3 0.0 copy-start.2
  69.3 2.5 convolution_bitcast_fusion
  71.8 0.0 all-reduce.2.cloned.1.call-update
  71.8 0.0 copy-done.1
  71.8 0.0 reduce-scatter.5.cloned.1.call-start
  71.8 0.0 copy-done
  71.8 0.0 copy-done.2
  71.9 0.4 convolution_convert_fusion
  72.3 0.1 reduce-scatter.5.cloned.1.call-update
  72.4 0.0 reduce-scatter.3.cloned.1.call-start
  72.4 2.5 broadcast_in_dim.62
  74.9 18.6 %while.35 = (s32[]{:T(128)}, f32[32,128,256]{2,0,1:T(8,128)}, s32[]{:T(128)}, s32[1,32]{1,0:T(1,128)S(1)}, s32[32]{0:T(128)S(1)}, /*index=5*/s32[1,32]{1,0:T(1,1...) while((s32[]{:T(128)}, f32[32,128,256]{2,0,1:T(8,128)}, ...), condition=%wide.region_1.2_spmd.clone.clone, body=%wide.region_0.1_spmd.clone.clone.sunk | while | flops 673190272 | bytes 32511760 | solution.py:30
  74.9 0.7 compare_and_fusion.5
  75.6 0.7 gather_fusion
  76.3 4.0 %fusion.76 = f32[32,256,128]{2,1,0:T(8,128)} fusion(bf16[32,128,128]{2,1,0:T(8,128)(2,1)} %get-tuple-element.856, bf16[32,128,256]{2,1,0:T(8,128)(2,1)S(1)} %gather_fusion, pred[32]{0:T(512)(128)(4,1)S(1)} %get-tuple-element.818), kind=kOutput, calls=%fused_computation.30.clone.1 | convolution fusion | flops 269484032 | bytes 7340064 | tf_op jit(solution)/shard_map/while/body/gij,gjd->gid/dot_general | solution.py:22
  80.3 5.5 %copy.21 = f32[32,256,128]{1,0,2:T(8,128)} copy(f32[32,256,128]{2,1,0:T(8,128)} %fusion.76) | data formatting | bytes 8388608 | tf_op jit(solution)/shard_map/while/body/gij,gjd->gid/dot_general | solution.py:22
  85.8 7.7 %fusion.78 = f32[32,128,256]{2,0,1:T(8,128)} fusion(f32[32,128,256]{2,0,1:T(8,128)} %get-tuple-element.834, f32[32,256,128]{1,0,2:T(8,128)} %copy.21, s32[32]{0:T(128)S(1)} %fusion.77, pred[32]{0:T(512)(128)(4,1)S(1)} %get-tuple-element.819), kind=kOutput, calls=%fused_computation.29.clone.1 | convolution fusion | flops 403703808 | bytes 12583072 | tf_op jit(solution)/shard_map/while/body/rg,gid->rid/dot_general | solution.py:24
  93.5 2.5 convert_element_type.25
  96.0 2.5 copy.11
  98.6 0.0 reduce-scatter.3.cloned.1.call-update
  98.6 103.3 %all-reduce.2.cloned.1.call-done = f32[256,256]{0,1:T(8,128)} async-done(((f32[256,256]{0,1:T(8,128)}), f32[256,256]{0,1:T(8,128)}) %all-reduce.2.cloned.1.call-update) | async-done | bytes 262160 | tf_op jit(solution)/shard_map/psum | solution.py:90
  201.9 1.0 broadcast_multiply_fusion
  202.9 0.8 copy.13
  203.7 27.9 %reduce-scatter.5.cloned.1.call-done = bf16[512,256]{1,0:T(8,128)(2,1)} async-done(((bf16[2048,256]{1,0:T(8,128)(2,1)}), bf16[512,256]{1,0:T(8,128)(2,1)}) %reduce-scatter.5.cloned.1.call-update) | async-done | bytes 262160 | tf_op jit(solution)/shard_map/reduce_scatter | solution.py:81
  231.7 1.9 convolution_convert_fusion.1
  233.6 36.9 %reduce-scatter.3.cloned.1.call-done = bf16[512,256]{1,0:T(8,128)(2,1)} async-done(((bf16[4096,256]{1,0:T(8,128)(2,1)}), bf16[512,256]{1,0:T(8,128)(2,1)}) %reduce-scatter.3.cloned.1.call-update) | async-done | bytes 262160 | tf_op jit(solution)/shard_map/reduce_scatter | solution.py:70
  (5 shorter events, 0.0 us)
Async XLA Ops:
  7.2 64.7 %copy-start = (bf16[256,256]{1,0:T(8,128)(2,1)S(1)}, bf16[256,256]{1,0:T(8,128)(2,1)}, u32[]{:S(2)}) copy-start(bf16[256,256]{1,0:T(8,128)(2,1)} %param.11) | copy-start | bytes 393220
  7.2 34.3 %all-gather.5.cloned.1.call-start = ((), (), s32[]{:S(2)}) async-start(), calls=%async_computation.4 | async-start | bytes 2359296 | tf_op jit(solution)/shard_map/all_gather | solution.py:76
  7.9 61.3 %all-gather.3.cloned.1.call-start = ((), (), s32[]{:S(2)}) async-start(), calls=%async_computation.2 | async-start | bytes 1310720 | tf_op jit(solution)/shard_map/all_gather | solution.py:65
  8.7 193.3 %all-reduce.2.cloned.1.call-start = ((), (), s32[]{:S(2)}) async-start(), calls=%async_computation.6 | async-start | bytes 524288 | tf_op jit(solution)/shard_map/psum | solution.py:90
  45.1 0.7 copy-start.3
  62.6 9.2 %copy-start.1 = (bf16[16,128,256]{2,1,0:T(8,128)(2,1)}, bf16[16,128,256]{2,1,0:T(8,128)(2,1)S(1)}, u32[]{:S(2)}) copy-start(bf16[16,128,256]{2,1,0:T(8,128)(2,1)S(1)} %copy.17) | copy-start | bytes 3145732
  69.3 2.6 copy-start.2
  71.8 159.9 %reduce-scatter.5.cloned.1.call-start = ((), (), s32[]{:S(2)}) async-start(), calls=%async_computation.5 | async-start | bytes 1310720 | tf_op jit(solution)/shard_map/reduce_scatter | solution.py:81
  72.4 198.1 %reduce-scatter.3.cloned.1.call-start = ((), (), s32[]{:S(2)}) async-start(), calls=%async_computation.3 | async-start | bytes 2359296 | tf_op jit(solution)/shard_map/reduce_scatter | solution.py:70
Sparse Core Ops, SparseCore 0:
  9.6 31.8 all-gather.4
  43.3 25.8 all-gather.2
  75.3 126.5 all-reduce.1
  204.7 26.9 reduce-scatter.4
  234.4 36.0 reduce-scatter.2
where the time goes:
time: 278 us; the launch traced here: 277 us
  waiting for transfers between devices  206 us (74%)
  matrix products  26 us (9%)
  local copies, waits for them, and re-layouts  22.9 us (8%)
  between operations  14.5 us (5%)
  other arithmetic  6.83 us (2%)
    psum x1, waiting for transfers between devices, body(): total = lax.psum(term, ('row', 'col'))  103 us
    reduce_scatter x1, waiting for transfers between devices, body(): lax.psum_scatter(partial_out.reshape(block_rows * size, width).astype(jnp...  36.9 us
    all_gather x1, waiting for transfers between devices, body(): grad_rows = lax.all_gather(cotangent, 'col', axis=0, tiled=True)  30.1 us
    reduce_scatter x1, waiting for transfers between devices, body(): lax.psum_scatter(partial_back.astype(jnp.bfloat16), 'row', scatter_dimens...  27.9 us
    dot_general x1, matrix products, forward_advance(): jnp.einsum('rg,gid->rid', selector.astype(jnp.float32), product, precisio...  7.68 us
    all_gather x1, waiting for transfers between devices, body(): gathered = lax.all_gather(features, 'row', axis=0, tiled=True)  6.68 us
  transfers between devices with their start and end apart: 5, of which 5 were waited for; matrix products, arithmetic and copies ran while one was open for 19% of the time, Pallas kernels for 0%

commit v1 on v0

v1 whole, which is shorter than its diff:
```python
import functools
import math

import jax
import jax.numpy as jnp
from jax import lax
from jax.experimental import pallas as pl
from jax.experimental.pallas import tpu as pltpu
from jax.sharding import PartitionSpec as P


AXES = ("row", "col")
F32 = jnp.float32
BF16 = jnp.bfloat16
UNROLL = 4
ANY = pl.BlockSpec(memory_space=pl.ANY)
VMEM = pl.BlockSpec(memory_space=pltpu.VMEM)
SMEM = pl.BlockSpec(memory_space=pltpu.SMEM)


def move(x, rows, cols, fn):
    pairs = []
    for r in range(rows):
        for c in range(cols):
            to = fn(r, c)
            if to is not None:
                pairs.append((r * cols + c, to[0] * cols + to[1]))
    return lax.ppermute(x, AXES, pairs)


def fwd_kernel(nrow, ncol, idx0, idx1, cnt0, cnt1, vals0, vals1, *rest):
    shards = rest[:2 * nrow]
    zs = ncol // 2
    outs = rest[2 * nrow:2 * nrow + zs]
    vbuf, fbuf, acc, todo, sem = rest[2 * nrow + zs:]
    slots, size = vals0.shape[0], vals0.shape[1]
    rows, _ = shards[0].shape
    per = rows // size
    block_cols = nrow * per
    full = zs * rows
    me_r = lax.axis_index("row")
    me_c = lax.axis_index("col")
    me_z, me_k = me_c // 2, me_c % 2
    copies = []
    for t, vals in enumerate((vals0, vals1)):
        copies.append(pltpu.make_async_copy(vals, vbuf.at[pl.ds(t * slots, slots)], sem.at[2 * nrow + t]))
        for s in range(nrow):
            at = pl.multiple_of((me_r ^ s) * rows + t * nrow * rows, rows)
            n = t * nrow + s
            copies.append(pltpu.make_async_copy(shards[n], fbuf.at[pl.ds(at, rows)], sem.at[n]))
    for copy in copies:
        copy.start()
    acc[...] = jnp.zeros_like(acc)

    def listed(t, idx, cnt, n):
        def one(g, n):
            q = idx[g]
            br, bc = q // block_cols, q % block_cols
            owner = br // per
            todo[0, n] = t * slots + g
            todo[1, n] = t * nrow * rows + bc * size
            todo[2, n] = ((owner // 2) ^ me_z) * rows + (br % per) * size
            return n + jnp.where(owner % 2 == me_k, 1, 0)

        return lax.fori_loop(0, cnt[0], one, n)

    count = listed(1, idx1, cnt1, listed(0, idx0, cnt0, 0))
    for u in range(UNROLL):
        todo[0, count + u] = 0
        todo[1, count + u] = 0
        todo[2, count + u] = full
    for copy in copies:
        copy.wait()

    def group(i, carry):
        prods = []
        for u in range(UNROLL):
            g = i * UNROLL + u
            block = fbuf[pl.ds(pl.multiple_of(todo[1, g], size), size), :]
            prods.append((pl.multiple_of(todo[2, g], size), jnp.dot(vbuf[todo[0, g]], block, preferred_element_type=F32)))
        for at, out in prods:
            acc[pl.ds(at, size), :] += out
        return carry

    lax.fori_loop(0, (count + UNROLL - 1) // UNROLL, group, 0)
    for s in range(zs):
        outs[s][...] = acc[s * rows:(s + 1) * rows, :].astype(BF16)


def bwd_kernel(nrow, ncol, idx, cnt, vals, *rest):
    feats = rest[:nrow]
    cots = rest[nrow:nrow + ncol]
    outs = rest[nrow + ncol:2 * nrow + ncol]
    tkeep, tsend, vbuf, fbuf, cbuf, acc, tbuf, sem = rest[2 * nrow + ncol:]
    size = vals.shape[1]
    rows, width = feats[0].shape
    per = rows // size
    block_cols = nrow * per
    full = nrow * rows
    me_r = lax.axis_index("row")
    me_c = lax.axis_index("col")
    me_k = me_c % 2
    copies = [pltpu.make_async_copy(vals, vbuf, sem.at[nrow + ncol])]
    for s in range(nrow):
        copies.append(pltpu.make_async_copy(feats[s], fbuf.at[pl.ds(s * rows, rows)], sem.at[s]))
    for s in range(ncol):
        at = pl.multiple_of((me_c ^ s) * rows, rows)
        copies.append(pltpu.make_async_copy(cots[s], cbuf.at[pl.ds(at, rows)], sem.at[nrow + s]))
    for copy in copies:
        copy.start()
    acc[...] = jnp.zeros_like(acc)
    for copy in copies:
        copy.wait()
    count = cnt[0]

    def group(i, carry):
        prods = []
        for u in range(UNROLL):
            g = i * UNROLL + u
            q = idx[g]
            br, bc = q // block_cols, q % block_cols
            at = ((bc // per) ^ me_r) * rows + (bc % per) * size
            at = pl.multiple_of(jnp.where(g < count, at, full), size)
            block = cbuf[pl.ds(pl.multiple_of(br * size, size), size), :]
            prods.append((at, lax.dot_general(vbuf[g], block, (((0,), (0,)), ((), ())), preferred_element_type=F32)))
        for at, out in prods:
            acc[pl.ds(at, size), :] += out
        return carry

    lax.fori_loop(0, (count + UNROLL - 1) // UNROLL, group, 0)
    term = jnp.zeros((width, width), F32)
    for s in range(nrow):
        back = acc[s * rows:(s + 1) * rows, :].astype(BF16)
        outs[s][...] = back
        term += lax.dot_general(
            fbuf[s * rows:(s + 1) * rows, :], back, (((0,), (0,)), ((), ())), preferred_element_type=F32
        )
    tbuf[...] = term
    part = width // 2
    tkeep[...] = tbuf[pl.ds(pl.multiple_of(me_k * part, part), part), :].astype(BF16)
    tsend[...] = tbuf[pl.ds(pl.multiple_of((1 - me_k) * part, part), part), :].astype(BF16)


def split_dot(x, w, dims):
    hi = x.astype(BF16)
    lo = (x - hi.astype(F32)).astype(BF16)
    return lax.dot_general(hi, w, dims, preferred_element_type=F32) + lax.dot_general(
        lo, w, dims, preferred_element_type=F32
    )


def sum_dot_kernel(parts, dims, w, *rest):
    total = rest[0][...].astype(F32)
    for s in range(1, parts):
        total += rest[s][...].astype(F32)
    rest[parts][...] = split_dot(total, w[...], dims).astype(BF16)


def join_kernel(nodes, mine, other, out):
    part = mine.shape[0]
    me_k = lax.axis_index("col") % 2
    out[pl.ds(pl.multiple_of(me_k * part, part), part), :] = mine[...].astype(F32) / math.sqrt(nodes)
    out[pl.ds(pl.multiple_of((1 - me_k) * part, part), part), :] = other[...].astype(F32) / math.sqrt(nodes)


def bits(n):
    return [1 << b for b in range(n.bit_length() - 1)]


def body(features, weight, cotangent, block_index, block_count, block_values):
    nrow, ncol = lax.axis_size("row"), lax.axis_size("col")
    rows, width = features.shape
    size = block_values.shape[-1]
    slots = block_values.shape[2]
    zs = ncol // 2
    part = width // 2
    shape = jax.ShapeDtypeStruct

    def over_row(x, s):
        return move(x, nrow, ncol, lambda r, c: (r ^ s, c))

    def over_col(x, s):
        return move(x, nrow, ncol, lambda r, c: (r, c ^ s))

    idx = block_index.reshape(slots)
    cnt = block_count.reshape(1)
    vals = block_values.reshape(slots, size, size)
    vals1 = over_col(vals, 1)
    idx1 = over_col(idx, 1)
    cnt1 = over_col(cnt, 1)
    cots = [cotangent, over_col(cotangent, 1)]
    feats = [features] + [over_row(features, s) for s in range(1, nrow)]
    for s in range(1, zs):
        got = over_col(cotangent, 2 * s)
        cots += [got, over_col(got, 1)]
    feats1 = [over_col(feats[s], 1) for s in range(nrow)]

    parts = pl.pallas_call(
        functools.partial(fwd_kernel, nrow, ncol),
        out_shape=[shape((rows, width), BF16)] * zs,
        in_specs=[SMEM] * 4 + [ANY] * (2 + 2 * nrow),
        out_specs=[VMEM] * zs,
        scratch_shapes=[
            pltpu.VMEM((2 * slots, size, size), BF16),
            pltpu.VMEM((2 * nrow * rows, width), BF16),
            pltpu.VMEM((zs * rows + size, width), F32),
            pltpu.SMEM((3, 2 * slots + UNROLL), jnp.int32),
            pltpu.SemaphoreType.DMA((2 * nrow + 2,)),
        ],
        compiler_params=pltpu.CompilerParams(vmem_limit_bytes=16 << 20),
        name="fwd_tile",
    )(idx, idx1, cnt, cnt1, vals, vals1, *feats, *feats1)
    parts = [parts[0]] + [over_col(parts[s], 2 * s) for s in range(1, zs)]
    hidden = pl.pallas_call(
        functools.partial(sum_dot_kernel, zs, (((1,), (0,)), ((), ()))),
        out_shape=shape((rows, width), BF16),
        in_specs=[VMEM] * (1 + zs),
        out_specs=VMEM,
        compiler_params=pltpu.CompilerParams(vmem_limit_bytes=8 << 20),
        name="hidden",
    )(weight, *parts)

    out = pl.pallas_call(
        functools.partial(bwd_kernel, nrow, ncol),
        out_shape=[shape((rows, width), BF16)] * nrow + [shape((part, width), BF16)] * 2,
        in_specs=[SMEM, SMEM] + [ANY] * (1 + nrow + ncol),
        out_specs=[VMEM] * (nrow + 2),
        scratch_shapes=[
            pltpu.VMEM((slots, size, size), BF16),
            pltpu.VMEM((nrow * rows, width), BF16),
            pltpu.VMEM((ncol * rows, width), BF16),
            pltpu.VMEM((nrow * rows + size, width), F32),
            pltpu.VMEM((width, width), F32),
            pltpu.SemaphoreType.DMA((nrow + ncol + 1,)),
        ],
        compiler_params=pltpu.CompilerParams(vmem_limit_bytes=16 << 20),
        name="bwd_tile",
    )(idx, cnt, vals, *feats, *cots)
    backs, term, send = out[:nrow], out[nrow], out[nrow + 1]
    backs = [backs[0]] + [over_row(backs[s], s) for s in range(1, nrow)]
    input_grad = pl.pallas_call(
        functools.partial(sum_dot_kernel, nrow, (((1,), (1,)), ((), ()))),
        out_shape=shape((rows, width), BF16),
        in_specs=[VMEM] * (1 + nrow),
        out_specs=VMEM,
        compiler_params=pltpu.CompilerParams(vmem_limit_bytes=8 << 20),
        name="input_grad",
    )(weight, *backs)

    term = term + over_col(send, 1)
    for s in bits(nrow):
        term = term + over_row(term, s)
    for s in bits(zs):
        term = term + over_col(term, 2 * s)
    weight_grad = pl.pallas_call(
        functools.partial(join_kernel, rows * nrow * ncol),
        out_shape=shape((width, width), F32),
        in_specs=[VMEM, VMEM],
        out_specs=VMEM,
        compiler_params=pltpu.CompilerParams(vmem_limit_bytes=8 << 20),
        name="weight_grad",
    )(term, over_col(term, 1))
    return (hidden, input_grad, weight_grad)


def solution(mesh):
    in_specs = (
        P(("col", "row"), None),
        P(),
        P(("row", "col"), None),
        P("row", "col", None),
        P("row", "col"),
        P("row", "col", None, None, None),
    )
    out_specs = (P(("row", "col"), None), P(("col", "row"), None), P())

    return jax.shard_map(body, mesh=mesh, in_specs=in_specs, out_specs=out_specs, check_vma=False)
```

time: 278 us -> 91.6 us (0.33)
  waiting for transfers between devices: 206 us -> 42.1 us
  starting transfers between devices: 0.2 us -> 31.8 us
  matrix products: 26 us -> 0 us
  local copies, waits for them, and re-layouts: 22.9 us -> 3.79 us
  between operations: 14.5 us -> 1.46 us
  Pallas kernels: 0 us -> 10.9 us
  other arithmetic: 6.83 us -> 0.09 us
    psum x1 -> x0, waiting for transfers between devices: 103 us -> none  [body(): total = lax.psum(term, ('row', 'col'))]
    reduce_scatter x2 -> x0, waiting for transfers between devices: 64.8 us -> none  [the longest x1 36.9 us: body(): lax.psum_scatter(partial_out.reshape(block_rows * size, width).astype(jnp...]
    ppermute x0 -> x29, waiting for transfers between devices: none -> 42.1 us  [move(): return lax.ppermute(x, AXES, pairs)]
    all_gather x2 -> x0, waiting for transfers between devices: 36.8 us -> none  [the longest x1 30.1 us: body(): grad_rows = lax.all_gather(cotangent, 'col', axis=0, tiled=True)]
    ppermute x0 -> x29, starting transfers between devices: none -> 31.8 us  [move(): return lax.ppermute(x, AXES, pairs)]
    dot_general x7 -> x0, matrix products: 26 us -> none  [the longest x1 7.68 us: forward_advance(): jnp.einsum('rg,gid->rid', selector.astype(jnp.float32), product, precisio...]
    dot_general x2 -> x0, local copies, waits for them, and re-layouts: 11 us -> none  [the longest x1 5.49 us: forward_advance(): jnp.einsum('gij,gjd->gid', values, picked, preferred_element_type=jnp.flo...]
    pallas_call x0 -> x5, Pallas kernels: none -> 10.9 us  [the longest x1 4.32 us: body(): pl.pallas_call(functools.partial(fwd_kernel, nrow, ncol), out_shape=[shap...]
  transfers between devices with their start and end apart: 5 -> 29, of which waited for: 5 -> 13; matrix products, arithmetic and copies ran while one was open for 19% -> 0% of each run, Pallas kernels for 0% -> 11%
where the time goes in v1:
time: 91.6 us; the launch traced here: 90.2 us
  waiting for transfers between devices  42.1 us (46%)
  starting transfers between devices  31.8 us (35%)
  Pallas kernels  10.9 us (12%)
  local copies, waits for them, and re-layouts  3.79 us (4%)
  between operations  1.46 us (2%)
    ppermute x29, waiting for transfers between devices, move(): return lax.ppermute(x, AXES, pairs)  42.1 us
    ppermute x29, starting transfers between devices, move(): return lax.ppermute(x, AXES, pairs)  31.8 us
    pallas_call x1, Pallas kernels, body(): pl.pallas_call(functools.partial(fwd_kernel, nrow, ncol), out_shape=[shap...  4.32 us
    unnamed x12, local copies, waits for them, and re-layouts  3.79 us
    pallas_call x1, Pallas kernels, body(): pl.pallas_call(functools.partial(bwd_kernel, nrow, ncol), out_shape=[shap...  3.78 us
  transfers between devices with their start and end apart: 29, of which 13 were waited for; matrix products, arithmetic and copies ran while one was open for 0% of the time, Pallas kernels for 11%

profile of v1, /device:TPU:0, one launch (start us, length us, event | category | flops | bytes accessed | tf_op | source)
XLA Modules:
  0.0 90.2 jit_solution(2434071220497583708)
XLA Ops:
  0.6 3.0 %collective-permute-start.3 = (bf16[512,256]{1,0:T(8,128)(2,1)}, bf16[512,256]{1,0:T(8,128)(2,1)S(1)}, u32[]{:S(2)}, u32[]{:S(2)}) collective-permute-start(bf16[512,256]{1,0:T(8,128)(2,1)} %rest_0_.3), channel_id=1, source_target_pairs={{0,8},{1,9},{2,10},{3,11},{4,12},{5,13},{6,14},{7,15},{8,0},{9,1},... | collective-permute-start | bytes 786440 | tf_op jit(solution)/shard_map/ppermute | solution.py:28
  3.7 1.5 %collective-permute-start.4 = (bf16[512,256]{1,0:T(8,128)(2,1)}, bf16[512,256]{1,0:T(8,128)(2,1)S(1)}, u32[]{:S(2)}, u32[]{:S(2)}) collective-permute-start(bf16[512,256]{1,0:T(8,128)(2,1)} %rest_0_.3), channel_id=1, source_target_pairs={{0,16},{1,17},{2,18},{3,19},{4,20},{5,21},{6,22},{7,23},{8,24},{9,... | collective-permute-start | bytes 786440 | tf_op jit(solution)/shard_map/ppermute | solution.py:28
  5.2 0.0 collective-permute-start.5
  5.2 2.0 %collective-permute-start.14 = (bf16[512,256]{1,0:T(8,128)(2,1)}, bf16[512,256]{1,0:T(8,128)(2,1)S(1)}, u32[]{:S(2)}, u32[]{:S(2)}) collective-permute-start(bf16[512,256]{1,0:T(8,128)(2,1)} %rest_4_.1), channel_id=1, source_target_pairs={{0,2},{1,3},{2,0},{3,1},{4,6},{5,7},{6,4},{7,5},{8,10},{9,11},{10,... | collective-permute-start | bytes 786440 | tf_op jit(solution)/shard_map/ppermute | solution.py:28
  7.2 3.8 %collective-permute-done.3.rest_1_ = bf16[512,256]{1,0:T(8,128)(2,1)S(1)} collective-permute-done((bf16[512,256]{1,0:T(8,128)(2,1)}, bf16[512,256]{1,0:T(8,128)(2,1)S(1)}, u32[]{:S(2)}, u32[]{:S(2)}) %collective-permute-start.3) | collective-permute-done | bytes 262176 | tf_op jit(solution)/shard_map/ppermute | solution.py:28
  11.0 3.1 %collective-permute-start.16 = (bf16[512,256]{1,0:T(8,128)(2,1)}, bf16[512,256]{1,0:T(8,128)(2,1)S(1)}, u32[]{:S(2)}, u32[]{:S(2)}) collective-permute-start(bf16[512,256]{1,0:T(8,128)(2,1)} %rest_4_.1), channel_id=1, source_target_pairs={{0,4},{1,5},{2,6},{3,7},{4,0},{5,1},{6,2},{7,3},{8,12},{9,13},{10,... | collective-permute-start | bytes 786440 | tf_op jit(solution)/shard_map/ppermute | solution.py:28
  14.1 3.1 %collective-permute-done.4.rest_2_ = bf16[512,256]{1,0:T(8,128)(2,1)S(1)} collective-permute-done((bf16[512,256]{1,0:T(8,128)(2,1)}, bf16[512,256]{1,0:T(8,128)(2,1)S(1)}, u32[]{:S(2)}, u32[]{:S(2)}) %collective-permute-start.4) | collective-permute-done | bytes 262176 | tf_op jit(solution)/shard_map/ppermute | solution.py:28
  17.3 3.6 %collective-permute-start.18 = (bf16[512,256]{1,0:T(8,128)(2,1)}, bf16[512,256]{1,0:T(8,128)(2,1)S(1)}, u32[]{:S(2)}, u32[]{:S(2)}) collective-permute-start(bf16[512,256]{1,0:T(8,128)(2,1)} %rest_4_.1), channel_id=1, source_target_pairs={{0,6},{1,7},{2,4},{3,5},{4,2},{5,3},{6,0},{7,1},{8,14},{9,15},{10,... | collective-permute-start | bytes 786440 | tf_op jit(solution)/shard_map/ppermute | solution.py:28
  20.9 0.0 collective-permute-done.5.rest_3_
  20.9 0.0 collective-permute-start.13
  20.9 0.5 collective-permute-start.15
  21.4 11.4 %collective-permute-done.16.rest_8_ = bf16[512,256]{1,0:T(8,128)(2,1)S(1)} collective-permute-done((bf16[512,256]{1,0:T(8,128)(2,1)}, bf16[512,256]{1,0:T(8,128)(2,1)S(1)}, u32[]{:S(2)}, u32[]{:S(2)}) %collective-permute-start.16) | collective-permute-done | bytes 262176 | tf_op jit(solution)/shard_map/ppermute | solution.py:28
  32.8 0.5 collective-permute-start.19
  33.3 0.1 collective-permute-start.6
  34.0 0.3 collective-permute-done.17.rest_9_
  34.3 0.4 collective-permute-done.19.rest_11_
  34.7 0.7 copy-done.5
  35.3 1.2 %copy-done = bf16[1,1,32,128,128]{4,3,2,1,0:T(8,128)(2,1)S(1)} copy-done((bf16[1,1,32,128,128]{4,3,2,1,0:T(8,128)(2,1)S(1)}, bf16[1,1,32,128,128]{4,3,2,1,0:T(8,128)(2,1)}, u32[]{:S(2)}) %copy-start) | copy-done | bytes 1048600
  36.5 0.9 %copy-done.2 = bf16[512,256]{1,0:T(8,128)(2,1)S(1)} copy-done((bf16[512,256]{1,0:T(8,128)(2,1)S(1)}, bf16[512,256]{1,0:T(8,128)(2,1)}, u32[]{:S(2)}) %copy-start.2) | copy-done | bytes 262168
  37.5 0.9 %copy-done.4 = bf16[512,256]{1,0:T(8,128)(2,1)S(1)} copy-done((bf16[512,256]{1,0:T(8,128)(2,1)S(1)}, bf16[512,256]{1,0:T(8,128)(2,1)}, u32[]{:S(2)}) %copy-start.4) | copy-done | bytes 262168
  38.4 3.8 %bwd_tile.1 = (bf16[512,256]{1,0:T(8,128)(2,1)S(1)}, bf16[512,256]{1,0:T(8,128)(2,1)S(1)}, bf16[512,256]{1,0:T(8,128)(2,1)S(1)}, bf16[512,256]{1,0:T(8,128)(2,1)...) custom-call(s32[32]{0:T(128)S(1)} %bitcast.8, s32[1]{0:T(128)} %bitcast.4.cnt, ...), custom_call_target="tpu_custom_call" | custom-call | tf_op jit(solution)/shard_map/bwd_tile/pallas_call | solution.py:223
  42.2 0.1 collective-permute-start.23
  42.3 1.2 %collective-permute-done.23 = bf16[128,256]{1,0:T(8,128)(2,1)S(1)} collective-permute-done((bf16[128,256]{1,0:T(8,128)(2,1)S(1)}, bf16[128,256]{1,0:T(8,128)(2,1)S(1)}, u32[]{:S(2)}, u32[]{:S(2)}) %collective-permute-start.23) | collective-permute-done | bytes 65568 | tf_op jit(solution)/shard_map/ppermute | solution.py:28
  43.6 0.8 collective-permute-start.24
  44.4 0.5 collective-permute-start.1
  44.9 3.0 %collective-permute-done.24 = bf16[128,256]{1,0:T(8,128)(2,1)S(1)} collective-permute-done((bf16[128,256]{1,0:T(8,128)(2,1)S(1)}, bf16[128,256]{1,0:T(8,128)(2,1)S(1)}, u32[]{:S(2)}, u32[]{:S(2)}) %collective-permute-start.24) | collective-permute-done | bytes 65568 | tf_op jit(solution)/shard_map/ppermute | solution.py:28
  47.9 0.5 collective-permute-start.25
  48.4 1.2 %collective-permute-done.idx1 = s32[32]{0:T(128)S(1)} collective-permute-done((s32[32]{0:T(128)S(1)}, s32[32]{0:T(128)S(1)}, u32[]{:S(2)}, u32[]{:S(2)}) %collective-permute-start) | collective-permute-done | bytes 160 | tf_op jit(solution)/shard_map/ppermute | solution.py:28
  49.6 0.2 collective-permute-start.8
  49.8 0.3 collective-permute-start.9
  50.1 2.1 %collective-permute-done.25 = bf16[128,256]{1,0:T(8,128)(2,1)S(1)} collective-permute-done((bf16[128,256]{1,0:T(8,128)(2,1)S(1)}, bf16[128,256]{1,0:T(8,128)(2,1)S(1)}, u32[]{:S(2)}, u32[]{:S(2)}) %collective-permute-start.25) | collective-permute-done | bytes 65568 | tf_op jit(solution)/shard_map/ppermute | solution.py:28
  52.3 0.8 collective-permute-start.20
  53.1 3.0 %collective-permute-start.26 = (bf16[128,256]{1,0:T(8,128)(2,1)S(1)}, bf16[128,256]{1,0:T(8,128)(2,1)S(1)}, u32[]{:S(2)}, u32[]{:S(2)}) collective-permute-start(bf16[128,256]{1,0:T(8,128)(2,1)S(1)} %add.17), channel_id=1, source_target_pairs={{0,2},{1,3},{2,0},{3,1},{4,6},{5,7},{6,4},{7,5},{8,10},{9,11},{10,... | collective-permute-start | bytes 196616 | tf_op jit(solution)/shard_map/ppermute | solution.py:28
  56.0 2.2 %collective-permute-done.26 = bf16[128,256]{1,0:T(8,128)(2,1)S(1)} collective-permute-done((bf16[128,256]{1,0:T(8,128)(2,1)S(1)}, bf16[128,256]{1,0:T(8,128)(2,1)S(1)}, u32[]{:S(2)}, u32[]{:S(2)}) %collective-permute-start.26) | collective-permute-done | bytes 65568 | tf_op jit(solution)/shard_map/ppermute | solution.py:28
  58.3 1.5 %collective-permute-start.21 = (bf16[512,256]{1,0:T(8,128)(2,1)S(1)}, bf16[512,256]{1,0:T(8,128)(2,1)S(1)}, u32[]{:S(2)}, u32[]{:S(2)}) collective-permute-start(bf16[512,256]{1,0:T(8,128)(2,1)S(1)} %get-tuple-element.19), channel_id=1, source_target_pairs={{0,16},{1,17},{2,18},{3,19},{4,20},{5,21},{6,22},{7,23},{8,24},{9,... | collective-permute-start | bytes 786440 | tf_op jit(solution)/shard_map/ppermute | solution.py:28
  59.8 5.3 %collective-permute-start.27 = (bf16[128,256]{1,0:T(8,128)(2,1)S(1)}, bf16[128,256]{1,0:T(8,128)(2,1)S(1)}, u32[]{:S(2)}, u32[]{:S(2)}) collective-permute-start(bf16[128,256]{1,0:T(8,128)(2,1)S(1)} %add.18), channel_id=1, source_target_pairs={{0,4},{1,5},{2,6},{3,7},{4,0},{5,1},{6,2},{7,3},{8,12},{9,13},{10,... | collective-permute-start | bytes 196616 | tf_op jit(solution)/shard_map/ppermute | solution.py:28
  65.1 4.3 %fwd_tile.1 = (bf16[512,256]{1,0:T(8,128)(2,1)S(1)}, bf16[512,256]{1,0:T(8,128)(2,1)S(1)}, bf16[512,256]{1,0:T(8,128)(2,1)S(1)}, bf16[512,256]{1,0:T(8,128)(2,1)S(1)}) custom-call(s32[32]{0:T(128)S(1)} %bitcast.10, s32[32]{0:T(128)S(1)} %collective-permute-done.idx1, s32[1]{0:T(128)} %bitcast.3.cnt0, s32[1]{0:T(128)} %collective-permute-done.1.cnt1, ...), custom_call_target="tpu_custom_call" | custom-call | tf_op jit(solution)/shard_map/fwd_tile/pallas_call | solution.py:198
  69.4 0.0 copy-start.3
  69.4 0.1 collective-permute-start.10
  69.5 0.1 collective-permute-start.11
  69.6 4.3 %collective-permute-start.12 = (bf16[512,256]{1,0:T(8,128)(2,1)S(1)}, bf16[512,256]{1,0:T(8,128)(2,1)S(1)}, u32[]{:S(2)}, u32[]{:S(2)}) collective-permute-start(bf16[512,256]{1,0:T(8,128)(2,1)S(1)} %get-tuple-element.16), channel_id=1, source_target_pairs={{0,6},{1,7},{2,4},{3,5},{4,2},{5,3},{6,0},{7,1},{8,14},{9,15},{10,... | collective-permute-start | bytes 786440 | tf_op jit(solution)/shard_map/ppermute | solution.py:28
  73.9 0.1 collective-permute-start.28
  74.0 1.1 %input_grad.1 = bf16[512,256]{1,0:T(8,128)(2,1)} custom-call(bf16[256,256]{1,0:T(8,128)(2,1)S(1)} %copy-done.3, bf16[512,256]{1,0:T(8,128)(2,1)S(1)} %get-tuple-element.17.rest_0_, bf16[512,256]{1,0:T(8,128)(2,1)S(1)} %collective-permute-done.20.rest_1_, bf16[512,256]{1,0:T(8,128)(2,1)S(1)} %collective-permute-done.21.rest_2_, ...), custom_call_target="tpu_custom_call" | custom-call | tf_op jit(solution)/shard_map/input_grad/pallas_call | solution.py:241
  75.1 0.2 collective-permute-done.28.other
  75.2 0.7 weight_grad.1
  76.0 4.9 %collective-permute-done.10.rest_1_ = bf16[512,256]{1,0:T(8,128)(2,1)S(1)} collective-permute-done((bf16[512,256]{1,0:T(8,128)(2,1)S(1)}, bf16[512,256]{1,0:T(8,128)(2,1)S(1)}, u32[]{:S(2)}, u32[]{:S(2)}) %collective-permute-start.10) | collective-permute-done | bytes 262176 | tf_op jit(solution)/shard_map/ppermute | solution.py:28
  80.9 8.3 %collective-permute-done.11.rest_2_ = bf16[512,256]{1,0:T(8,128)(2,1)S(1)} collective-permute-done((bf16[512,256]{1,0:T(8,128)(2,1)S(1)}, bf16[512,256]{1,0:T(8,128)(2,1)S(1)}, u32[]{:S(2)}, u32[]{:S(2)}) %collective-permute-start.11) | collective-permute-done | bytes 262176 | tf_op jit(solution)/shard_map/ppermute | solution.py:28
  89.2 1.0 %hidden.1 = bf16[512,256]{1,0:T(8,128)(2,1)} custom-call(bf16[256,256]{1,0:T(8,128)(2,1)S(1)} %copy-done.3, bf16[512,256]{1,0:T(8,128)(2,1)S(1)} %get-tuple-element.13.rest_0_, bf16[512,256]{1,0:T(8,128)(2,1)S(1)} %collective-permute-done.10.rest_1_, bf16[512,256]{1,0:T(8,128)(2,1)S(1)} %collective-permute-done.11.rest_2_, ...), custom_call_target="tpu_custom_call" | custom-call | tf_op jit(solution)/shard_map/hidden/pallas_call | solution.py:214
  (32 shorter events, 0.2 us)
Async XLA Ops:
  0.6 10.4 %collective-permute-start.3 = (bf16[512,256]{1,0:T(8,128)(2,1)}, bf16[512,256]{1,0:T(8,128)(2,1)S(1)}, u32[]{:S(2)}, u32[]{:S(2)}) collective-permute-start(bf16[512,256]{1,0:T(8,128)(2,1)} %rest_0_.3), channel_id=1, source_target_pairs={{0,8},{1,9},{2,10},{3,11},{4,12},{5,13},{6,14},{7,15},{8,0},{9,1},... | collective-permute-start | bytes 786440 | tf_op jit(solution)/shard_map/ppermute | solution.py:28
  3.7 13.6 %collective-permute-start.4 = (bf16[512,256]{1,0:T(8,128)(2,1)}, bf16[512,256]{1,0:T(8,128)(2,1)S(1)}, u32[]{:S(2)}, u32[]{:S(2)}) collective-permute-start(bf16[512,256]{1,0:T(8,128)(2,1)} %rest_0_.3), channel_id=1, source_target_pairs={{0,16},{1,17},{2,18},{3,19},{4,20},{5,21},{6,22},{7,23},{8,24},{9,... | collective-permute-start | bytes 786440 | tf_op jit(solution)/shard_map/ppermute | solution.py:28
  5.2 15.7 %collective-permute-start.5 = (bf16[512,256]{1,0:T(8,128)(2,1)}, bf16[512,256]{1,0:T(8,128)(2,1)S(1)}, u32[]{:S(2)}, u32[]{:S(2)}) collective-permute-start(bf16[512,256]{1,0:T(8,128)(2,1)} %rest_0_.3), channel_id=1, source_target_pairs={{0,24},{1,25},{2,26},{3,27},{4,28},{5,29},{6,30},{7,31},{8,16},{9,... | collective-permute-start | bytes 786440 | tf_op jit(solution)/shard_map/ppermute | solution.py:28
  5.2 59.9 %collective-permute-start.2 = (bf16[32,128,128]{2,1,0:T(8,128)(2,1)}, bf16[32,128,128]{2,1,0:T(8,128)(2,1)S(1)}, u32[]{:S(2)}, u32[]{:S(2)}) collective-permute-start(bf16[32,128,128]{2,1,0:T(8,128)(2,1)} %bitcast.5), channel_id=1, source_target_pairs={{0,1},{1,0},{2,3},{3,2},{4,5},{5,4},{6,7},{7,6},{8,9},{9,8},{10,11... | collective-permute-start | bytes 3145736 | tf_op jit(solution)/shard_map/ppermute | solution.py:28
  5.2 15.7 %collective-permute-start.14 = (bf16[512,256]{1,0:T(8,128)(2,1)}, bf16[512,256]{1,0:T(8,128)(2,1)S(1)}, u32[]{:S(2)}, u32[]{:S(2)}) collective-permute-start(bf16[512,256]{1,0:T(8,128)(2,1)} %rest_4_.1), channel_id=1, source_target_pairs={{0,2},{1,3},{2,0},{3,1},{4,6},{5,7},{6,4},{7,5},{8,10},{9,11},{10,... | collective-permute-start | bytes 786440 | tf_op jit(solution)/shard_map/ppermute | solution.py:28
  11.0 21.7 %collective-permute-start.16 = (bf16[512,256]{1,0:T(8,128)(2,1)}, bf16[512,256]{1,0:T(8,128)(2,1)S(1)}, u32[]{:S(2)}, u32[]{:S(2)}) collective-permute-start(bf16[512,256]{1,0:T(8,128)(2,1)} %rest_4_.1), channel_id=1, source_target_pairs={{0,4},{1,5},{2,6},{3,7},{4,0},{5,1},{6,2},{7,3},{8,12},{9,13},{10,... | collective-permute-start | bytes 786440 | tf_op jit(solution)/shard_map/ppermute | solution.py:28
  17.3 15.5 %collective-permute-start.18 = (bf16[512,256]{1,0:T(8,128)(2,1)}, bf16[512,256]{1,0:T(8,128)(2,1)S(1)}, u32[]{:S(2)}, u32[]{:S(2)}) collective-permute-start(bf16[512,256]{1,0:T(8,128)(2,1)} %rest_4_.1), channel_id=1, source_target_pairs={{0,6},{1,7},{2,4},{3,5},{4,2},{5,3},{6,0},{7,1},{8,14},{9,15},{10,... | collective-permute-start | bytes 786440 | tf_op jit(solution)/shard_map/ppermute | solution.py:28
  20.9 12.4 %collective-permute-start.13 = (bf16[512,256]{1,0:T(8,128)(2,1)}, bf16[512,256]{1,0:T(8,128)(2,1)S(1)}, u32[]{:S(2)}, u32[]{:S(2)}) collective-permute-start(bf16[512,256]{1,0:T(8,128)(2,1)} %rest_4_.1), channel_id=1, source_target_pairs={{0,1},{1,0},{2,3},{3,2},{4,5},{5,4},{6,7},{7,6},{8,9},{9,8},{10,11... | collective-permute-start | bytes 786440 | tf_op jit(solution)/shard_map/ppermute | solution.py:28
  20.9 13.1 %collective-permute-start.15 = (bf16[512,256]{1,0:T(8,128)(2,1)S(1)}, bf16[512,256]{1,0:T(8,128)(2,1)S(1)}, u32[]{:S(2)}, u32[]{:S(2)}) collective-permute-start(bf16[512,256]{1,0:T(8,128)(2,1)S(1)} %collective-permute-done.14.rest_6_), channel_id=1, source_target_pairs={{0,1},{1,0},{2,3},{3,2},{4,5},{5,4},{6,7},{7,6},{8,9},{9,8},{10,11... | collective-permute-start | bytes 786440 | tf_op jit(solution)/shard_map/ppermute | solution.py:28
  32.7 1.5 %collective-permute-start.17 = (bf16[512,256]{1,0:T(8,128)(2,1)S(1)}, bf16[512,256]{1,0:T(8,128)(2,1)S(1)}, u32[]{:S(2)}, u32[]{:S(2)}) collective-permute-start(bf16[512,256]{1,0:T(8,128)(2,1)S(1)} %collective-permute-done.16.rest_8_), channel_id=1, source_target_pairs={{0,1},{1,0},{2,3},{3,2},{4,5},{5,4},{6,7},{7,6},{8,9},{9,8},{10,11... | collective-permute-start | bytes 786440 | tf_op jit(solution)/shard_map/ppermute | solution.py:28
  32.8 1.9 %collective-permute-start.19 = (bf16[512,256]{1,0:T(8,128)(2,1)S(1)}, bf16[512,256]{1,0:T(8,128)(2,1)S(1)}, u32[]{:S(2)}, u32[]{:S(2)}) collective-permute-start(bf16[512,256]{1,0:T(8,128)(2,1)S(1)} %collective-permute-done.18.rest_10_), channel_id=1, source_target_pairs={{0,1},{1,0},{2,3},{3,2},{4,5},{5,4},{6,7},{7,6},{8,9},{9,8},{10,11... | collective-permute-start | bytes 786440 | tf_op jit(solution)/shard_map/ppermute | solution.py:28
  33.3 16.5 %collective-permute-start.6 = (bf16[512,256]{1,0:T(8,128)(2,1)}, bf16[512,256]{1,0:T(8,128)(2,1)S(1)}, u32[]{:S(2)}, u32[]{:S(2)}) collective-permute-start(bf16[512,256]{1,0:T(8,128)(2,1)} %rest_0_.3), channel_id=1, source_target_pairs={{0,1},{1,0},{2,3},{3,2},{4,5},{5,4},{6,7},{7,6},{8,9},{9,8},{10,11... | collective-permute-start | bytes 786440 | tf_op jit(solution)/shard_map/ppermute | solution.py:28
  34.7 0.7 copy-start.5
  35.3 1.2 %copy-start = (bf16[1,1,32,128,128]{4,3,2,1,0:T(8,128)(2,1)S(1)}, bf16[1,1,32,128,128]{4,3,2,1,0:T(8,128)(2,1)}, u32[]{:S(2)}) copy-start(bf16[1,1,32,128,128]{4,3,2,1,0:T(8,128)(2,1)} %param.11) | copy-start | bytes 3145732
  36.5 0.9 %copy-start.2 = (bf16[512,256]{1,0:T(8,128)(2,1)S(1)}, bf16[512,256]{1,0:T(8,128)(2,1)}, u32[]{:S(2)}) copy-start(bf16[512,256]{1,0:T(8,128)(2,1)} %rest_0_.3) | copy-start | bytes 786436
  37.5 0.9 %copy-start.4 = (bf16[512,256]{1,0:T(8,128)(2,1)S(1)}, bf16[512,256]{1,0:T(8,128)(2,1)}, u32[]{:S(2)}) copy-start(bf16[512,256]{1,0:T(8,128)(2,1)} %rest_4_.1) | copy-start | bytes 786436
  38.4 26.6 %copy-start.1 = (bf16[1,1,32,128,128]{4,3,2,1,0:T(8,128)(2,1)S(1)}, bf16[1,1,32,128,128]{4,3,2,1,0:T(8,128)(2,1)}, u32[]{:S(2)}) copy-start(bf16[1,1,32,128,128]{4,3,2,1,0:T(8,128)(2,1)} %param.11) | copy-start | bytes 3145732
  42.2 1.3 %collective-permute-start.23 = (bf16[128,256]{1,0:T(8,128)(2,1)S(1)}, bf16[128,256]{1,0:T(8,128)(2,1)S(1)}, u32[]{:S(2)}, u32[]{:S(2)}) collective-permute-start(bf16[128,256]{1,0:T(8,128)(2,1)S(1)} %get-tuple-element.22), channel_id=1, source_target_pairs={{0,1},{1,0},{2,3},{3,2},{4,5},{5,4},{6,7},{7,6},{8,9},{9,8},{10,11... | collective-permute-start | bytes 196616 | tf_op jit(solution)/shard_map/ppermute | solution.py:28
  43.6 4.3 %collective-permute-start.24 = (bf16[128,256]{1,0:T(8,128)(2,1)S(1)}, bf16[128,256]{1,0:T(8,128)(2,1)S(1)}, u32[]{:S(2)}, u32[]{:S(2)}) collective-permute-start(bf16[128,256]{1,0:T(8,128)(2,1)S(1)} %add.15), channel_id=1, source_target_pairs={{0,8},{1,9},{2,10},{3,11},{4,12},{5,13},{6,14},{7,15},{8,0},{9,1},... | collective-permute-start | bytes 196616 | tf_op jit(solution)/shard_map/ppermute | solution.py:28
  44.4 8.6 %collective-permute-start.7 = (bf16[512,256]{1,0:T(8,128)(2,1)S(1)}, bf16[512,256]{1,0:T(8,128)(2,1)S(1)}, u32[]{:S(2)}, u32[]{:S(2)}) collective-permute-start(bf16[512,256]{1,0:T(8,128)(2,1)S(1)} %collective-permute-done.3.rest_1_), channel_id=1, source_target_pairs={{0,1},{1,0},{2,3},{3,2},{4,5},{5,4},{6,7},{7,6},{8,9},{9,8},{10,11... | collective-permute-start | bytes 786440 | tf_op jit(solution)/shard_map/ppermute | solution.py:28
  44.4 4.0 %collective-permute-start.1 = (s32[1]{0:T(128)}, s32[1]{0:T(128)}, u32[]{:S(2)}, u32[]{:S(2)}) collective-permute-start(s32[1]{0:T(128)} %bitcast.1), channel_id=1, source_target_pairs={{0,1},{1,0},{2,3},{3,2},{4,5},{5,4},{6,7},{7,6},{8,9},{9,8},{10,11... | collective-permute-start | bytes 20 | tf_op jit(solution)/shard_map/ppermute | solution.py:28
  47.9 4.3 %collective-permute-start.25 = (bf16[128,256]{1,0:T(8,128)(2,1)S(1)}, bf16[128,256]{1,0:T(8,128)(2,1)S(1)}, u32[]{:S(2)}, u32[]{:S(2)}) collective-permute-start(bf16[128,256]{1,0:T(8,128)(2,1)S(1)} %add.16), channel_id=1, source_target_pairs={{0,16},{1,17},{2,18},{3,19},{4,20},{5,21},{6,22},{7,23},{8,24},{9,... | collective-permute-start | bytes 196616 | tf_op jit(solution)/shard_map/ppermute | solution.py:28
  48.4 1.2 %collective-permute-start = (s32[32]{0:T(128)S(1)}, s32[32]{0:T(128)S(1)}, u32[]{:S(2)}, u32[]{:S(2)}) collective-permute-start(s32[32]{0:T(128)S(1)} %bitcast.9), channel_id=1, source_target_pairs={{0,1},{1,0},{2,3},{3,2},{4,5},{5,4},{6,7},{7,6},{8,9},{9,8},{10,11... | collective-permute-start | bytes 392 | tf_op jit(solution)/shard_map/ppermute | solution.py:28
  49.6 10.2 %collective-permute-start.8 = (bf16[512,256]{1,0:T(8,128)(2,1)S(1)}, bf16[512,256]{1,0:T(8,128)(2,1)S(1)}, u32[]{:S(2)}, u32[]{:S(2)}) collective-permute-start(bf16[512,256]{1,0:T(8,128)(2,1)S(1)} %collective-permute-done.4.rest_2_), channel_id=1, source_target_pairs={{0,1},{1,0},{2,3},{3,2},{4,5},{5,4},{6,7},{7,6},{8,9},{9,8},{10,11... | collective-permute-start | bytes 786440 | tf_op jit(solution)/shard_map/ppermute | solution.py:28
  49.8 15.3 %collective-permute-start.9 = (bf16[512,256]{1,0:T(8,128)(2,1)S(1)}, bf16[512,256]{1,0:T(8,128)(2,1)S(1)}, u32[]{:S(2)}, u32[]{:S(2)}) collective-permute-start(bf16[512,256]{1,0:T(8,128)(2,1)S(1)} %collective-permute-done.5.rest_3_), channel_id=1, source_target_pairs={{0,1},{1,0},{2,3},{3,2},{4,5},{5,4},{6,7},{7,6},{8,9},{9,8},{10,11... | collective-permute-start | bytes 786440 | tf_op jit(solution)/shard_map/ppermute | solution.py:28
  52.3 17.2 %collective-permute-start.20 = (bf16[512,256]{1,0:T(8,128)(2,1)S(1)}, bf16[512,256]{1,0:T(8,128)(2,1)S(1)}, u32[]{:S(2)}, u32[]{:S(2)}) collective-permute-start(bf16[512,256]{1,0:T(8,128)(2,1)S(1)} %get-tuple-element.18), channel_id=1, source_target_pairs={{0,8},{1,9},{2,10},{3,11},{4,12},{5,13},{6,14},{7,15},{8,0},{9,1},... | collective-permute-start | bytes 786440 | tf_op jit(solution)/shard_map/ppermute | solution.py:28
  53.1 5.2 %collective-permute-start.26 = (bf16[128,256]{1,0:T(8,128)(2,1)S(1)}, bf16[128,256]{1,0:T(8,128)(2,1)S(1)}, u32[]{:S(2)}, u32[]{:S(2)}) collective-permute-start(bf16[128,256]{1,0:T(8,128)(2,1)S(1)} %add.17), channel_id=1, source_target_pairs={{0,2},{1,3},{2,0},{3,1},{4,6},{5,7},{6,4},{7,5},{8,10},{9,11},{10,... | collective-permute-start | bytes 196616 | tf_op jit(solution)/shard_map/ppermute | solution.py:28
  58.3 15.6 %collective-permute-start.21 = (bf16[512,256]{1,0:T(8,128)(2,1)S(1)}, bf16[512,256]{1,0:T(8,128)(2,1)S(1)}, u32[]{:S(2)}, u32[]{:S(2)}) collective-permute-start(bf16[512,256]{1,0:T(8,128)(2,1)S(1)} %get-tuple-element.19), channel_id=1, source_target_pairs={{0,16},{1,17},{2,18},{3,19},{4,20},{5,21},{6,22},{7,23},{8,24},{9,... | collective-permute-start | bytes 786440 | tf_op jit(solution)/shard_map/ppermute | solution.py:28
  59.8 9.8 %collective-permute-start.27 = (bf16[128,256]{1,0:T(8,128)(2,1)S(1)}, bf16[128,256]{1,0:T(8,128)(2,1)S(1)}, u32[]{:S(2)}, u32[]{:S(2)}) collective-permute-start(bf16[128,256]{1,0:T(8,128)(2,1)S(1)} %add.18), channel_id=1, source_target_pairs={{0,4},{1,5},{2,6},{3,7},{4,0},{5,1},{6,2},{7,3},{8,12},{9,13},{10,... | collective-permute-start | bytes 196616 | tf_op jit(solution)/shard_map/ppermute | solution.py:28
  65.1 8.9 %collective-permute-start.22 = (bf16[512,256]{1,0:T(8,128)(2,1)S(1)}, bf16[512,256]{1,0:T(8,128)(2,1)S(1)}, u32[]{:S(2)}, u32[]{:S(2)}) collective-permute-start(bf16[512,256]{1,0:T(8,128)(2,1)S(1)} %get-tuple-element.20), channel_id=1, source_target_pairs={{0,24},{1,25},{2,26},{3,27},{4,28},{5,29},{6,30},{7,31},{8,16},{9,... | collective-permute-start | bytes 786440 | tf_op jit(solution)/shard_map/ppermute | solution.py:28
  69.4 4.6 %copy-start.3 = (bf16[256,256]{1,0:T(8,128)(2,1)S(1)}, bf16[256,256]{1,0:T(8,128)(2,1)}, u32[]{:S(2)}) copy-start(bf16[256,256]{1,0:T(8,128)(2,1)} %w.3) | copy-start | bytes 393220
  69.4 11.5 %collective-permute-start.10 = (bf16[512,256]{1,0:T(8,128)(2,1)S(1)}, bf16[512,256]{1,0:T(8,128)(2,1)S(1)}, u32[]{:S(2)}, u32[]{:S(2)}) collective-permute-start(bf16[512,256]{1,0:T(8,128)(2,1)S(1)} %get-tuple-element.14), channel_id=1, source_target_pairs={{0,2},{1,3},{2,0},{3,1},{4,6},{5,7},{6,4},{7,5},{8,10},{9,11},{10,... | collective-permute-start | bytes 786440 | tf_op jit(solution)/shard_map/ppermute | solution.py:28
  69.5 19.7 %collective-permute-start.11 = (bf16[512,256]{1,0:T(8,128)(2,1)S(1)}, bf16[512,256]{1,0:T(8,128)(2,1)S(1)}, u32[]{:S(2)}, u32[]{:S(2)}) collective-permute-start(bf16[512,256]{1,0:T(8,128)(2,1)S(1)} %get-tuple-element.15), channel_id=1, source_target_pairs={{0,4},{1,5},{2,6},{3,7},{4,0},{5,1},{6,2},{7,3},{8,12},{9,13},{10,... | collective-permute-start | bytes 786440 | tf_op jit(solution)/shard_map/ppermute | solution.py:28
  69.6 19.6 %collective-permute-start.12 = (bf16[512,256]{1,0:T(8,128)(2,1)S(1)}, bf16[512,256]{1,0:T(8,128)(2,1)S(1)}, u32[]{:S(2)}, u32[]{:S(2)}) collective-permute-start(bf16[512,256]{1,0:T(8,128)(2,1)S(1)} %get-tuple-element.16), channel_id=1, source_target_pairs={{0,6},{1,7},{2,4},{3,5},{4,2},{5,3},{6,0},{7,1},{8,14},{9,15},{10,... | collective-permute-start | bytes 786440 | tf_op jit(solution)/shard_map/ppermute | solution.py:28
  73.9 1.3 %collective-permute-start.28 = (bf16[128,256]{1,0:T(8,128)(2,1)S(1)}, bf16[128,256]{1,0:T(8,128)(2,1)S(1)}, u32[]{:S(2)}, u32[]{:S(2)}) collective-permute-start(bf16[128,256]{1,0:T(8,128)(2,1)S(1)} %add.19.mine), channel_id=1, source_target_pairs={{0,1},{1,0},{2,3},{3,2},{4,5},{5,4},{6,7},{7,6},{8,9},{9,8},{10,11... | collective-permute-start | bytes 196616 | tf_op jit(solution)/shard_map/ppermute | solution.py:28

commit v2 on v1

--- a/solution.py
+++ b/solution.py
@@ -14,6 +14,7 @@
 BF16 = jnp.bfloat16
 UNROLL = 4
 ANY = pl.BlockSpec(memory_space=pl.ANY)
+HBM = pl.BlockSpec(memory_space=pltpu.HBM)
 VMEM = pl.BlockSpec(memory_space=pltpu.VMEM)
 SMEM = pl.BlockSpec(memory_space=pltpu.SMEM)
 
@@ -167,6 +168,12 @@
     return [1 << b for b in range(n.bit_length() - 1)]
 
 
+def tree(terms):
+    while len(terms) > 1:
+        terms = [terms[i] + terms[i + 1] for i in range(0, len(terms), 2)]
+    return terms[0]
+
+
 def body(features, weight, cotangent, block_index, block_count, block_values):
     nrow, ncol = lax.axis_size("row"), lax.axis_size("col")
     rows, width = features.shape
@@ -186,6 +193,7 @@
     cnt = block_count.reshape(1)
     vals = block_values.reshape(slots, size, size)
     vals1 = over_col(vals, 1)
+    vals = pltpu.with_memory_space_constraint(vals, pltpu.HBM)
     idx1 = over_col(idx, 1)
     cnt1 = over_col(cnt, 1)
     cots = [cotangent, over_col(cotangent, 1)]
@@ -194,11 +202,13 @@
         got = over_col(cotangent, 2 * s)
         cots += [got, over_col(got, 1)]
     feats1 = [over_col(feats[s], 1) for s in range(nrow)]
+    feats[0] = pltpu.with_memory_space_constraint(features, pltpu.HBM)
+    cots[0] = pltpu.with_memory_space_constraint(cotangent, pltpu.HBM)
 
     parts = pl.pallas_call(
         functools.partial(fwd_kernel, nrow, ncol),
         out_shape=[shape((rows, width), BF16)] * zs,
-        in_specs=[SMEM] * 4 + [ANY] * (2 + 2 * nrow),
+        in_specs=[SMEM] * 4 + [HBM, ANY, HBM] + [ANY] * (2 * nrow - 1),
         out_specs=[VMEM] * zs,
         scratch_shapes=[
             pltpu.VMEM((2 * slots, size, size), BF16),
@@ -223,7 +233,7 @@
     out = pl.pallas_call(
         functools.partial(bwd_kernel, nrow, ncol),
         out_shape=[shape((rows, width), BF16)] * nrow + [shape((part, width), BF16)] * 2,
-        in_specs=[SMEM, SMEM] + [ANY] * (1 + nrow + ncol),
+        in_specs=[SMEM, SMEM, HBM, HBM] + [ANY] * (nrow - 1) + [HBM] + [ANY] * (ncol - 1),
         out_specs=[VMEM] * (nrow + 2),
         scratch_shapes=[
             pltpu.VMEM((slots, size, size), BF16),
@@ -248,8 +258,7 @@
     )(weight, *backs)
 
     term = term + over_col(send, 1)
-    for s in bits(nrow):
-        term = term + over_row(term, s)
+    term = tree([term] + [over_row(term, s) for s in range(1, nrow)])
     for s in bits(zs):
         term = term + over_col(term, 2 * s)
     weight_grad = pl.pallas_call(

time: 91.6 us -> 86 us (0.939)
  the two profiles are of different devices: /device:TPU:0 before, /device:TPU:8 now
where the time goes in v2:
time: 86 us; the launch traced here: 85.8 us
  waiting for transfers between devices  51.5 us (60%)
  starting transfers between devices  22.9 us (27%)
  Pallas kernels  9.23 us (11%)
  between operations  1.39 us (2%)
    ppermute x30, waiting for transfers between devices, move(): return lax.ppermute(x, AXES, pairs)  51.5 us
    ppermute x30, starting transfers between devices, move(): return lax.ppermute(x, AXES, pairs)  22.9 us
    pallas_call x1, Pallas kernels, body(): pl.pallas_call(functools.partial(fwd_kernel, nrow, ncol), out_shape=[shap...  3.31 us
    pallas_call x1, Pallas kernels, body(): pl.pallas_call(functools.partial(bwd_kernel, nrow, ncol), out_shape=[shap...  3.08 us
  transfers between devices with their start and end apart: 30, of which 16 were waited for; matrix products, arithmetic and copies ran while one was open for 0% of the time, Pallas kernels for 10%

profile of v2, /device:TPU:8, one launch (start us, length us, event | category | flops | bytes accessed | tf_op | source)
XLA Modules:
  0.0 85.8 jit_solution(2328085360357067262)
XLA Ops:
  0.6 1.6 %collective-permute-start.3 = (bf16[512,256]{1,0:T(8,128)(2,1)}, bf16[512,256]{1,0:T(8,128)(2,1)S(1)}, u32[]{:S(2)}, u32[]{:S(2)}) collective-permute-start(bf16[512,256]{1,0:T(8,128)(2,1)} %rest_0_.3), channel_id=1, source_target_pairs={{0,8},{1,9},{2,10},{3,11},{4,12},{5,13},{6,14},{7,15},{8,0},{9,1},... | collective-permute-start | bytes 786440 | tf_op jit(solution)/shard_map/ppermute | solution.py:29
  2.2 1.5 %collective-permute-start.4 = (bf16[512,256]{1,0:T(8,128)(2,1)}, bf16[512,256]{1,0:T(8,128)(2,1)S(1)}, u32[]{:S(2)}, u32[]{:S(2)}) collective-permute-start(bf16[512,256]{1,0:T(8,128)(2,1)} %rest_0_.3), channel_id=1, source_target_pairs={{0,16},{1,17},{2,18},{3,19},{4,20},{5,21},{6,22},{7,23},{8,24},{9,... | collective-permute-start | bytes 786440 | tf_op jit(solution)/shard_map/ppermute | solution.py:29
  3.7 0.5 collective-permute-start.5
  4.2 0.0 collective-permute-start.14
  4.2 3.0 %collective-permute-start.16 = (bf16[512,256]{1,0:T(8,128)(2,1)}, bf16[512,256]{1,0:T(8,128)(2,1)S(1)}, u32[]{:S(2)}, u32[]{:S(2)}) collective-permute-start(bf16[512,256]{1,0:T(8,128)(2,1)} %rest_4_.1), channel_id=1, source_target_pairs={{0,4},{1,5},{2,6},{3,7},{4,0},{5,1},{6,2},{7,3},{8,12},{9,13},{10,... | collective-permute-start | bytes 786440 | tf_op jit(solution)/shard_map/ppermute | solution.py:29
  7.2 2.9 %collective-permute-done.3.rest_1_ = bf16[512,256]{1,0:T(8,128)(2,1)S(1)} collective-permute-done((bf16[512,256]{1,0:T(8,128)(2,1)}, bf16[512,256]{1,0:T(8,128)(2,1)S(1)}, u32[]{:S(2)}, u32[]{:S(2)}) %collective-permute-start.3) | collective-permute-done | bytes 262176 | tf_op jit(solution)/shard_map/ppermute | solution.py:29
  10.1 1.6 %collective-permute-start.18 = (bf16[512,256]{1,0:T(8,128)(2,1)}, bf16[512,256]{1,0:T(8,128)(2,1)S(1)}, u32[]{:S(2)}, u32[]{:S(2)}) collective-permute-start(bf16[512,256]{1,0:T(8,128)(2,1)} %rest_4_.1), channel_id=1, source_target_pairs={{0,6},{1,7},{2,4},{3,5},{4,2},{5,3},{6,0},{7,1},{8,14},{9,15},{10,... | collective-permute-start | bytes 786440 | tf_op jit(solution)/shard_map/ppermute | solution.py:29
  11.7 4.1 %collective-permute-done.4.rest_2_ = bf16[512,256]{1,0:T(8,128)(2,1)S(1)} collective-permute-done((bf16[512,256]{1,0:T(8,128)(2,1)}, bf16[512,256]{1,0:T(8,128)(2,1)S(1)}, u32[]{:S(2)}, u32[]{:S(2)}) %collective-permute-start.4) | collective-permute-done | bytes 262176 | tf_op jit(solution)/shard_map/ppermute | solution.py:29
  15.8 0.0 collective-permute-start.2
  15.8 0.0 collective-permute-done.5.rest_3_
  15.8 0.5 collective-permute-start.13
  16.3 0.0 collective-permute-done.14.rest_6_
  16.3 0.1 collective-permute-start.15
  16.4 9.1 %collective-permute-done.16.rest_8_ = bf16[512,256]{1,0:T(8,128)(2,1)S(1)} collective-permute-done((bf16[512,256]{1,0:T(8,128)(2,1)}, bf16[512,256]{1,0:T(8,128)(2,1)S(1)}, u32[]{:S(2)}, u32[]{:S(2)}) %collective-permute-start.16) | collective-permute-done | bytes 262176 | tf_op jit(solution)/shard_map/ppermute | solution.py:29
  25.5 4.2 %collective-permute-done.18.rest_10_ = bf16[512,256]{1,0:T(8,128)(2,1)S(1)} collective-permute-done((bf16[512,256]{1,0:T(8,128)(2,1)}, bf16[512,256]{1,0:T(8,128)(2,1)S(1)}, u32[]{:S(2)}, u32[]{:S(2)}) %collective-permute-start.18) | collective-permute-done | bytes 262176 | tf_op jit(solution)/shard_map/ppermute | solution.py:29
  29.7 0.0 collective-permute-start.19
  30.4 0.8 collective-permute-done.19.rest_11_
  31.2 0.7 copy-done.1
  31.9 3.1 %bwd_tile.1 = (bf16[512,256]{1,0:T(8,128)(2,1)S(1)}, bf16[512,256]{1,0:T(8,128)(2,1)S(1)}, bf16[512,256]{1,0:T(8,128)(2,1)S(1)}, bf16[512,256]{1,0:T(8,128)(2,1)...) custom-call(s32[32]{0:T(128)S(1)} %bitcast.5, s32[1]{0:T(128)} %bitcast.4.cnt, ...), custom_call_target="tpu_custom_call" | custom-call | tf_op jit(solution)/shard_map/bwd_tile/pallas_call | solution.py:233
  35.0 0.2 collective-permute-start.23
  35.2 1.1 %collective-permute-done.23 = bf16[128,256]{1,0:T(8,128)(2,1)S(1)} collective-permute-done((bf16[128,256]{1,0:T(8,128)(2,1)S(1)}, bf16[128,256]{1,0:T(8,128)(2,1)S(1)}, u32[]{:S(2)}, u32[]{:S(2)}) %collective-permute-start.23) | collective-permute-done | bytes 65568 | tf_op jit(solution)/shard_map/ppermute | solution.py:29
  36.3 1.9 %collective-permute-start.25 = (bf16[128,256]{1,0:T(8,128)(2,1)S(1)}, bf16[128,256]{1,0:T(8,128)(2,1)S(1)}, u32[]{:S(2)}, u32[]{:S(2)}) collective-permute-start(bf16[128,256]{1,0:T(8,128)(2,1)S(1)} %add.18), channel_id=1, source_target_pairs={{0,16},{1,17},{2,18},{3,19},{4,20},{5,21},{6,22},{7,23},{8,24},{9,... | collective-permute-start | bytes 196616 | tf_op jit(solution)/shard_map/ppermute | solution.py:29
  38.2 1.5 %collective-permute-start.26 = (bf16[128,256]{1,0:T(8,128)(2,1)S(1)}, bf16[128,256]{1,0:T(8,128)(2,1)S(1)}, u32[]{:S(2)}, u32[]{:S(2)}) collective-permute-start(bf16[128,256]{1,0:T(8,128)(2,1)S(1)} %add.18), channel_id=1, source_target_pairs={{0,24},{1,25},{2,26},{3,27},{4,28},{5,29},{6,30},{7,31},{8,16},{9,... | collective-permute-start | bytes 196616 | tf_op jit(solution)/shard_map/ppermute | solution.py:29
  39.7 0.2 collective-permute-start.24
  39.9 1.5 %collective-permute-done.25 = bf16[128,256]{1,0:T(8,128)(2,1)S(1)} collective-permute-done((bf16[128,256]{1,0:T(8,128)(2,1)S(1)}, bf16[128,256]{1,0:T(8,128)(2,1)S(1)}, u32[]{:S(2)}, u32[]{:S(2)}) %collective-permute-start.25) | collective-permute-done | bytes 65568 | tf_op jit(solution)/shard_map/ppermute | solution.py:29
  41.4 2.3 %collective-permute-done.26 = bf16[128,256]{1,0:T(8,128)(2,1)S(1)} collective-permute-done((bf16[128,256]{1,0:T(8,128)(2,1)S(1)}, bf16[128,256]{1,0:T(8,128)(2,1)S(1)}, u32[]{:S(2)}, u32[]{:S(2)}) %collective-permute-start.26) | collective-permute-done | bytes 65568 | tf_op jit(solution)/shard_map/ppermute | solution.py:29
  43.7 0.2 collective-permute-done.24
  43.9 0.3 collective-permute-start.7
  44.2 0.7 collective-permute-done.1.cnt1
  45.0 0.2 collective-permute-start.8
  45.2 0.4 collective-permute-start.9
  45.5 3.9 %collective-permute-done.27 = bf16[128,256]{1,0:T(8,128)(2,1)S(1)} collective-permute-done((bf16[128,256]{1,0:T(8,128)(2,1)S(1)}, bf16[128,256]{1,0:T(8,128)(2,1)S(1)}, u32[]{:S(2)}, u32[]{:S(2)}) %collective-permute-start.27) | collective-permute-done | bytes 65568 | tf_op jit(solution)/shard_map/ppermute | solution.py:29
  49.5 1.7 %collective-permute-start.20 = (bf16[512,256]{1,0:T(8,128)(2,1)S(1)}, bf16[512,256]{1,0:T(8,128)(2,1)S(1)}, u32[]{:S(2)}, u32[]{:S(2)}) collective-permute-start(bf16[512,256]{1,0:T(8,128)(2,1)S(1)} %get-tuple-element.18), channel_id=1, source_target_pairs={{0,8},{1,9},{2,10},{3,11},{4,12},{5,13},{6,14},{7,15},{8,0},{9,1},... | collective-permute-start | bytes 786440 | tf_op jit(solution)/shard_map/ppermute | solution.py:29
  51.2 0.6 collective-permute-start.21
  51.8 1.8 %collective-permute-start.28 = (bf16[128,256]{1,0:T(8,128)(2,1)S(1)}, bf16[128,256]{1,0:T(8,128)(2,1)S(1)}, u32[]{:S(2)}, u32[]{:S(2)}) collective-permute-start(bf16[128,256]{1,0:T(8,128)(2,1)S(1)} %add.22), channel_id=1, source_target_pairs={{0,4},{1,5},{2,6},{3,7},{4,0},{5,1},{6,2},{7,3},{8,12},{9,13},{10,... | collective-permute-start | bytes 196616 | tf_op jit(solution)/shard_map/ppermute | solution.py:29
  53.6 1.2 %collective-permute-start.22 = (bf16[512,256]{1,0:T(8,128)(2,1)S(1)}, bf16[512,256]{1,0:T(8,128)(2,1)S(1)}, u32[]{:S(2)}, u32[]{:S(2)}) collective-permute-start(bf16[512,256]{1,0:T(8,128)(2,1)S(1)} %get-tuple-element.20), channel_id=1, source_target_pairs={{0,24},{1,25},{2,26},{3,27},{4,28},{5,29},{6,30},{7,31},{8,16},{9,... | collective-permute-start | bytes 786440 | tf_op jit(solution)/shard_map/ppermute | solution.py:29
  54.8 3.3 %fwd_tile.1 = (bf16[512,256]{1,0:T(8,128)(2,1)S(1)}, bf16[512,256]{1,0:T(8,128)(2,1)S(1)}, bf16[512,256]{1,0:T(8,128)(2,1)S(1)}, bf16[512,256]{1,0:T(8,128)(2,1)S(1)}) custom-call(s32[32]{0:T(128)S(1)} %bitcast.7, s32[32]{0:T(128)S(1)} %collective-permute-done.idx1, s32[1]{0:T(128)} %bitcast.3.cnt0, s32[1]{0:T(128)} %collective-permute-done.1.cnt1, ...), custom_call_target="tpu_custom_call" | custom-call | tf_op jit(solution)/shard_map/fwd_tile/pallas_call | solution.py:208
  58.1 0.0 copy-start
  58.2 2.7 %collective-permute-start.10 = (bf16[512,256]{1,0:T(8,128)(2,1)S(1)}, bf16[512,256]{1,0:T(8,128)(2,1)S(1)}, u32[]{:S(2)}, u32[]{:S(2)}) collective-permute-start(bf16[512,256]{1,0:T(8,128)(2,1)S(1)} %get-tuple-element.14), channel_id=1, source_target_pairs={{0,2},{1,3},{2,0},{3,1},{4,6},{5,7},{6,4},{7,5},{8,10},{9,11},{10,... | collective-permute-start | bytes 786440 | tf_op jit(solution)/shard_map/ppermute | solution.py:29
  60.8 1.5 %collective-permute-start.12 = (bf16[512,256]{1,0:T(8,128)(2,1)S(1)}, bf16[512,256]{1,0:T(8,128)(2,1)S(1)}, u32[]{:S(2)}, u32[]{:S(2)}) collective-permute-start(bf16[512,256]{1,0:T(8,128)(2,1)S(1)} %get-tuple-element.16), channel_id=1, source_target_pairs={{0,6},{1,7},{2,4},{3,5},{4,2},{5,3},{6,0},{7,1},{8,14},{9,15},{10,... | collective-permute-start | bytes 786440 | tf_op jit(solution)/shard_map/ppermute | solution.py:29
  62.4 1.9 %collective-permute-done.21.rest_2_ = bf16[512,256]{1,0:T(8,128)(2,1)S(1)} collective-permute-done((bf16[512,256]{1,0:T(8,128)(2,1)S(1)}, bf16[512,256]{1,0:T(8,128)(2,1)S(1)}, u32[]{:S(2)}, u32[]{:S(2)}) %collective-permute-start.21) | collective-permute-done | bytes 262176 | tf_op jit(solution)/shard_map/ppermute | solution.py:29
  64.3 1.1 %input_grad.1 = bf16[512,256]{1,0:T(8,128)(2,1)} custom-call(bf16[256,256]{1,0:T(8,128)(2,1)S(1)} %copy-done, bf16[512,256]{1,0:T(8,128)(2,1)S(1)} %get-tuple-element.17.rest_0_, bf16[512,256]{1,0:T(8,128)(2,1)S(1)} %collective-permute-done.20.rest_1_, bf16[512,256]{1,0:T(8,128)(2,1)S(1)} %collective-permute-done.21.rest_2_, ...), custom_call_target="tpu_custom_call" | custom-call | tf_op jit(solution)/shard_map/input_grad/pallas_call | solution.py:251
  65.4 0.2 collective-permute-done.29.other
  65.5 0.7 weight_grad.1
  66.3 3.1 %collective-permute-done.10.rest_1_ = bf16[512,256]{1,0:T(8,128)(2,1)S(1)} collective-permute-done((bf16[512,256]{1,0:T(8,128)(2,1)S(1)}, bf16[512,256]{1,0:T(8,128)(2,1)S(1)}, u32[]{:S(2)}, u32[]{:S(2)}) %collective-permute-start.10) | collective-permute-done | bytes 262176 | tf_op jit(solution)/shard_map/ppermute | solution.py:29
  69.4 9.4 %collective-permute-done.11.rest_2_ = bf16[512,256]{1,0:T(8,128)(2,1)S(1)} collective-permute-done((bf16[512,256]{1,0:T(8,128)(2,1)S(1)}, bf16[512,256]{1,0:T(8,128)(2,1)S(1)}, u32[]{:S(2)}, u32[]{:S(2)}) %collective-permute-start.11) | collective-permute-done | bytes 262176 | tf_op jit(solution)/shard_map/ppermute | solution.py:29
  78.8 6.0 %collective-permute-done.12.rest_3_ = bf16[512,256]{1,0:T(8,128)(2,1)S(1)} collective-permute-done((bf16[512,256]{1,0:T(8,128)(2,1)S(1)}, bf16[512,256]{1,0:T(8,128)(2,1)S(1)}, u32[]{:S(2)}, u32[]{:S(2)}) %collective-permute-start.12) | collective-permute-done | bytes 262176 | tf_op jit(solution)/shard_map/ppermute | solution.py:29
  84.8 1.0 %hidden.1 = bf16[512,256]{1,0:T(8,128)(2,1)} custom-call(bf16[256,256]{1,0:T(8,128)(2,1)S(1)} %copy-done, bf16[512,256]{1,0:T(8,128)(2,1)S(1)} %get-tuple-element.13.rest_0_, bf16[512,256]{1,0:T(8,128)(2,1)S(1)} %collective-permute-done.10.rest_1_, bf16[512,256]{1,0:T(8,128)(2,1)S(1)} %collective-permute-done.11.rest_2_, ...), custom_call_target="tpu_custom_call" | custom-call | tf_op jit(solution)/shard_map/hidden/pallas_call | solution.py:224
  (27 shorter events, 0.1 us)
Async XLA Ops:
  0.6 9.5 %collective-permute-start.3 = (bf16[512,256]{1,0:T(8,128)(2,1)}, bf16[512,256]{1,0:T(8,128)(2,1)S(1)}, u32[]{:S(2)}, u32[]{:S(2)}) collective-permute-start(bf16[512,256]{1,0:T(8,128)(2,1)} %rest_0_.3), channel_id=1, source_target_pairs={{0,8},{1,9},{2,10},{3,11},{4,12},{5,13},{6,14},{7,15},{8,0},{9,1},... | collective-permute-start | bytes 786440 | tf_op jit(solution)/shard_map/ppermute | solution.py:29
  2.2 13.6 %collective-permute-start.4 = (bf16[512,256]{1,0:T(8,128)(2,1)}, bf16[512,256]{1,0:T(8,128)(2,1)S(1)}, u32[]{:S(2)}, u32[]{:S(2)}) collective-permute-start(bf16[512,256]{1,0:T(8,128)(2,1)} %rest_0_.3), channel_id=1, source_target_pairs={{0,16},{1,17},{2,18},{3,19},{4,20},{5,21},{6,22},{7,23},{8,24},{9,... | collective-permute-start | bytes 786440 | tf_op jit(solution)/shard_map/ppermute | solution.py:29
  3.7 12.1 %collective-permute-start.5 = (bf16[512,256]{1,0:T(8,128)(2,1)}, bf16[512,256]{1,0:T(8,128)(2,1)S(1)}, u32[]{:S(2)}, u32[]{:S(2)}) collective-permute-start(bf16[512,256]{1,0:T(8,128)(2,1)} %rest_0_.3), channel_id=1, source_target_pairs={{0,24},{1,25},{2,26},{3,27},{4,28},{5,29},{6,30},{7,31},{8,16},{9,... | collective-permute-start | bytes 786440 | tf_op jit(solution)/shard_map/ppermute | solution.py:29
  4.2 12.1 %collective-permute-start.14 = (bf16[512,256]{1,0:T(8,128)(2,1)}, bf16[512,256]{1,0:T(8,128)(2,1)S(1)}, u32[]{:S(2)}, u32[]{:S(2)}) collective-permute-start(bf16[512,256]{1,0:T(8,128)(2,1)} %rest_4_.1), channel_id=1, source_target_pairs={{0,2},{1,3},{2,0},{3,1},{4,6},{5,7},{6,4},{7,5},{8,10},{9,11},{10,... | collective-permute-start | bytes 786440 | tf_op jit(solution)/shard_map/ppermute | solution.py:29
  4.2 21.3 %collective-permute-start.16 = (bf16[512,256]{1,0:T(8,128)(2,1)}, bf16[512,256]{1,0:T(8,128)(2,1)S(1)}, u32[]{:S(2)}, u32[]{:S(2)}) collective-permute-start(bf16[512,256]{1,0:T(8,128)(2,1)} %rest_4_.1), channel_id=1, source_target_pairs={{0,4},{1,5},{2,6},{3,7},{4,0},{5,1},{6,2},{7,3},{8,12},{9,13},{10,... | collective-permute-start | bytes 786440 | tf_op jit(solution)/shard_map/ppermute | solution.py:29
  10.1 19.6 %collective-permute-start.18 = (bf16[512,256]{1,0:T(8,128)(2,1)}, bf16[512,256]{1,0:T(8,128)(2,1)S(1)}, u32[]{:S(2)}, u32[]{:S(2)}) collective-permute-start(bf16[512,256]{1,0:T(8,128)(2,1)} %rest_4_.1), channel_id=1, source_target_pairs={{0,6},{1,7},{2,4},{3,5},{4,2},{5,3},{6,0},{7,1},{8,14},{9,15},{10,... | collective-permute-start | bytes 786440 | tf_op jit(solution)/shard_map/ppermute | solution.py:29
  15.8 39.0 %collective-permute-start.2 = (bf16[32,128,128]{2,1,0:T(8,128)(2,1)}, bf16[32,128,128]{2,1,0:T(8,128)(2,1)S(1)}, u32[]{:S(2)}, u32[]{:S(2)}) collective-permute-start(bf16[32,128,128]{2,1,0:T(8,128)(2,1)} %bitcast.8), channel_id=1, source_target_pairs={{0,1},{1,0},{2,3},{3,2},{4,5},{5,4},{6,7},{7,6},{8,9},{9,8},{10,11... | collective-permute-start | bytes 3145736 | tf_op jit(solution)/shard_map/ppermute | solution.py:29
  15.8 14.6 %collective-permute-start.13 = (bf16[512,256]{1,0:T(8,128)(2,1)}, bf16[512,256]{1,0:T(8,128)(2,1)S(1)}, u32[]{:S(2)}, u32[]{:S(2)}) collective-permute-start(bf16[512,256]{1,0:T(8,128)(2,1)} %rest_4_.1), channel_id=1, source_target_pairs={{0,1},{1,0},{2,3},{3,2},{4,5},{5,4},{6,7},{7,6},{8,9},{9,8},{10,11... | collective-permute-start | bytes 786440 | tf_op jit(solution)/shard_map/ppermute | solution.py:29
  16.3 14.1 %collective-permute-start.15 = (bf16[512,256]{1,0:T(8,128)(2,1)S(1)}, bf16[512,256]{1,0:T(8,128)(2,1)S(1)}, u32[]{:S(2)}, u32[]{:S(2)}) collective-permute-start(bf16[512,256]{1,0:T(8,128)(2,1)S(1)} %collective-permute-done.14.rest_6_), channel_id=1, source_target_pairs={{0,1},{1,0},{2,3},{3,2},{4,5},{5,4},{6,7},{7,6},{8,9},{9,8},{10,11... | collective-permute-start | bytes 786440 | tf_op jit(solution)/shard_map/ppermute | solution.py:29
  25.5 4.9 %collective-permute-start.17 = (bf16[512,256]{1,0:T(8,128)(2,1)S(1)}, bf16[512,256]{1,0:T(8,128)(2,1)S(1)}, u32[]{:S(2)}, u32[]{:S(2)}) collective-permute-start(bf16[512,256]{1,0:T(8,128)(2,1)S(1)} %collective-permute-done.16.rest_8_), channel_id=1, source_target_pairs={{0,1},{1,0},{2,3},{3,2},{4,5},{5,4},{6,7},{7,6},{8,9},{9,8},{10,11... | collective-permute-start | bytes 786440 | tf_op jit(solution)/shard_map/ppermute | solution.py:29
  29.7 1.5 %collective-permute-start.19 = (bf16[512,256]{1,0:T(8,128)(2,1)S(1)}, bf16[512,256]{1,0:T(8,128)(2,1)S(1)}, u32[]{:S(2)}, u32[]{:S(2)}) collective-permute-start(bf16[512,256]{1,0:T(8,128)(2,1)S(1)} %collective-permute-done.18.rest_10_), channel_id=1, source_target_pairs={{0,1},{1,0},{2,3},{3,2},{4,5},{5,4},{6,7},{7,6},{8,9},{9,8},{10,11... | collective-permute-start | bytes 786440 | tf_op jit(solution)/shard_map/ppermute | solution.py:29
  31.2 0.7 copy-start.1
  31.9 9.5 %copy-start.2 = (bf16[512,256]{1,0:T(8,128)(2,1)S(1)}, bf16[512,256]{1,0:T(8,128)(2,1)}, u32[]{:S(2)}) copy-start(bf16[512,256]{1,0:T(8,128)(2,1)} %rest_0_.3) | copy-start | bytes 786436
  35.0 1.3 %collective-permute-start.23 = (bf16[128,256]{1,0:T(8,128)(2,1)S(1)}, bf16[128,256]{1,0:T(8,128)(2,1)S(1)}, u32[]{:S(2)}, u32[]{:S(2)}) collective-permute-start(bf16[128,256]{1,0:T(8,128)(2,1)S(1)} %get-tuple-element.22), channel_id=1, source_target_pairs={{0,1},{1,0},{2,3},{3,2},{4,5},{5,4},{6,7},{7,6},{8,9},{9,8},{10,11... | collective-permute-start | bytes 196616 | tf_op jit(solution)/shard_map/ppermute | solution.py:29
  36.3 5.1 %collective-permute-start.25 = (bf16[128,256]{1,0:T(8,128)(2,1)S(1)}, bf16[128,256]{1,0:T(8,128)(2,1)S(1)}, u32[]{:S(2)}, u32[]{:S(2)}) collective-permute-start(bf16[128,256]{1,0:T(8,128)(2,1)S(1)} %add.18), channel_id=1, source_target_pairs={{0,16},{1,17},{2,18},{3,19},{4,20},{5,21},{6,22},{7,23},{8,24},{9,... | collective-permute-start | bytes 196616 | tf_op jit(solution)/shard_map/ppermute | solution.py:29
  38.2 5.5 %collective-permute-start.26 = (bf16[128,256]{1,0:T(8,128)(2,1)S(1)}, bf16[128,256]{1,0:T(8,128)(2,1)S(1)}, u32[]{:S(2)}, u32[]{:S(2)}) collective-permute-start(bf16[128,256]{1,0:T(8,128)(2,1)S(1)} %add.18), channel_id=1, source_target_pairs={{0,24},{1,25},{2,26},{3,27},{4,28},{5,29},{6,30},{7,31},{8,16},{9,... | collective-permute-start | bytes 196616 | tf_op jit(solution)/shard_map/ppermute | solution.py:29
  39.7 4.3 %collective-permute-start.24 = (bf16[128,256]{1,0:T(8,128)(2,1)S(1)}, bf16[128,256]{1,0:T(8,128)(2,1)S(1)}, u32[]{:S(2)}, u32[]{:S(2)}) collective-permute-start(bf16[128,256]{1,0:T(8,128)(2,1)S(1)} %add.18), channel_id=1, source_target_pairs={{0,8},{1,9},{2,10},{3,11},{4,12},{5,13},{6,14},{7,15},{8,0},{9,1},... | collective-permute-start | bytes 196616 | tf_op jit(solution)/shard_map/ppermute | solution.py:29
  39.9 5.3 %collective-permute-start = (s32[32]{0:T(128)S(1)}, s32[32]{0:T(128)S(1)}, u32[]{:S(2)}, u32[]{:S(2)}) collective-permute-start(s32[32]{0:T(128)S(1)} %bitcast.6), channel_id=1, source_target_pairs={{0,1},{1,0},{2,3},{3,2},{4,5},{5,4},{6,7},{7,6},{8,9},{9,8},{10,11... | collective-permute-start | bytes 392 | tf_op jit(solution)/shard_map/ppermute | solution.py:29
  41.4 3.7 %collective-permute-start.6 = (bf16[512,256]{1,0:T(8,128)(2,1)S(1)}, bf16[512,256]{1,0:T(8,128)(2,1)S(1)}, u32[]{:S(2)}, u32[]{:S(2)}) collective-permute-start(bf16[512,256]{1,0:T(8,128)(2,1)S(1)} %copy-done.2), channel_id=1, source_target_pairs={{0,1},{1,0},{2,3},{3,2},{4,5},{5,4},{6,7},{7,6},{8,9},{9,8},{10,11... | collective-permute-start | bytes 786440 | tf_op jit(solution)/shard_map/ppermute | solution.py:29
  43.7 1.3 %collective-permute-start.1 = (s32[1]{0:T(128)}, s32[1]{0:T(128)}, u32[]{:S(2)}, u32[]{:S(2)}) collective-permute-start(s32[1]{0:T(128)} %bitcast.1), channel_id=1, source_target_pairs={{0,1},{1,0},{2,3},{3,2},{4,5},{5,4},{6,7},{7,6},{8,9},{9,8},{10,11... | collective-permute-start | bytes 20 | tf_op jit(solution)/shard_map/ppermute | solution.py:29
  43.9 7.3 %collective-permute-start.7 = (bf16[512,256]{1,0:T(8,128)(2,1)S(1)}, bf16[512,256]{1,0:T(8,128)(2,1)S(1)}, u32[]{:S(2)}, u32[]{:S(2)}) collective-permute-start(bf16[512,256]{1,0:T(8,128)(2,1)S(1)} %collective-permute-done.3.rest_1_), channel_id=1, source_target_pairs={{0,1},{1,0},{2,3},{3,2},{4,5},{5,4},{6,7},{7,6},{8,9},{9,8},{10,11... | collective-permute-start | bytes 786440 | tf_op jit(solution)/shard_map/ppermute | solution.py:29
  45.0 6.8 %collective-permute-start.8 = (bf16[512,256]{1,0:T(8,128)(2,1)S(1)}, bf16[512,256]{1,0:T(8,128)(2,1)S(1)}, u32[]{:S(2)}, u32[]{:S(2)}) collective-permute-start(bf16[512,256]{1,0:T(8,128)(2,1)S(1)} %collective-permute-done.4.rest_2_), channel_id=1, source_target_pairs={{0,1},{1,0},{2,3},{3,2},{4,5},{5,4},{6,7},{7,6},{8,9},{9,8},{10,11... | collective-permute-start | bytes 786440 | tf_op jit(solution)/shard_map/ppermute | solution.py:29
  45.1 4.3 %collective-permute-start.27 = (bf16[128,256]{1,0:T(8,128)(2,1)S(1)}, bf16[128,256]{1,0:T(8,128)(2,1)S(1)}, u32[]{:S(2)}, u32[]{:S(2)}) collective-permute-start(bf16[128,256]{1,0:T(8,128)(2,1)S(1)} %add_add_fusion), channel_id=1, source_target_pairs={{0,2},{1,3},{2,0},{3,1},{4,6},{5,7},{6,4},{7,5},{8,10},{9,11},{10,... | collective-permute-start | bytes 196616 | tf_op jit(solution)/shard_map/ppermute | solution.py:29
  45.2 8.5 %collective-permute-start.9 = (bf16[512,256]{1,0:T(8,128)(2,1)S(1)}, bf16[512,256]{1,0:T(8,128)(2,1)S(1)}, u32[]{:S(2)}, u32[]{:S(2)}) collective-permute-start(bf16[512,256]{1,0:T(8,128)(2,1)S(1)} %collective-permute-done.5.rest_3_), channel_id=1, source_target_pairs={{0,1},{1,0},{2,3},{3,2},{4,5},{5,4},{6,7},{7,6},{8,9},{9,8},{10,11... | collective-permute-start | bytes 786440 | tf_op jit(solution)/shard_map/ppermute | solution.py:29
  49.5 11.4 %collective-permute-start.20 = (bf16[512,256]{1,0:T(8,128)(2,1)S(1)}, bf16[512,256]{1,0:T(8,128)(2,1)S(1)}, u32[]{:S(2)}, u32[]{:S(2)}) collective-permute-start(bf16[512,256]{1,0:T(8,128)(2,1)S(1)} %get-tuple-element.18), channel_id=1, source_target_pairs={{0,8},{1,9},{2,10},{3,11},{4,12},{5,13},{6,14},{7,15},{8,0},{9,1},... | collective-permute-start | bytes 786440 | tf_op jit(solution)/shard_map/ppermute | solution.py:29
  51.2 13.1 %collective-permute-start.21 = (bf16[512,256]{1,0:T(8,128)(2,1)S(1)}, bf16[512,256]{1,0:T(8,128)(2,1)S(1)}, u32[]{:S(2)}, u32[]{:S(2)}) collective-permute-start(bf16[512,256]{1,0:T(8,128)(2,1)S(1)} %get-tuple-element.19), channel_id=1, source_target_pairs={{0,16},{1,17},{2,18},{3,19},{4,20},{5,21},{6,22},{7,23},{8,24},{9,... | collective-permute-start | bytes 786440 | tf_op jit(solution)/shard_map/ppermute | solution.py:29
  51.8 9.0 %collective-permute-start.28 = (bf16[128,256]{1,0:T(8,128)(2,1)S(1)}, bf16[128,256]{1,0:T(8,128)(2,1)S(1)}, u32[]{:S(2)}, u32[]{:S(2)}) collective-permute-start(bf16[128,256]{1,0:T(8,128)(2,1)S(1)} %add.22), channel_id=1, source_target_pairs={{0,4},{1,5},{2,6},{3,7},{4,0},{5,1},{6,2},{7,3},{8,12},{9,13},{10,... | collective-permute-start | bytes 196616 | tf_op jit(solution)/shard_map/ppermute | solution.py:29
  53.6 10.7 %collective-permute-start.22 = (bf16[512,256]{1,0:T(8,128)(2,1)S(1)}, bf16[512,256]{1,0:T(8,128)(2,1)S(1)}, u32[]{:S(2)}, u32[]{:S(2)}) collective-permute-start(bf16[512,256]{1,0:T(8,128)(2,1)S(1)} %get-tuple-element.20), channel_id=1, source_target_pairs={{0,24},{1,25},{2,26},{3,27},{4,28},{5,29},{6,30},{7,31},{8,16},{9,... | collective-permute-start | bytes 786440 | tf_op jit(solution)/shard_map/ppermute | solution.py:29
  58.1 6.2 %copy-start = (bf16[256,256]{1,0:T(8,128)(2,1)S(1)}, bf16[256,256]{1,0:T(8,128)(2,1)}, u32[]{:S(2)}) copy-start(bf16[256,256]{1,0:T(8,128)(2,1)} %w.3) | copy-start | bytes 393220
  58.2 11.2 %collective-permute-start.10 = (bf16[512,256]{1,0:T(8,128)(2,1)S(1)}, bf16[512,256]{1,0:T(8,128)(2,1)S(1)}, u32[]{:S(2)}, u32[]{:S(2)}) collective-permute-start(bf16[512,256]{1,0:T(8,128)(2,1)S(1)} %get-tuple-element.14), channel_id=1, source_target_pairs={{0,2},{1,3},{2,0},{3,1},{4,6},{5,7},{6,4},{7,5},{8,10},{9,11},{10,... | collective-permute-start | bytes 786440 | tf_op jit(solution)/shard_map/ppermute | solution.py:29
  60.8 17.9 %collective-permute-start.11 = (bf16[512,256]{1,0:T(8,128)(2,1)S(1)}, bf16[512,256]{1,0:T(8,128)(2,1)S(1)}, u32[]{:S(2)}, u32[]{:S(2)}) collective-permute-start(bf16[512,256]{1,0:T(8,128)(2,1)S(1)} %get-tuple-element.15), channel_id=1, source_target_pairs={{0,4},{1,5},{2,6},{3,7},{4,0},{5,1},{6,2},{7,3},{8,12},{9,13},{10,... | collective-permute-start | bytes 786440 | tf_op jit(solution)/shard_map/ppermute | solution.py:29
  60.8 23.9 %collective-permute-start.12 = (bf16[512,256]{1,0:T(8,128)(2,1)S(1)}, bf16[512,256]{1,0:T(8,128)(2,1)S(1)}, u32[]{:S(2)}, u32[]{:S(2)}) collective-permute-start(bf16[512,256]{1,0:T(8,128)(2,1)S(1)} %get-tuple-element.16), channel_id=1, source_target_pairs={{0,6},{1,7},{2,4},{3,5},{4,2},{5,3},{6,0},{7,1},{8,14},{9,15},{10,... | collective-permute-start | bytes 786440 | tf_op jit(solution)/shard_map/ppermute | solution.py:29
  64.3 1.3 %collective-permute-start.29 = (bf16[128,256]{1,0:T(8,128)(2,1)S(1)}, bf16[128,256]{1,0:T(8,128)(2,1)S(1)}, u32[]{:S(2)}, u32[]{:S(2)}) collective-permute-start(bf16[128,256]{1,0:T(8,128)(2,1)S(1)} %add.23.mine), channel_id=1, source_target_pairs={{0,1},{1,0},{2,3},{3,2},{4,5},{5,4},{6,7},{7,6},{8,9},{9,8},{10,11... | collective-permute-start | bytes 196616 | tf_op jit(solution)/shard_map/ppermute | solution.py:29

commit v3 on v2

--- a/solution.py
+++ b/solution.py
@@ -16,7 +16,6 @@
 ANY = pl.BlockSpec(memory_space=pl.ANY)
 HBM = pl.BlockSpec(memory_space=pltpu.HBM)
 VMEM = pl.BlockSpec(memory_space=pltpu.VMEM)
-SMEM = pl.BlockSpec(memory_space=pltpu.SMEM)
 
 
 def move(x, rows, cols, fn):
@@ -29,11 +28,11 @@
     return lax.ppermute(x, AXES, pairs)
 
 
-def fwd_kernel(nrow, ncol, idx0, idx1, cnt0, cnt1, vals0, vals1, *rest):
+def fwd_kernel(nrow, ncol, idx0_hbm, idx1_hbm, cnt0_hbm, cnt1_hbm, vals0, vals1, *rest):
     shards = rest[:2 * nrow]
     zs = ncol // 2
     outs = rest[2 * nrow:2 * nrow + zs]
-    vbuf, fbuf, acc, todo, sem = rest[2 * nrow + zs:]
+    vbuf, fbuf, acc, todo, idx0, idx1, cnt0, cnt1, sem, meta_sem = rest[2 * nrow + zs:]
     slots, size = vals0.shape[0], vals0.shape[1]
     rows, _ = shards[0].shape
     per = rows // size
@@ -42,6 +41,10 @@
     me_r = lax.axis_index("row")
     me_c = lax.axis_index("col")
     me_z, me_k = me_c // 2, me_c % 2
+    pairs = ((idx0_hbm, idx0), (idx1_hbm, idx1), (cnt0_hbm, cnt0), (cnt1_hbm, cnt1))
+    metas = [pltpu.make_async_copy(src, dst, meta_sem.at[i]) for i, (src, dst) in enumerate(pairs)]
+    for copy in metas:
+        copy.start()
     copies = []
     for t, vals in enumerate((vals0, vals1)):
         copies.append(pltpu.make_async_copy(vals, vbuf.at[pl.ds(t * slots, slots)], sem.at[2 * nrow + t]))
@@ -53,6 +56,9 @@
         copy.start()
     acc[...] = jnp.zeros_like(acc)
 
+    for copy in metas:
+        copy.wait()
+
     def listed(t, idx, cnt, n):
         def one(g, n):
             q = idx[g]
@@ -88,11 +94,11 @@
         outs[s][...] = acc[s * rows:(s + 1) * rows, :].astype(BF16)
 
 
-def bwd_kernel(nrow, ncol, idx, cnt, vals, *rest):
+def bwd_kernel(nrow, ncol, idx_hbm, cnt_hbm, vals, *rest):
     feats = rest[:nrow]
     cots = rest[nrow:nrow + ncol]
     outs = rest[nrow + ncol:2 * nrow + ncol]
-    tkeep, tsend, vbuf, fbuf, cbuf, acc, tbuf, sem = rest[2 * nrow + ncol:]
+    tkeep, tsend, vbuf, fbuf, cbuf, acc, tbuf, idx, cnt, sem, meta_sem = rest[2 * nrow + ncol:]
     size = vals.shape[1]
     rows, width = feats[0].shape
     per = rows // size
@@ -101,7 +107,8 @@
     me_r = lax.axis_index("row")
     me_c = lax.axis_index("col")
     me_k = me_c % 2
-    copies = [pltpu.make_async_copy(vals, vbuf, sem.at[nrow + ncol])]
+    metas = [pltpu.make_async_copy(idx_hbm, idx, meta_sem.at[0]), pltpu.make_async_copy(cnt_hbm, cnt, meta_sem.at[1])]
+    copies = metas + [pltpu.make_async_copy(vals, vbuf, sem.at[nrow + ncol])]
     for s in range(nrow):
         copies.append(pltpu.make_async_copy(feats[s], fbuf.at[pl.ds(s * rows, rows)], sem.at[s]))
     for s in range(ncol):
@@ -168,6 +175,10 @@
     return [1 << b for b in range(n.bit_length() - 1)]
 
 
+def ones(s):
+    return s.bit_count()
+
+
 def tree(terms):
     while len(terms) > 1:
         terms = [terms[i] + terms[i + 1] for i in range(0, len(terms), 2)]
@@ -198,9 +209,11 @@
     cnt1 = over_col(cnt, 1)
     cots = [cotangent, over_col(cotangent, 1)]
     feats = [features] + [over_row(features, s) for s in range(1, nrow)]
-    for s in range(1, zs):
-        got = over_col(cotangent, 2 * s)
-        cots += [got, over_col(got, 1)]
+    cots += [None] * (ncol - 2)
+    for s in sorted(range(1, zs), key=ones):
+        low = s & -s
+        got = over_col(cots[2 * (s ^ low)], 2 * low)
+        cots[2 * s:2 * s + 2] = [got, over_col(got, 1)]
     feats1 = [over_col(feats[s], 1) for s in range(nrow)]
     feats[0] = pltpu.with_memory_space_constraint(features, pltpu.HBM)
     cots[0] = pltpu.with_memory_space_constraint(cotangent, pltpu.HBM)
@@ -208,23 +221,37 @@
     parts = pl.pallas_call(
         functools.partial(fwd_kernel, nrow, ncol),
         out_shape=[shape((rows, width), BF16)] * zs,
-        in_specs=[SMEM] * 4 + [HBM, ANY, HBM] + [ANY] * (2 * nrow - 1),
+        in_specs=[ANY] * 4 + [HBM, ANY, HBM] + [ANY] * (2 * nrow - 1),
         out_specs=[VMEM] * zs,
         scratch_shapes=[
             pltpu.VMEM((2 * slots, size, size), BF16),
             pltpu.VMEM((2 * nrow * rows, width), BF16),
             pltpu.VMEM((zs * rows + size, width), F32),
             pltpu.SMEM((3, 2 * slots + UNROLL), jnp.int32),
+            pltpu.SMEM((slots,), jnp.int32),
+            pltpu.SMEM((slots,), jnp.int32),
+            pltpu.SMEM((1,), jnp.int32),
+            pltpu.SMEM((1,), jnp.int32),
             pltpu.SemaphoreType.DMA((2 * nrow + 2,)),
+            pltpu.SemaphoreType.DMA((4,)),
         ],
         compiler_params=pltpu.CompilerParams(vmem_limit_bytes=16 << 20),
         name="fwd_tile",
     )(idx, idx1, cnt, cnt1, vals, vals1, *feats, *feats1)
-    parts = [parts[0]] + [over_col(parts[s], 2 * s) for s in range(1, zs)]
+    parts = list(parts)
+    final = [parts[0]]
+    for s in sorted(range(1, zs), key=ones, reverse=True):
+        low = s & -s
+        got = over_col(parts[s], 2 * low)
+        if s == low:
+            final.append(got)
+        else:
+            parts[s ^ low] = parts[s ^ low] + got
+    parts = final
     hidden = pl.pallas_call(
-        functools.partial(sum_dot_kernel, zs, (((1,), (0,)), ((), ()))),
+        functools.partial(sum_dot_kernel, len(parts), (((1,), (0,)), ((), ()))),
         out_shape=shape((rows, width), BF16),
-        in_specs=[VMEM] * (1 + zs),
+        in_specs=[VMEM] * (1 + len(parts)),
         out_specs=VMEM,
         compiler_params=pltpu.CompilerParams(vmem_limit_bytes=8 << 20),
         name="hidden",
@@ -233,7 +260,7 @@
     out = pl.pallas_call(
         functools.partial(bwd_kernel, nrow, ncol),
         out_shape=[shape((rows, width), BF16)] * nrow + [shape((part, width), BF16)] * 2,
-        in_specs=[SMEM, SMEM, HBM, HBM] + [ANY] * (nrow - 1) + [HBM] + [ANY] * (ncol - 1),
+        in_specs=[ANY, ANY, HBM, HBM] + [ANY] * (nrow - 1) + [HBM] + [ANY] * (ncol - 1),
         out_specs=[VMEM] * (nrow + 2),
         scratch_shapes=[
             pltpu.VMEM((slots, size, size), BF16),
@@ -241,7 +268,10 @@
             pltpu.VMEM((ncol * rows, width), BF16),
             pltpu.VMEM((nrow * rows + size, width), F32),
             pltpu.VMEM((width, width), F32),
+            pltpu.SMEM((slots,), jnp.int32),
+            pltpu.SMEM((1,), jnp.int32),
             pltpu.SemaphoreType.DMA((nrow + ncol + 1,)),
+            pltpu.SemaphoreType.DMA((2,)),
         ],
         compiler_params=pltpu.CompilerParams(vmem_limit_bytes=16 << 20),
         name="bwd_tile",

time: 86 us -> 74.6 us (0.87)
  the two profiles are of different devices: /device:TPU:8 before, /device:TPU:0 now
where the time goes in v3:
time: 74.6 us; the launch traced here: 74.4 us
  waiting for transfers between devices  37 us (50%)
  starting transfers between devices  24.3 us (33%)
  Pallas kernels  10.9 us (15%)
  between operations  1.45 us (2%)
    ppermute x30, waiting for transfers between devices, move(): return lax.ppermute(x, AXES, pairs)  37 us
    ppermute x30, starting transfers between devices, move(): return lax.ppermute(x, AXES, pairs)  24.3 us
    pallas_call x1, Pallas kernels, body(): pl.pallas_call(functools.partial(bwd_kernel, nrow, ncol), out_shape=[shap...  4.18 us
    pallas_call x1, Pallas kernels, body(): pl.pallas_call(functools.partial(fwd_kernel, nrow, ncol), out_shape=[shap...  3.85 us
  transfers between devices with their start and end apart: 30, of which 12 were waited for; matrix products, arithmetic and copies ran while one was open for 0% of the time, Pallas kernels for 13%

profile of v3, /device:TPU:0, one launch (start us, length us, event | category | flops | bytes accessed | tf_op | source)
XLA Modules:
  0.0 74.4 jit_solution(5786737999427150532)
XLA Ops:
  0.6 3.0 %collective-permute-start.3 = (bf16[512,256]{1,0:T(8,128)(2,1)}, bf16[512,256]{1,0:T(8,128)(2,1)S(1)}, u32[]{:S(2)}, u32[]{:S(2)}) collective-permute-start(bf16[512,256]{1,0:T(8,128)(2,1)} %rest_0_.3), channel_id=1, source_target_pairs={{0,8},{1,9},{2,10},{3,11},{4,12},{5,13},{6,14},{7,15},{8,0},{9,1},... | collective-permute-start | bytes 786440 | tf_op jit(solution)/shard_map/ppermute | solution.py:28
  3.7 2.6 %collective-permute-start.16 = (bf16[512,256]{1,0:T(8,128)(2,1)}, bf16[512,256]{1,0:T(8,128)(2,1)S(1)}, u32[]{:S(2)}, u32[]{:S(2)}) collective-permute-start(bf16[512,256]{1,0:T(8,128)(2,1)} %rest_4_.1), channel_id=1, source_target_pairs={{0,4},{1,5},{2,6},{3,7},{4,0},{5,1},{6,2},{7,3},{8,12},{9,13},{10,... | collective-permute-start | bytes 786440 | tf_op jit(solution)/shard_map/ppermute | solution.py:28
  6.3 0.0 collective-permute-start.2
  6.3 1.5 %collective-permute-start.4 = (bf16[512,256]{1,0:T(8,128)(2,1)}, bf16[512,256]{1,0:T(8,128)(2,1)S(1)}, u32[]{:S(2)}, u32[]{:S(2)}) collective-permute-start(bf16[512,256]{1,0:T(8,128)(2,1)} %rest_0_.3), channel_id=1, source_target_pairs={{0,16},{1,17},{2,18},{3,19},{4,20},{5,21},{6,22},{7,23},{8,24},{9,... | collective-permute-start | bytes 786440 | tf_op jit(solution)/shard_map/ppermute | solution.py:28
  7.8 0.5 collective-permute-start.5
  8.3 1.9 %collective-permute-done.3.rest_1_ = bf16[512,256]{1,0:T(8,128)(2,1)S(1)} collective-permute-done((bf16[512,256]{1,0:T(8,128)(2,1)}, bf16[512,256]{1,0:T(8,128)(2,1)S(1)}, u32[]{:S(2)}, u32[]{:S(2)}) %collective-permute-start.3) | collective-permute-done | bytes 262176 | tf_op jit(solution)/shard_map/ppermute | solution.py:28
  10.2 1.8 %collective-permute-start.14 = (bf16[512,256]{1,0:T(8,128)(2,1)}, bf16[512,256]{1,0:T(8,128)(2,1)S(1)}, u32[]{:S(2)}, u32[]{:S(2)}) collective-permute-start(bf16[512,256]{1,0:T(8,128)(2,1)} %rest_4_.1), channel_id=1, source_target_pairs={{0,2},{1,3},{2,0},{3,1},{4,6},{5,7},{6,4},{7,5},{8,10},{9,11},{10,... | collective-permute-start | bytes 786440 | tf_op jit(solution)/shard_map/ppermute | solution.py:28
  12.0 6.3 %collective-permute-done.16.rest_8_ = bf16[512,256]{1,0:T(8,128)(2,1)S(1)} collective-permute-done((bf16[512,256]{1,0:T(8,128)(2,1)}, bf16[512,256]{1,0:T(8,128)(2,1)S(1)}, u32[]{:S(2)}, u32[]{:S(2)}) %collective-permute-start.16) | collective-permute-done | bytes 262176 | tf_op jit(solution)/shard_map/ppermute | solution.py:28
  18.3 0.7 collective-permute-start.18
  19.0 1.8 %collective-permute-done.4.rest_2_ = bf16[512,256]{1,0:T(8,128)(2,1)S(1)} collective-permute-done((bf16[512,256]{1,0:T(8,128)(2,1)}, bf16[512,256]{1,0:T(8,128)(2,1)S(1)}, u32[]{:S(2)}, u32[]{:S(2)}) %collective-permute-start.4) | collective-permute-done | bytes 262176 | tf_op jit(solution)/shard_map/ppermute | solution.py:28
  20.8 0.5 collective-permute-start.17
  21.3 2.6 %collective-permute-done.14.rest_6_ = bf16[512,256]{1,0:T(8,128)(2,1)S(1)} collective-permute-done((bf16[512,256]{1,0:T(8,128)(2,1)}, bf16[512,256]{1,0:T(8,128)(2,1)S(1)}, u32[]{:S(2)}, u32[]{:S(2)}) %collective-permute-start.14) | collective-permute-done | bytes 262176 | tf_op jit(solution)/shard_map/ppermute | solution.py:28
  23.9 0.0 collective-permute-start.15
  23.9 4.1 %collective-permute-done.18.rest_10_ = bf16[512,256]{1,0:T(8,128)(2,1)S(1)} collective-permute-done((bf16[512,256]{1,0:T(8,128)(2,1)S(1)}, bf16[512,256]{1,0:T(8,128)(2,1)S(1)}, u32[]{:S(2)}, u32[]{:S(2)}) %collective-permute-start.18) | collective-permute-done | bytes 262176 | tf_op jit(solution)/shard_map/ppermute | solution.py:28
  28.7 0.8 %collective-permute-done.19.rest_11_ = bf16[512,256]{1,0:T(8,128)(2,1)S(1)} collective-permute-done((bf16[512,256]{1,0:T(8,128)(2,1)S(1)}, bf16[512,256]{1,0:T(8,128)(2,1)S(1)}, u32[]{:S(2)}, u32[]{:S(2)}) %collective-permute-start.19) | collective-permute-done | bytes 262176 | tf_op jit(solution)/shard_map/ppermute | solution.py:28
  29.5 0.7 copy-done.1
  30.2 4.2 %bwd_tile.1 = (bf16[512,256]{1,0:T(8,128)(2,1)S(1)}, bf16[512,256]{1,0:T(8,128)(2,1)S(1)}, bf16[512,256]{1,0:T(8,128)(2,1)S(1)}, bf16[512,256]{1,0:T(8,128)(2,1)...) custom-call(s32[32]{0:T(128)S(1)} %bitcast.5, s32[1]{0:T(128)} %bitcast.4.cnt_hbm, ...), custom_call_target="tpu_custom_call" | custom-call | tf_op jit(solution)/shard_map/bwd_tile/pallas_call | solution.py:260
  34.4 0.1 collective-permute-start.23
  34.4 0.5 collective-permute-start
  34.9 0.1 collective-permute-start.6
  35.0 0.4 collective-permute-start.1
  35.5 1.0 %collective-permute-done.1.cnt1_hbm = s32[1]{0:T(128)} collective-permute-done((s32[1]{0:T(128)}, s32[1]{0:T(128)}, u32[]{:S(2)}, u32[]{:S(2)}) %collective-permute-start.1) | collective-permute-done | bytes 36 | tf_op jit(solution)/shard_map/ppermute | solution.py:28
  36.5 0.2 collective-permute-start.7
  36.7 0.3 collective-permute-start.8
  37.0 0.2 collective-permute-start.9
  37.3 0.1 collective-permute-start.25
  37.4 0.7 collective-permute-done.7.rest_5_
  38.0 1.6 %collective-permute-start.26 = (bf16[128,256]{1,0:T(8,128)(2,1)S(1)}, bf16[128,256]{1,0:T(8,128)(2,1)S(1)}, u32[]{:S(2)}, u32[]{:S(2)}) collective-permute-start(bf16[128,256]{1,0:T(8,128)(2,1)S(1)} %add.22), channel_id=1, source_target_pairs={{0,24},{1,25},{2,26},{3,27},{4,28},{5,29},{6,30},{7,31},{8,16},{9,... | collective-permute-start | bytes 196616 | tf_op jit(solution)/shard_map/ppermute | solution.py:28
  39.6 1.2 %collective-permute-start.24 = (bf16[128,256]{1,0:T(8,128)(2,1)S(1)}, bf16[128,256]{1,0:T(8,128)(2,1)S(1)}, u32[]{:S(2)}, u32[]{:S(2)}) collective-permute-start(bf16[128,256]{1,0:T(8,128)(2,1)S(1)} %add.22), channel_id=1, source_target_pairs={{0,8},{1,9},{2,10},{3,11},{4,12},{5,13},{6,14},{7,15},{8,0},{9,1},... | collective-permute-start | bytes 196616 | tf_op jit(solution)/shard_map/ppermute | solution.py:28
  40.9 3.9 %fwd_tile.1 = (bf16[512,256]{1,0:T(8,128)(2,1)S(1)}, bf16[512,256]{1,0:T(8,128)(2,1)S(1)}, bf16[512,256]{1,0:T(8,128)(2,1)S(1)}, bf16[512,256]{1,0:T(8,128)(2,1)S(1)}) custom-call(s32[32]{0:T(128)S(1)} %bitcast.7, s32[32]{0:T(128)S(1)} %collective-permute-done.idx1_hbm, s32[1]{0:T(128)} %bitcast.3.cnt0_hbm, s32[1]{0:T(128)} %collective-permute-done.1.cnt1_hbm, ...), custom_call_target="tpu_custom_call" | custom-call | tf_op jit(solution)/shard_map/fwd_tile/pallas_call | solution.py:221
  44.7 0.1 collective-permute-start.11
  44.8 2.1 %collective-permute-start.27 = (bf16[128,256]{1,0:T(8,128)(2,1)S(1)}, bf16[128,256]{1,0:T(8,128)(2,1)S(1)}, u32[]{:S(2)}, u32[]{:S(2)}) collective-permute-start(bf16[128,256]{1,0:T(8,128)(2,1)S(1)} %add_add_fusion), channel_id=1, source_target_pairs={{0,2},{1,3},{2,0},{3,1},{4,6},{5,7},{6,4},{7,5},{8,10},{9,11},{10,... | collective-permute-start | bytes 196616 | tf_op jit(solution)/shard_map/ppermute | solution.py:28
  46.9 0.1 collective-permute-start.20
  47.0 7.5 %collective-permute-done.27 = bf16[128,256]{1,0:T(8,128)(2,1)S(1)} collective-permute-done((bf16[128,256]{1,0:T(8,128)(2,1)S(1)}, bf16[128,256]{1,0:T(8,128)(2,1)S(1)}, u32[]{:S(2)}, u32[]{:S(2)}) %collective-permute-start.27) | collective-permute-done | bytes 65568 | tf_op jit(solution)/shard_map/ppermute | solution.py:28
  54.5 1.8 %collective-permute-start.28 = (bf16[128,256]{1,0:T(8,128)(2,1)S(1)}, bf16[128,256]{1,0:T(8,128)(2,1)S(1)}, u32[]{:S(2)}, u32[]{:S(2)}) collective-permute-start(bf16[128,256]{1,0:T(8,128)(2,1)S(1)} %add.26), channel_id=1, source_target_pairs={{0,4},{1,5},{2,6},{3,7},{4,0},{5,1},{6,2},{7,3},{8,12},{9,13},{10,... | collective-permute-start | bytes 196616 | tf_op jit(solution)/shard_map/ppermute | solution.py:28
  56.3 0.8 %collective-permute-start.21 = (bf16[512,256]{1,0:T(8,128)(2,1)S(1)}, bf16[512,256]{1,0:T(8,128)(2,1)S(1)}, u32[]{:S(2)}, u32[]{:S(2)}) collective-permute-start(bf16[512,256]{1,0:T(8,128)(2,1)S(1)} %get-tuple-element.19), channel_id=1, source_target_pairs={{0,16},{1,17},{2,18},{3,19},{4,20},{5,21},{6,22},{7,23},{8,24},{9,... | collective-permute-start | bytes 786440 | tf_op jit(solution)/shard_map/ppermute | solution.py:28
  57.1 0.7 collective-permute-start.22
  57.7 1.7 %collective-permute-start.10 = (bf16[512,256]{1,0:T(8,128)(2,1)S(1)}, bf16[512,256]{1,0:T(8,128)(2,1)S(1)}, u32[]{:S(2)}, u32[]{:S(2)}) collective-permute-start(bf16[512,256]{1,0:T(8,128)(2,1)S(1)} %get-tuple-element.14), channel_id=1, source_target_pairs={{0,2},{1,3},{2,0},{3,1},{4,6},{5,7},{6,4},{7,5},{8,10},{9,11},{10,... | collective-permute-start | bytes 786440 | tf_op jit(solution)/shard_map/ppermute | solution.py:28
  59.4 0.1 add.21
  59.5 0.0 copy-start
  59.5 0.9 %collective-permute-done.28 = bf16[128,256]{1,0:T(8,128)(2,1)S(1)} collective-permute-done((bf16[128,256]{1,0:T(8,128)(2,1)S(1)}, bf16[128,256]{1,0:T(8,128)(2,1)S(1)}, u32[]{:S(2)}, u32[]{:S(2)}) %collective-permute-start.28) | collective-permute-done | bytes 65568 | tf_op jit(solution)/shard_map/ppermute | solution.py:28
  60.4 1.7 %collective-permute-start.12 = (bf16[512,256]{1,0:T(8,128)(2,1)S(1)}, bf16[512,256]{1,0:T(8,128)(2,1)S(1)}, u32[]{:S(2)}, u32[]{:S(2)}) collective-permute-start(bf16[512,256]{1,0:T(8,128)(2,1)S(1)} %add.21), channel_id=1, source_target_pairs={{0,4},{1,5},{2,6},{3,7},{4,0},{5,1},{6,2},{7,3},{8,12},{9,13},{10,... | collective-permute-start | bytes 786440 | tf_op jit(solution)/shard_map/ppermute | solution.py:28
  62.2 0.1 collective-permute-start.29
  62.3 7.2 %collective-permute-done.21.rest_2_ = bf16[512,256]{1,0:T(8,128)(2,1)S(1)} collective-permute-done((bf16[512,256]{1,0:T(8,128)(2,1)S(1)}, bf16[512,256]{1,0:T(8,128)(2,1)S(1)}, u32[]{:S(2)}, u32[]{:S(2)}) %collective-permute-start.21) | collective-permute-done | bytes 262176 | tf_op jit(solution)/shard_map/ppermute | solution.py:28
  69.4 1.1 %input_grad.1 = bf16[512,256]{1,0:T(8,128)(2,1)} custom-call(bf16[256,256]{1,0:T(8,128)(2,1)S(1)} %copy-done, bf16[512,256]{1,0:T(8,128)(2,1)S(1)} %get-tuple-element.17.rest_0_, bf16[512,256]{1,0:T(8,128)(2,1)S(1)} %collective-permute-done.20.rest_1_, bf16[512,256]{1,0:T(8,128)(2,1)S(1)} %collective-permute-done.21.rest_2_, ...), custom_call_target="tpu_custom_call" | custom-call | tf_op jit(solution)/shard_map/input_grad/pallas_call | solution.py:281
  70.5 0.7 weight_grad.1
  71.2 2.2 %collective-permute-done.12.rest_2_ = bf16[512,256]{1,0:T(8,128)(2,1)S(1)} collective-permute-done((bf16[512,256]{1,0:T(8,128)(2,1)S(1)}, bf16[512,256]{1,0:T(8,128)(2,1)S(1)}, u32[]{:S(2)}, u32[]{:S(2)}) %collective-permute-start.12) | collective-permute-done | bytes 262176 | tf_op jit(solution)/shard_map/ppermute | solution.py:28
  73.4 1.0 %hidden.1 = bf16[512,256]{1,0:T(8,128)(2,1)} custom-call(bf16[256,256]{1,0:T(8,128)(2,1)S(1)} %copy-done, bf16[512,256]{1,0:T(8,128)(2,1)S(1)} %get-tuple-element.13.rest_0_, bf16[512,256]{1,0:T(8,128)(2,1)S(1)} %collective-permute-done.10.rest_1_, bf16[512,256]{1,0:T(8,128)(2,1)S(1)} %collective-permute-done.12.rest_2_), custom_call_target="tpu_custom_call" | custom-call | tf_op jit(solution)/shard_map/hidden/pallas_call | solution.py:251
  (28 shorter events, 0.1 us)
Async XLA Ops:
  0.6 9.6 %collective-permute-start.3 = (bf16[512,256]{1,0:T(8,128)(2,1)}, bf16[512,256]{1,0:T(8,128)(2,1)S(1)}, u32[]{:S(2)}, u32[]{:S(2)}) collective-permute-start(bf16[512,256]{1,0:T(8,128)(2,1)} %rest_0_.3), channel_id=1, source_target_pairs={{0,8},{1,9},{2,10},{3,11},{4,12},{5,13},{6,14},{7,15},{8,0},{9,1},... | collective-permute-start | bytes 786440 | tf_op jit(solution)/shard_map/ppermute | solution.py:28
  3.7 14.6 %collective-permute-start.16 = (bf16[512,256]{1,0:T(8,128)(2,1)}, bf16[512,256]{1,0:T(8,128)(2,1)S(1)}, u32[]{:S(2)}, u32[]{:S(2)}) collective-permute-start(bf16[512,256]{1,0:T(8,128)(2,1)} %rest_4_.1), channel_id=1, source_target_pairs={{0,4},{1,5},{2,6},{3,7},{4,0},{5,1},{6,2},{7,3},{8,12},{9,13},{10,... | collective-permute-start | bytes 786440 | tf_op jit(solution)/shard_map/ppermute | solution.py:28
  6.3 34.6 %collective-permute-start.2 = (bf16[32,128,128]{2,1,0:T(8,128)(2,1)}, bf16[32,128,128]{2,1,0:T(8,128)(2,1)S(1)}, u32[]{:S(2)}, u32[]{:S(2)}) collective-permute-start(bf16[32,128,128]{2,1,0:T(8,128)(2,1)} %bitcast.8), channel_id=1, source_target_pairs={{0,1},{1,0},{2,3},{3,2},{4,5},{5,4},{6,7},{7,6},{8,9},{9,8},{10,11... | collective-permute-start | bytes 3145736 | tf_op jit(solution)/shard_map/ppermute | solution.py:28
  6.3 14.5 %collective-permute-start.4 = (bf16[512,256]{1,0:T(8,128)(2,1)}, bf16[512,256]{1,0:T(8,128)(2,1)S(1)}, u32[]{:S(2)}, u32[]{:S(2)}) collective-permute-start(bf16[512,256]{1,0:T(8,128)(2,1)} %rest_0_.3), channel_id=1, source_target_pairs={{0,16},{1,17},{2,18},{3,19},{4,20},{5,21},{6,22},{7,23},{8,24},{9,... | collective-permute-start | bytes 786440 | tf_op jit(solution)/shard_map/ppermute | solution.py:28
  7.8 13.0 %collective-permute-start.5 = (bf16[512,256]{1,0:T(8,128)(2,1)}, bf16[512,256]{1,0:T(8,128)(2,1)S(1)}, u32[]{:S(2)}, u32[]{:S(2)}) collective-permute-start(bf16[512,256]{1,0:T(8,128)(2,1)} %rest_0_.3), channel_id=1, source_target_pairs={{0,24},{1,25},{2,26},{3,27},{4,28},{5,29},{6,30},{7,31},{8,16},{9,... | collective-permute-start | bytes 786440 | tf_op jit(solution)/shard_map/ppermute | solution.py:28
  10.2 13.7 %collective-permute-start.14 = (bf16[512,256]{1,0:T(8,128)(2,1)}, bf16[512,256]{1,0:T(8,128)(2,1)S(1)}, u32[]{:S(2)}, u32[]{:S(2)}) collective-permute-start(bf16[512,256]{1,0:T(8,128)(2,1)} %rest_4_.1), channel_id=1, source_target_pairs={{0,2},{1,3},{2,0},{3,1},{4,6},{5,7},{6,4},{7,5},{8,10},{9,11},{10,... | collective-permute-start | bytes 786440 | tf_op jit(solution)/shard_map/ppermute | solution.py:28
  18.3 9.7 %collective-permute-start.18 = (bf16[512,256]{1,0:T(8,128)(2,1)S(1)}, bf16[512,256]{1,0:T(8,128)(2,1)S(1)}, u32[]{:S(2)}, u32[]{:S(2)}) collective-permute-start(bf16[512,256]{1,0:T(8,128)(2,1)S(1)} %collective-permute-done.16.rest_8_), channel_id=1, source_target_pairs={{0,2},{1,3},{2,0},{3,1},{4,6},{5,7},{6,4},{7,5},{8,10},{9,11},{10,... | collective-permute-start | bytes 786440 | tf_op jit(solution)/shard_map/ppermute | solution.py:28
  20.8 7.8 %collective-permute-start.13 = (bf16[512,256]{1,0:T(8,128)(2,1)}, bf16[512,256]{1,0:T(8,128)(2,1)S(1)}, u32[]{:S(2)}, u32[]{:S(2)}) collective-permute-start(bf16[512,256]{1,0:T(8,128)(2,1)} %rest_4_.1), channel_id=1, source_target_pairs={{0,1},{1,0},{2,3},{3,2},{4,5},{5,4},{6,7},{7,6},{8,9},{9,8},{10,11... | collective-permute-start | bytes 786440 | tf_op jit(solution)/shard_map/ppermute | solution.py:28
  20.8 7.9 %collective-permute-start.17 = (bf16[512,256]{1,0:T(8,128)(2,1)S(1)}, bf16[512,256]{1,0:T(8,128)(2,1)S(1)}, u32[]{:S(2)}, u32[]{:S(2)}) collective-permute-start(bf16[512,256]{1,0:T(8,128)(2,1)S(1)} %collective-permute-done.16.rest_8_), channel_id=1, source_target_pairs={{0,1},{1,0},{2,3},{3,2},{4,5},{5,4},{6,7},{7,6},{8,9},{9,8},{10,11... | collective-permute-start | bytes 786440 | tf_op jit(solution)/shard_map/ppermute | solution.py:28
  23.9 4.8 %collective-permute-start.15 = (bf16[512,256]{1,0:T(8,128)(2,1)S(1)}, bf16[512,256]{1,0:T(8,128)(2,1)S(1)}, u32[]{:S(2)}, u32[]{:S(2)}) collective-permute-start(bf16[512,256]{1,0:T(8,128)(2,1)S(1)} %collective-permute-done.14.rest_6_), channel_id=1, source_target_pairs={{0,1},{1,0},{2,3},{3,2},{4,5},{5,4},{6,7},{7,6},{8,9},{9,8},{10,11... | collective-permute-start | bytes 786440 | tf_op jit(solution)/shard_map/ppermute | solution.py:28
  28.0 1.5 %collective-permute-start.19 = (bf16[512,256]{1,0:T(8,128)(2,1)S(1)}, bf16[512,256]{1,0:T(8,128)(2,1)S(1)}, u32[]{:S(2)}, u32[]{:S(2)}) collective-permute-start(bf16[512,256]{1,0:T(8,128)(2,1)S(1)} %collective-permute-done.18.rest_10_), channel_id=1, source_target_pairs={{0,1},{1,0},{2,3},{3,2},{4,5},{5,4},{6,7},{7,6},{8,9},{9,8},{10,11... | collective-permute-start | bytes 786440 | tf_op jit(solution)/shard_map/ppermute | solution.py:28
  29.5 0.7 copy-start.1
  30.2 4.8 %copy-start.2 = (bf16[512,256]{1,0:T(8,128)(2,1)S(1)}, bf16[512,256]{1,0:T(8,128)(2,1)}, u32[]{:S(2)}) copy-start(bf16[512,256]{1,0:T(8,128)(2,1)} %rest_0_.3) | copy-start | bytes 786436
  34.4 2.6 %collective-permute-start.23 = (bf16[128,256]{1,0:T(8,128)(2,1)S(1)}, bf16[128,256]{1,0:T(8,128)(2,1)S(1)}, u32[]{:S(2)}, u32[]{:S(2)}) collective-permute-start(bf16[128,256]{1,0:T(8,128)(2,1)S(1)} %get-tuple-element.22), channel_id=1, source_target_pairs={{0,1},{1,0},{2,3},{3,2},{4,5},{5,4},{6,7},{7,6},{8,9},{9,8},{10,11... | collective-permute-start | bytes 196616 | tf_op jit(solution)/shard_map/ppermute | solution.py:28
  34.4 2.3 %collective-permute-start = (s32[32]{0:T(128)S(1)}, s32[32]{0:T(128)S(1)}, u32[]{:S(2)}, u32[]{:S(2)}) collective-permute-start(s32[32]{0:T(128)S(1)} %bitcast.6), channel_id=1, source_target_pairs={{0,1},{1,0},{2,3},{3,2},{4,5},{5,4},{6,7},{7,6},{8,9},{9,8},{10,11... | collective-permute-start | bytes 392 | tf_op jit(solution)/shard_map/ppermute | solution.py:28
  34.9 2.3 %collective-permute-start.6 = (bf16[512,256]{1,0:T(8,128)(2,1)S(1)}, bf16[512,256]{1,0:T(8,128)(2,1)S(1)}, u32[]{:S(2)}, u32[]{:S(2)}) collective-permute-start(bf16[512,256]{1,0:T(8,128)(2,1)S(1)} %copy-done.2), channel_id=1, source_target_pairs={{0,1},{1,0},{2,3},{3,2},{4,5},{5,4},{6,7},{7,6},{8,9},{9,8},{10,11... | collective-permute-start | bytes 786440 | tf_op jit(solution)/shard_map/ppermute | solution.py:28
  35.0 1.5 %collective-permute-start.1 = (s32[1]{0:T(128)}, s32[1]{0:T(128)}, u32[]{:S(2)}, u32[]{:S(2)}) collective-permute-start(s32[1]{0:T(128)} %bitcast.1), channel_id=1, source_target_pairs={{0,1},{1,0},{2,3},{3,2},{4,5},{5,4},{6,7},{7,6},{8,9},{9,8},{10,11... | collective-permute-start | bytes 20 | tf_op jit(solution)/shard_map/ppermute | solution.py:28
  36.5 1.5 %collective-permute-start.7 = (bf16[512,256]{1,0:T(8,128)(2,1)S(1)}, bf16[512,256]{1,0:T(8,128)(2,1)S(1)}, u32[]{:S(2)}, u32[]{:S(2)}) collective-permute-start(bf16[512,256]{1,0:T(8,128)(2,1)S(1)} %collective-permute-done.3.rest_1_), channel_id=1, source_target_pairs={{0,1},{1,0},{2,3},{3,2},{4,5},{5,4},{6,7},{7,6},{8,9},{9,8},{10,11... | collective-permute-start | bytes 786440 | tf_op jit(solution)/shard_map/ppermute | solution.py:28
  36.7 2.9 %collective-permute-start.8 = (bf16[512,256]{1,0:T(8,128)(2,1)S(1)}, bf16[512,256]{1,0:T(8,128)(2,1)S(1)}, u32[]{:S(2)}, u32[]{:S(2)}) collective-permute-start(bf16[512,256]{1,0:T(8,128)(2,1)S(1)} %collective-permute-done.4.rest_2_), channel_id=1, source_target_pairs={{0,1},{1,0},{2,3},{3,2},{4,5},{5,4},{6,7},{7,6},{8,9},{9,8},{10,11... | collective-permute-start | bytes 786440 | tf_op jit(solution)/shard_map/ppermute | solution.py:28
  37.0 3.8 %collective-permute-start.9 = (bf16[512,256]{1,0:T(8,128)(2,1)S(1)}, bf16[512,256]{1,0:T(8,128)(2,1)S(1)}, u32[]{:S(2)}, u32[]{:S(2)}) collective-permute-start(bf16[512,256]{1,0:T(8,128)(2,1)S(1)} %collective-permute-done.5.rest_3_), channel_id=1, source_target_pairs={{0,1},{1,0},{2,3},{3,2},{4,5},{5,4},{6,7},{7,6},{8,9},{9,8},{10,11... | collective-permute-start | bytes 786440 | tf_op jit(solution)/shard_map/ppermute | solution.py:28
  37.3 7.5 %collective-permute-start.25 = (bf16[128,256]{1,0:T(8,128)(2,1)S(1)}, bf16[128,256]{1,0:T(8,128)(2,1)S(1)}, u32[]{:S(2)}, u32[]{:S(2)}) collective-permute-start(bf16[128,256]{1,0:T(8,128)(2,1)S(1)} %add.22), channel_id=1, source_target_pairs={{0,16},{1,17},{2,18},{3,19},{4,20},{5,21},{6,22},{7,23},{8,24},{9,... | collective-permute-start | bytes 196616 | tf_op jit(solution)/shard_map/ppermute | solution.py:28
  38.0 6.8 %collective-permute-start.26 = (bf16[128,256]{1,0:T(8,128)(2,1)S(1)}, bf16[128,256]{1,0:T(8,128)(2,1)S(1)}, u32[]{:S(2)}, u32[]{:S(2)}) collective-permute-start(bf16[128,256]{1,0:T(8,128)(2,1)S(1)} %add.22), channel_id=1, source_target_pairs={{0,24},{1,25},{2,26},{3,27},{4,28},{5,29},{6,30},{7,31},{8,16},{9,... | collective-permute-start | bytes 196616 | tf_op jit(solution)/shard_map/ppermute | solution.py:28
  39.6 5.2 %collective-permute-start.24 = (bf16[128,256]{1,0:T(8,128)(2,1)S(1)}, bf16[128,256]{1,0:T(8,128)(2,1)S(1)}, u32[]{:S(2)}, u32[]{:S(2)}) collective-permute-start(bf16[128,256]{1,0:T(8,128)(2,1)S(1)} %add.22), channel_id=1, source_target_pairs={{0,8},{1,9},{2,10},{3,11},{4,12},{5,13},{6,14},{7,15},{8,0},{9,1},... | collective-permute-start | bytes 196616 | tf_op jit(solution)/shard_map/ppermute | solution.py:28
  44.7 13.0 %collective-permute-start.11 = (bf16[512,256]{1,0:T(8,128)(2,1)S(1)}, bf16[512,256]{1,0:T(8,128)(2,1)S(1)}, u32[]{:S(2)}, u32[]{:S(2)}) collective-permute-start(bf16[512,256]{1,0:T(8,128)(2,1)S(1)} %get-tuple-element.16), channel_id=1, source_target_pairs={{0,2},{1,3},{2,0},{3,1},{4,6},{5,7},{6,4},{7,5},{8,10},{9,11},{10,... | collective-permute-start | bytes 786440 | tf_op jit(solution)/shard_map/ppermute | solution.py:28
  44.8 9.7 %collective-permute-start.27 = (bf16[128,256]{1,0:T(8,128)(2,1)S(1)}, bf16[128,256]{1,0:T(8,128)(2,1)S(1)}, u32[]{:S(2)}, u32[]{:S(2)}) collective-permute-start(bf16[128,256]{1,0:T(8,128)(2,1)S(1)} %add_add_fusion), channel_id=1, source_target_pairs={{0,2},{1,3},{2,0},{3,1},{4,6},{5,7},{6,4},{7,5},{8,10},{9,11},{10,... | collective-permute-start | bytes 196616 | tf_op jit(solution)/shard_map/ppermute | solution.py:28
  46.9 15.3 %collective-permute-start.20 = (bf16[512,256]{1,0:T(8,128)(2,1)S(1)}, bf16[512,256]{1,0:T(8,128)(2,1)S(1)}, u32[]{:S(2)}, u32[]{:S(2)}) collective-permute-start(bf16[512,256]{1,0:T(8,128)(2,1)S(1)} %get-tuple-element.18), channel_id=1, source_target_pairs={{0,8},{1,9},{2,10},{3,11},{4,12},{5,13},{6,14},{7,15},{8,0},{9,1},... | collective-permute-start | bytes 786440 | tf_op jit(solution)/shard_map/ppermute | solution.py:28
  54.5 5.9 %collective-permute-start.28 = (bf16[128,256]{1,0:T(8,128)(2,1)S(1)}, bf16[128,256]{1,0:T(8,128)(2,1)S(1)}, u32[]{:S(2)}, u32[]{:S(2)}) collective-permute-start(bf16[128,256]{1,0:T(8,128)(2,1)S(1)} %add.26), channel_id=1, source_target_pairs={{0,4},{1,5},{2,6},{3,7},{4,0},{5,1},{6,2},{7,3},{8,12},{9,13},{10,... | collective-permute-start | bytes 196616 | tf_op jit(solution)/shard_map/ppermute | solution.py:28
  56.3 13.1 %collective-permute-start.21 = (bf16[512,256]{1,0:T(8,128)(2,1)S(1)}, bf16[512,256]{1,0:T(8,128)(2,1)S(1)}, u32[]{:S(2)}, u32[]{:S(2)}) collective-permute-start(bf16[512,256]{1,0:T(8,128)(2,1)S(1)} %get-tuple-element.19), channel_id=1, source_target_pairs={{0,16},{1,17},{2,18},{3,19},{4,20},{5,21},{6,22},{7,23},{8,24},{9,... | collective-permute-start | bytes 786440 | tf_op jit(solution)/shard_map/ppermute | solution.py:28
  57.1 12.3 %collective-permute-start.22 = (bf16[512,256]{1,0:T(8,128)(2,1)S(1)}, bf16[512,256]{1,0:T(8,128)(2,1)S(1)}, u32[]{:S(2)}, u32[]{:S(2)}) collective-permute-start(bf16[512,256]{1,0:T(8,128)(2,1)S(1)} %get-tuple-element.20), channel_id=1, source_target_pairs={{0,24},{1,25},{2,26},{3,27},{4,28},{5,29},{6,30},{7,31},{8,16},{9,... | collective-permute-start | bytes 786440 | tf_op jit(solution)/shard_map/ppermute | solution.py:28
  57.7 13.5 %collective-permute-start.10 = (bf16[512,256]{1,0:T(8,128)(2,1)S(1)}, bf16[512,256]{1,0:T(8,128)(2,1)S(1)}, u32[]{:S(2)}, u32[]{:S(2)}) collective-permute-start(bf16[512,256]{1,0:T(8,128)(2,1)S(1)} %get-tuple-element.14), channel_id=1, source_target_pairs={{0,2},{1,3},{2,0},{3,1},{4,6},{5,7},{6,4},{7,5},{8,10},{9,11},{10,... | collective-permute-start | bytes 786440 | tf_op jit(solution)/shard_map/ppermute | solution.py:28
  59.5 9.9 %copy-start = (bf16[256,256]{1,0:T(8,128)(2,1)S(1)}, bf16[256,256]{1,0:T(8,128)(2,1)}, u32[]{:S(2)}) copy-start(bf16[256,256]{1,0:T(8,128)(2,1)} %w.3) | copy-start | bytes 393220
  60.4 13.0 %collective-permute-start.12 = (bf16[512,256]{1,0:T(8,128)(2,1)S(1)}, bf16[512,256]{1,0:T(8,128)(2,1)S(1)}, u32[]{:S(2)}, u32[]{:S(2)}) collective-permute-start(bf16[512,256]{1,0:T(8,128)(2,1)S(1)} %add.21), channel_id=1, source_target_pairs={{0,4},{1,5},{2,6},{3,7},{4,0},{5,1},{6,2},{7,3},{8,12},{9,13},{10,... | collective-permute-start | bytes 786440 | tf_op jit(solution)/shard_map/ppermute | solution.py:28
  62.2 8.3 %collective-permute-start.29 = (bf16[128,256]{1,0:T(8,128)(2,1)S(1)}, bf16[128,256]{1,0:T(8,128)(2,1)S(1)}, u32[]{:S(2)}, u32[]{:S(2)}) collective-permute-start(bf16[128,256]{1,0:T(8,128)(2,1)S(1)} %add.27.mine), channel_id=1, source_target_pairs={{0,1},{1,0},{2,3},{3,2},{4,5},{5,4},{6,7},{7,6},{8,9},{9,8},{10,11... | collective-permute-start | bytes 196616 | tf_op jit(solution)/shard_map/ppermute | solution.py:28

commit v4 on v3

--- a/solution.py
+++ b/solution.py
@@ -16,6 +16,7 @@
 ANY = pl.BlockSpec(memory_space=pl.ANY)
 HBM = pl.BlockSpec(memory_space=pltpu.HBM)
 VMEM = pl.BlockSpec(memory_space=pltpu.VMEM)
+SMEM = pl.BlockSpec(memory_space=pltpu.SMEM)
 
 
 def move(x, rows, cols, fn):
@@ -28,92 +29,121 @@
     return lax.ppermute(x, AXES, pairs)
 
 
-def fwd_kernel(nrow, ncol, idx0_hbm, idx1_hbm, cnt0_hbm, cnt1_hbm, vals0, vals1, *rest):
-    shards = rest[:2 * nrow]
+def fwd_blocks(todo, count, vbuf, fbuf, acc, size):
+    span = todo.shape[0] // 3
+
+    def group(i, carry):
+        prods = []
+        for u in range(UNROLL):
+            g = i * UNROLL + u
+            block = fbuf[pl.ds(pl.multiple_of(todo[span + g], size), size), :]
+            at = pl.multiple_of(todo[2 * span + g], size)
+            prods.append((at, jnp.dot(vbuf[todo[g]], block, preferred_element_type=F32)))
+        for at, out in prods:
+            acc[pl.ds(at, size), :] += out
+        return carry
+
+    lax.fori_loop(0, (count + UNROLL - 1) // UNROLL, group, 0)
+
+
+def fwd_first(nrow, ncol, idx0_hbm, idx1_hbm, cnt0_hbm, cnt1_hbm, vals0, vals1, shard0, shard1, *rest):
+    acc, later, vbuf, fbuf, todo, idx0, idx1, cnt0, cnt1, sem, meta_sem = rest
     zs = ncol // 2
-    outs = rest[2 * nrow:2 * nrow + zs]
-    vbuf, fbuf, acc, todo, idx0, idx1, cnt0, cnt1, sem, meta_sem = rest[2 * nrow + zs:]
     slots, size = vals0.shape[0], vals0.shape[1]
-    rows, _ = shards[0].shape
+    rows, _ = shard0.shape
     per = rows // size
     block_cols = nrow * per
     full = zs * rows
+    span = todo.shape[0] // 3
     me_r = lax.axis_index("row")
     me_c = lax.axis_index("col")
     me_z, me_k = me_c // 2, me_c % 2
     pairs = ((idx0_hbm, idx0), (idx1_hbm, idx1), (cnt0_hbm, cnt0), (cnt1_hbm, cnt1))
     metas = [pltpu.make_async_copy(src, dst, meta_sem.at[i]) for i, (src, dst) in enumerate(pairs)]
-    for copy in metas:
-        copy.start()
     copies = []
-    for t, vals in enumerate((vals0, vals1)):
-        copies.append(pltpu.make_async_copy(vals, vbuf.at[pl.ds(t * slots, slots)], sem.at[2 * nrow + t]))
-        for s in range(nrow):
-            at = pl.multiple_of((me_r ^ s) * rows + t * nrow * rows, rows)
-            n = t * nrow + s
-            copies.append(pltpu.make_async_copy(shards[n], fbuf.at[pl.ds(at, rows)], sem.at[n]))
-    for copy in copies:
+    for t, (vals, shard) in enumerate(((vals0, shard0), (vals1, shard1))):
+        copies.append(pltpu.make_async_copy(vals, vbuf.at[pl.ds(t * slots, slots)], sem.at[2 * t]))
+        copies.append(pltpu.make_async_copy(shard, fbuf.at[pl.ds(t * rows, rows)], sem.at[2 * t + 1]))
+    for copy in metas + copies:
         copy.start()
     acc[...] = jnp.zeros_like(acc)
-
     for copy in metas:
         copy.wait()
 
-    def listed(t, idx, cnt, n):
-        def one(g, n):
+    def listed(t, idx, cnt, counts):
+        def one(g, counts):
+            now, late = counts
             q = idx[g]
             br, bc = q // block_cols, q % block_cols
             owner = br // per
-            todo[0, n] = t * slots + g
-            todo[1, n] = t * nrow * rows + bc * size
-            todo[2, n] = ((owner // 2) ^ me_z) * rows + (br % per) * size
-            return n + jnp.where(owner % 2 == me_k, 1, 0)
-
-        return lax.fori_loop(0, cnt[0], one, n)
-
-    count = listed(1, idx1, cnt1, listed(0, idx0, cnt0, 0))
+            s = (bc // per) ^ me_r
+            at = ((owner // 2) ^ me_z) * rows + (br % per) * size
+            inside = (bc % per) * size
+            mine = owner % 2 == me_k
+            todo[now] = t * slots + g
+            todo[span + now] = t * rows + inside
+            todo[2 * span + now] = at
+            later[late] = t * slots + g
+            later[span + late] = (t * (nrow - 1) + s - 1) * rows + inside
+            later[2 * span + late] = at
+            return (
+                now + jnp.where(mine & (s == 0), 1, 0),
+                late + jnp.where(mine & (s != 0), 1, 0),
+            )
+
+        return lax.fori_loop(0, cnt[0], one, counts)
+
+    now, late = listed(1, idx1, cnt1, listed(0, idx0, cnt0, (0, 0)))
     for u in range(UNROLL):
-        todo[0, count + u] = 0
-        todo[1, count + u] = 0
-        todo[2, count + u] = full
+        for ref, n in ((todo, now), (later, late)):
+            ref[n + u] = 0
+            ref[span + n + u] = 0
+            ref[2 * span + n + u] = full
+    later[span - 1] = late
     for copy in copies:
         copy.wait()
-
-    def group(i, carry):
-        prods = []
-        for u in range(UNROLL):
-            g = i * UNROLL + u
-            block = fbuf[pl.ds(pl.multiple_of(todo[1, g], size), size), :]
-            prods.append((pl.multiple_of(todo[2, g], size), jnp.dot(vbuf[todo[0, g]], block, preferred_element_type=F32)))
-        for at, out in prods:
-            acc[pl.ds(at, size), :] += out
-        return carry
-
-    lax.fori_loop(0, (count + UNROLL - 1) // UNROLL, group, 0)
+    fwd_blocks(todo, now, vbuf, fbuf, acc, size)
+
+
+def fwd_rest(nrow, ncol, acc_in, later_hbm, vals0, vals1, *rest):
+    zs = ncol // 2
+    shards = rest[:2 * nrow - 2]
+    acc = rest[2 * nrow - 2]
+    outs = rest[2 * nrow - 1:2 * nrow - 1 + zs]
+    vbuf, fbuf, todo, sem = rest[2 * nrow - 1 + zs:]
+    slots, size = vals0.shape[0], vals0.shape[1]
+    rows, _ = shards[0].shape
+    span = todo.shape[0] // 3
+    copies = [pltpu.make_async_copy(later_hbm, todo, sem.at[2 * nrow])]
+    for t, vals in enumerate((vals0, vals1)):
+        copies.append(pltpu.make_async_copy(vals, vbuf.at[pl.ds(t * slots, slots)], sem.at[2 * nrow - 2 + t]))
+    for n in range(2 * nrow - 2):
+        copies.append(pltpu.make_async_copy(shards[n], fbuf.at[pl.ds(n * rows, rows)], sem.at[n]))
+    for copy in copies:
+        copy.start()
+    for copy in copies:
+        copy.wait()
+    fwd_blocks(todo, todo[span - 1], vbuf, fbuf, acc, size)
     for s in range(zs):
         outs[s][...] = acc[s * rows:(s + 1) * rows, :].astype(BF16)
 
 
 def bwd_kernel(nrow, ncol, idx_hbm, cnt_hbm, vals, *rest):
-    feats = rest[:nrow]
-    cots = rest[nrow:nrow + ncol]
-    outs = rest[nrow + ncol:2 * nrow + ncol]
-    tkeep, tsend, vbuf, fbuf, cbuf, acc, tbuf, idx, cnt, sem, meta_sem = rest[2 * nrow + ncol:]
+    cots = rest[:ncol]
+    outs = rest[ncol:nrow + ncol]
+    vbuf, cbuf, acc, idx, cnt, sem = rest[nrow + ncol:]
     size = vals.shape[1]
-    rows, width = feats[0].shape
+    rows, _ = cots[0].shape
     per = rows // size
     block_cols = nrow * per
     full = nrow * rows
     me_r = lax.axis_index("row")
     me_c = lax.axis_index("col")
-    me_k = me_c % 2
-    metas = [pltpu.make_async_copy(idx_hbm, idx, meta_sem.at[0]), pltpu.make_async_copy(cnt_hbm, cnt, meta_sem.at[1])]
-    copies = metas + [pltpu.make_async_copy(vals, vbuf, sem.at[nrow + ncol])]
-    for s in range(nrow):
-        copies.append(pltpu.make_async_copy(feats[s], fbuf.at[pl.ds(s * rows, rows)], sem.at[s]))
+    pairs = ((idx_hbm, idx), (cnt_hbm, cnt), (vals, vbuf))
+    copies = [pltpu.make_async_copy(src, dst, sem.at[ncol + i]) for i, (src, dst) in enumerate(pairs)]
     for s in range(ncol):
         at = pl.multiple_of((me_c ^ s) * rows, rows)
-        copies.append(pltpu.make_async_copy(cots[s], cbuf.at[pl.ds(at, rows)], sem.at[nrow + s]))
+        copies.append(pltpu.make_async_copy(cots[s], cbuf.at[pl.ds(at, rows)], sem.at[s]))
     for copy in copies:
         copy.start()
     acc[...] = jnp.zeros_like(acc)
@@ -136,15 +166,19 @@
         return carry
 
     lax.fori_loop(0, (count + UNROLL - 1) // UNROLL, group, 0)
-    term = jnp.zeros((width, width), F32)
     for s in range(nrow):
-        back = acc[s * rows:(s + 1) * rows, :].astype(BF16)
-        outs[s][...] = back
-        term += lax.dot_general(
-            fbuf[s * rows:(s + 1) * rows, :], back, (((0,), (0,)), ((), ())), preferred_element_type=F32
+        outs[s][...] = acc[s * rows:(s + 1) * rows, :].astype(BF16)
+
+
+def term_kernel(zs, *rest):
+    tkeep, tsend, tbuf = rest[2 * zs:]
+    part = tkeep.shape[0]
+    me_k = lax.axis_index("col") % 2
+    for s in range(zs):
+        out = lax.dot_general(
+            rest[s][...], rest[zs + s][...], (((0,), (0,)), ((), ())), preferred_element_type=F32
         )
-    tbuf[...] = term
-    part = width // 2
+        tbuf[...] = out if s == 0 else tbuf[...] + out
     tkeep[...] = tbuf[pl.ds(pl.multiple_of(me_k * part, part), part), :].astype(BF16)
     tsend[...] = tbuf[pl.ds(pl.multiple_of((1 - me_k) * part, part), part), :].astype(BF16)
 
@@ -177,12 +211,6 @@
 
 def ones(s):
     return s.bit_count()
-
-
-def tree(terms):
-    while len(terms) > 1:
-        terms = [terms[i] + terms[i + 1] for i in range(0, len(terms), 2)]
-    return terms[0]
 
 
 def body(features, weight, cotangent, block_index, block_count, block_values):
@@ -218,26 +246,50 @@
     feats[0] = pltpu.with_memory_space_constraint(features, pltpu.HBM)
     cots[0] = pltpu.with_memory_space_constraint(cotangent, pltpu.HBM)
 
-    parts = pl.pallas_call(
-        functools.partial(fwd_kernel, nrow, ncol),
-        out_shape=[shape((rows, width), BF16)] * zs,
-        in_specs=[ANY] * 4 + [HBM, ANY, HBM] + [ANY] * (2 * nrow - 1),
-        out_specs=[VMEM] * zs,
+    span = 2 * slots + 2 * UNROLL
+    acc, later = pl.pallas_call(
+        functools.partial(fwd_first, nrow, ncol),
+        out_shape=[shape((zs * rows + size, width), F32), shape((3 * span,), jnp.int32)],
+        in_specs=[ANY] * 4 + [HBM, ANY, HBM, ANY],
+        out_specs=[VMEM, SMEM],
         scratch_shapes=[
             pltpu.VMEM((2 * slots, size, size), BF16),
-            pltpu.VMEM((2 * nrow * rows, width), BF16),
-            pltpu.VMEM((zs * rows + size, width), F32),
-            pltpu.SMEM((3, 2 * slots + UNROLL), jnp.int32),
+            pltpu.VMEM((2 * rows, width), BF16),
+            pltpu.SMEM((3 * span,), jnp.int32),
             pltpu.SMEM((slots,), jnp.int32),
             pltpu.SMEM((slots,), jnp.int32),
             pltpu.SMEM((1,), jnp.int32),
             pltpu.SMEM((1,), jnp.int32),
-            pltpu.SemaphoreType.DMA((2 * nrow + 2,)),
+            pltpu.SemaphoreType.DMA((4,)),
             pltpu.SemaphoreType.DMA((4,)),
         ],
+        compiler_params=pltpu.CompilerParams(vmem_limit_bytes=12 << 20),
+        name="fwd_first",
+    )(idx, idx1, cnt, cnt1, vals, vals1, feats[0], feats1[0])
+    parts = pl.pallas_call(
+        functools.partial(fwd_rest, nrow, ncol),
+        out_shape=[shape(acc.shape, F32)] + [shape((rows, width), BF16)] * zs,
+        in_specs=[VMEM, ANY, HBM, ANY] + [ANY] * (2 * nrow - 2),
+        out_specs=[VMEM] * (1 + zs),
+        scratch_shapes=[
+            pltpu.VMEM((2 * slots, size, size), BF16),
+            pltpu.VMEM(((2 * nrow - 2) * rows, width), BF16),
+            pltpu.SMEM((3 * span,), jnp.int32),
+            pltpu.SemaphoreType.DMA((2 * nrow + 1,)),
+        ],
+        input_output_aliases={0: 0},
         compiler_params=pltpu.CompilerParams(vmem_limit_bytes=16 << 20),
         name="fwd_tile",
-    )(idx, idx1, cnt, cnt1, vals, vals1, *feats, *feats1)
+    )(acc, later, vals, vals1, *feats[1:], *feats1[1:])[1:]
+    term, send = pl.pallas_call(
+        functools.partial(term_kernel, zs),
+        out_shape=[shape((part, width), BF16)] * 2,
+        in_specs=[VMEM] * (2 * zs),
+        out_specs=[VMEM] * 2,
+        scratch_shapes=[pltpu.VMEM((width, width), F32)],
+        compiler_params=pltpu.CompilerParams(vmem_limit_bytes=8 << 20),
+        name="weight_term",
+    )(*parts, cotangent, *cots[2::2])
     parts = list(parts)
     final = [parts[0]]
     for s in sorted(range(1, zs), key=ones, reverse=True):
@@ -257,26 +309,22 @@
         name="hidden",
     )(weight, *parts)
 
-    out = pl.pallas_call(
+    backs = pl.pallas_call(
         functools.partial(bwd_kernel, nrow, ncol),
-        out_shape=[shape((rows, width), BF16)] * nrow + [shape((part, width), BF16)] * 2,
-        in_specs=[ANY, ANY, HBM, HBM] + [ANY] * (nrow - 1) + [HBM] + [ANY] * (ncol - 1),
-        out_specs=[VMEM] * (nrow + 2),
+        out_shape=[shape((rows, width), BF16)] * nrow,
+        in_specs=[ANY, ANY, HBM, HBM] + [ANY] * (ncol - 1),
+        out_specs=[VMEM] * nrow,
         scratch_shapes=[
             pltpu.VMEM((slots, size, size), BF16),
-            pltpu.VMEM((nrow * rows, width), BF16),
             pltpu.VMEM((ncol * rows, width), BF16),
             pltpu.VMEM((nrow * rows + size, width), F32),
-            pltpu.VMEM((width, width), F32),
             pltpu.SMEM((slots,), jnp.int32),
             pltpu.SMEM((1,), jnp.int32),
-            pltpu.SemaphoreType.DMA((nrow + ncol + 1,)),
-            pltpu.SemaphoreType.DMA((2,)),
+            pltpu.SemaphoreType.DMA((ncol + 3,)),
         ],
         compiler_params=pltpu.CompilerParams(vmem_limit_bytes=16 << 20),
         name="bwd_tile",
-    )(idx, cnt, vals, *feats, *cots)
-    backs, term, send = out[:nrow], out[nrow], out[nrow + 1]
+    )(idx, cnt, vals, *cots)
     backs = [backs[0]] + [over_row(backs[s], s) for s in range(1, nrow)]
     input_grad = pl.pallas_call(
         functools.partial(sum_dot_kernel, nrow, (((1,), (1,)), ((), ()))),
@@ -288,7 +336,8 @@
     )(weight, *backs)
 
     term = term + over_col(send, 1)
-    term = tree([term] + [over_row(term, s) for s in range(1, nrow)])
+    for s in bits(nrow):
+        term = term + over_row(term, s)
     for s in bits(zs):
         term = term + over_col(term, 2 * s)
     weight_grad = pl.pallas_call(

time: 74.6 us -> 73.8 us (0.989)
  waiting for transfers between devices: 37 us -> 30.8 us
  starting transfers between devices: 24.3 us -> 27.4 us
  Pallas kernels: 10.9 us -> 13.1 us
    ppermute x30 -> x29, waiting for transfers between devices: 37 us -> 30.8 us  [move(): return lax.ppermute(x, AXES, pairs)]
    ppermute x30 -> x29, starting transfers between devices: 24.3 us -> 27.4 us  [move(): return lax.ppermute(x, AXES, pairs)]
    pallas_call x1 -> x3, Pallas kernels: 3.85 us -> 6.67 us  [the longest x1 3.78 us: body(): pl.pallas_call(functools.partial(fwd_first, nrow, ncol), out_shape=[shape...]
  transfers between devices with their start and end apart: 30 -> 29, of which waited for: 12 -> 11; matrix products, arithmetic and copies ran while one was open for 0% -> 0% of each run, Pallas kernels for 13% -> 16%
where the time goes in v4:
time: 73.8 us; the launch traced here: 73.6 us
  waiting for transfers between devices  30.8 us (42%)
  starting transfers between devices  27.4 us (37%)
  Pallas kernels  13.1 us (18%)
  between operations  1.47 us (2%)
    ppermute x29, waiting for transfers between devices, move(): return lax.ppermute(x, AXES, pairs)  30.8 us
    ppermute x29, starting transfers between devices, move(): return lax.ppermute(x, AXES, pairs)  27.4 us
    pallas_call x1, Pallas kernels, body(): pl.pallas_call(functools.partial(fwd_first, nrow, ncol), out_shape=[shape...  3.78 us
    pallas_call x1, Pallas kernels, body(): pl.pallas_call(functools.partial(bwd_kernel, nrow, ncol), out_shape=[shap...  3.61 us
    pallas_call x1, Pallas kernels, body(): pl.pallas_call(functools.partial(fwd_rest, nrow, ncol), out_shape=[shape(...  2.38 us
  transfers between devices with their start and end apart: 29, of which 11 were waited for; matrix products, arithmetic and copies ran while one was open for 0% of the time, Pallas kernels for 16%

profile of v4, /device:TPU:0, one launch (start us, length us, event | category | flops | bytes accessed | tf_op | source)
XLA Modules:
  0.0 73.6 jit_solution(10288518015673108177)
XLA Ops:
  0.6 0.6 collective-permute-start.2
  1.2 0.1 collective-permute-start.3
  1.3 2.9 %collective-permute-start.4 = (bf16[512,256]{1,0:T(8,128)(2,1)}, bf16[512,256]{1,0:T(8,128)(2,1)S(1)}, u32[]{:S(2)}, u32[]{:S(2)}) collective-permute-start(bf16[512,256]{1,0:T(8,128)(2,1)} %shard0.1), channel_id=1, source_target_pairs={{0,8},{1,9},{2,10},{3,11},{4,12},{5,13},{6,14},{7,15},{8,0},{9,1},... | collective-permute-start | bytes 786440 | tf_op jit(solution)/shard_map/ppermute | solution.py:29
  4.2 0.5 collective-permute-start.1
  4.7 1.0 %collective-permute-done.1.cnt1_hbm = s32[1]{0:T(128)} collective-permute-done((s32[1]{0:T(128)}, s32[1]{0:T(128)}, u32[]{:S(2)}, u32[]{:S(2)}) %collective-permute-start.1) | collective-permute-done | bytes 36 | tf_op jit(solution)/shard_map/ppermute | solution.py:29
  5.6 1.5 %collective-permute-start.5 = (bf16[512,256]{1,0:T(8,128)(2,1)}, bf16[512,256]{1,0:T(8,128)(2,1)S(1)}, u32[]{:S(2)}, u32[]{:S(2)}) collective-permute-start(bf16[512,256]{1,0:T(8,128)(2,1)} %shard0.1), channel_id=1, source_target_pairs={{0,16},{1,17},{2,18},{3,19},{4,20},{5,21},{6,22},{7,23},{8,24},{9,... | collective-permute-start | bytes 786440 | tf_op jit(solution)/shard_map/ppermute | solution.py:29
  7.2 1.2 %collective-permute-start.6 = (bf16[512,256]{1,0:T(8,128)(2,1)}, bf16[512,256]{1,0:T(8,128)(2,1)S(1)}, u32[]{:S(2)}, u32[]{:S(2)}) collective-permute-start(bf16[512,256]{1,0:T(8,128)(2,1)} %shard0.1), channel_id=1, source_target_pairs={{0,24},{1,25},{2,26},{3,27},{4,28},{5,29},{6,30},{7,31},{8,16},{9,... | collective-permute-start | bytes 786440 | tf_op jit(solution)/shard_map/ppermute | solution.py:29
  8.4 2.6 %collective-permute-start.16 = (bf16[512,256]{1,0:T(8,128)(2,1)}, bf16[512,256]{1,0:T(8,128)(2,1)S(1)}, u32[]{:S(2)}, u32[]{:S(2)}) collective-permute-start(bf16[512,256]{1,0:T(8,128)(2,1)} %rest_4_.1), channel_id=1, source_target_pairs={{0,4},{1,5},{2,6},{3,7},{4,0},{5,1},{6,2},{7,3},{8,12},{9,13},{10,... | collective-permute-start | bytes 786440 | tf_op jit(solution)/shard_map/ppermute | solution.py:29
  11.0 0.6 collective-permute-done.4.rest_0_
  11.5 8.5 %collective-permute-done.5.rest_1_ = bf16[512,256]{1,0:T(8,128)(2,1)S(1)} collective-permute-done((bf16[512,256]{1,0:T(8,128)(2,1)}, bf16[512,256]{1,0:T(8,128)(2,1)S(1)}, u32[]{:S(2)}, u32[]{:S(2)}) %collective-permute-start.5) | collective-permute-done | bytes 262176 | tf_op jit(solution)/shard_map/ppermute | solution.py:29
  20.0 0.5 collective-permute-start.9
  20.5 2.4 %collective-permute-done.16.rest_4_.rest_6_ = bf16[512,256]{1,0:T(8,128)(2,1)S(1)} collective-permute-done((bf16[512,256]{1,0:T(8,128)(2,1)}, bf16[512,256]{1,0:T(8,128)(2,1)S(1)}, u32[]{:S(2)}, u32[]{:S(2)}) %collective-permute-start.16) | collective-permute-done | bytes 262176 | tf_op jit(solution)/shard_map/ppermute | solution.py:29
  22.9 0.8 %collective-permute-start.14 = (bf16[512,256]{1,0:T(8,128)(2,1)}, bf16[512,256]{1,0:T(8,128)(2,1)S(1)}, u32[]{:S(2)}, u32[]{:S(2)}) collective-permute-start(bf16[512,256]{1,0:T(8,128)(2,1)} %rest_4_.1), channel_id=1, source_target_pairs={{0,2},{1,3},{2,0},{3,1},{4,6},{5,7},{6,4},{7,5},{8,10},{9,11},{10,... | collective-permute-start | bytes 786440 | tf_op jit(solution)/shard_map/ppermute | solution.py:29
  23.7 1.2 %collective-permute-start.18 = (bf16[512,256]{1,0:T(8,128)(2,1)S(1)}, bf16[512,256]{1,0:T(8,128)(2,1)S(1)}, u32[]{:S(2)}, u32[]{:S(2)}) collective-permute-start(bf16[512,256]{1,0:T(8,128)(2,1)S(1)} %collective-permute-done.16.rest_4_.rest_6_), channel_id=1, source_target_pairs={{0,2},{1,3},{2,0},{3,1},{4,6},{5,7},{6,4},{7,5},{8,10},{9,11},{10,... | collective-permute-start | bytes 786440 | tf_op jit(solution)/shard_map/ppermute | solution.py:29
  25.6 0.0 copy-start.2
  25.6 0.6 copy-done.2
  26.2 3.8 %fwd_first.1 = (f32[2176,256]{1,0:T(8,128)S(1)}, s32[216]{0:T(256)S(1)}) custom-call(s32[32]{0:T(128)S(1)} %bitcast.6, s32[32]{0:T(128)S(1)} %collective-permute-done.idx1_hbm, s32[1]{0:T(128)} %bitcast.3.cnt0_hbm, s32[1]{0:T(128)} %collective-permute-done.1.cnt1_hbm, bf16[32,128,128]{2,1,0:T(8,128)(2,1)} %bitcast.9, ...), custom_call_target="tpu_custom_call" | custom-call | tf_op jit(solution)/shard_map/fwd_first/pallas_call | solution.py:250
  30.1 0.0 copy-start
  30.1 2.4 %fwd_tile.1 = (f32[2176,256]{1,0:T(8,128)S(1)}, bf16[512,256]{1,0:T(8,128)(2,1)S(1)}, bf16[512,256]{1,0:T(8,128)(2,1)S(1)}, bf16[512,256]{1,0:T(8,128)(2,1)S(1)}, bf16[512,256]{1,0:T(8,128)(2,1)S(1)}) custom-call(f32[2176,256]{1,0:T(8,128)S(1)} %get-tuple-element.15.acc_in, s32[216]{0:T(256)S(1)} %get-tuple-element.16.later_hbm, ...), custom_call_target="tpu_custom_call", output_to_operand_aliasing={{0}: (0, {})} | custom-call | tf_op jit(solution)/shard_map/fwd_tile/pallas_call | solution.py:269
  32.5 0.0 copy-start.3
  32.5 3.5 %collective-permute-done.18.rest_6_.rest_7_ = bf16[512,256]{1,0:T(8,128)(2,1)S(1)} collective-permute-done((bf16[512,256]{1,0:T(8,128)(2,1)S(1)}, bf16[512,256]{1,0:T(8,128)(2,1)S(1)}, u32[]{:S(2)}, u32[]{:S(2)}) %collective-permute-start.18) | collective-permute-done | bytes 262176 | tf_op jit(solution)/shard_map/ppermute | solution.py:29
  36.0 0.5 weight_term.1
  36.5 0.1 collective-permute-start.23
  36.6 1.2 %collective-permute-done.23 = bf16[128,256]{1,0:T(8,128)(2,1)S(1)} collective-permute-done((bf16[128,256]{1,0:T(8,128)(2,1)S(1)}, bf16[128,256]{1,0:T(8,128)(2,1)S(1)}, u32[]{:S(2)}, u32[]{:S(2)}) %collective-permute-start.23) | collective-permute-done | bytes 65568 | tf_op jit(solution)/shard_map/ppermute | solution.py:29
  37.9 1.0 %collective-permute-start.24 = (bf16[128,256]{1,0:T(8,128)(2,1)S(1)}, bf16[128,256]{1,0:T(8,128)(2,1)S(1)}, u32[]{:S(2)}, u32[]{:S(2)}) collective-permute-start(bf16[128,256]{1,0:T(8,128)(2,1)S(1)} %add.19), channel_id=1, source_target_pairs={{0,8},{1,9},{2,10},{3,11},{4,12},{5,13},{6,14},{7,15},{8,0},{9,1},... | collective-permute-start | bytes 196616 | tf_op jit(solution)/shard_map/ppermute | solution.py:29
  38.9 0.5 collective-permute-start.17
  39.4 0.5 collective-permute-start.19
  39.9 2.3 %collective-permute-done.24 = bf16[128,256]{1,0:T(8,128)(2,1)S(1)} collective-permute-done((bf16[128,256]{1,0:T(8,128)(2,1)S(1)}, bf16[128,256]{1,0:T(8,128)(2,1)S(1)}, u32[]{:S(2)}, u32[]{:S(2)}) %collective-permute-start.24) | collective-permute-done | bytes 65568 | tf_op jit(solution)/shard_map/ppermute | solution.py:29
  42.2 0.0 copy-start.1
  42.2 1.6 %collective-permute-start.25 = (bf16[128,256]{1,0:T(8,128)(2,1)S(1)}, bf16[128,256]{1,0:T(8,128)(2,1)S(1)}, u32[]{:S(2)}, u32[]{:S(2)}) collective-permute-start(bf16[128,256]{1,0:T(8,128)(2,1)S(1)} %add.20), channel_id=1, source_target_pairs={{0,16},{1,17},{2,18},{3,19},{4,20},{5,21},{6,22},{7,23},{8,24},{9,... | collective-permute-start | bytes 196616 | tf_op jit(solution)/shard_map/ppermute | solution.py:29
  43.8 2.7 %collective-permute-done.25 = bf16[128,256]{1,0:T(8,128)(2,1)S(1)} collective-permute-done((bf16[128,256]{1,0:T(8,128)(2,1)S(1)}, bf16[128,256]{1,0:T(8,128)(2,1)S(1)}, u32[]{:S(2)}, u32[]{:S(2)}) %collective-permute-start.25) | collective-permute-done | bytes 65568 | tf_op jit(solution)/shard_map/ppermute | solution.py:29
  46.5 1.7 %collective-permute-start.11 = (bf16[512,256]{1,0:T(8,128)(2,1)S(1)}, bf16[512,256]{1,0:T(8,128)(2,1)S(1)}, u32[]{:S(2)}, u32[]{:S(2)}) collective-permute-start(bf16[512,256]{1,0:T(8,128)(2,1)S(1)} %get-tuple-element.20.rest_3_), channel_id=1, source_target_pairs={{0,2},{1,3},{2,0},{3,1},{4,6},{5,7},{6,4},{7,5},{8,10},{9,11},{10,... | collective-permute-start | bytes 786440 | tf_op jit(solution)/shard_map/ppermute | solution.py:29
  48.3 0.3 collective-permute-start.26
  48.7 3.6 %bwd_tile.1 = (bf16[512,256]{1,0:T(8,128)(2,1)S(1)}, bf16[512,256]{1,0:T(8,128)(2,1)S(1)}, bf16[512,256]{1,0:T(8,128)(2,1)S(1)}, bf16[512,256]{1,0:T(8,128)(2,1)S(1)}) custom-call(s32[32]{0:T(128)S(1)} %bitcast.7, s32[1]{0:T(128)} %bitcast.4.cnt_hbm, bf16[32,128,128]{2,1,0:T(8,128)(2,1)} %bitcast.11, bf16[512,256]{1,0:T(8,128)(2,1)} %rest_4_.1, ...), custom_call_target="tpu_custom_call" | custom-call | tf_op jit(solution)/shard_map/bwd_tile/pallas_call | solution.py:312
  52.3 0.2 collective-permute-start.20
  52.5 1.5 %collective-permute-done.26 = bf16[128,256]{1,0:T(8,128)(2,1)S(1)} collective-permute-done((bf16[128,256]{1,0:T(8,128)(2,1)S(1)}, bf16[128,256]{1,0:T(8,128)(2,1)S(1)}, u32[]{:S(2)}, u32[]{:S(2)}) %collective-permute-start.26) | collective-permute-done | bytes 65568 | tf_op jit(solution)/shard_map/ppermute | solution.py:29
  54.0 3.7 %collective-permute-start.27 = (bf16[128,256]{1,0:T(8,128)(2,1)S(1)}, bf16[128,256]{1,0:T(8,128)(2,1)S(1)}, u32[]{:S(2)}, u32[]{:S(2)}) collective-permute-start(bf16[128,256]{1,0:T(8,128)(2,1)S(1)} %add.22), channel_id=1, source_target_pairs={{0,4},{1,5},{2,6},{3,7},{4,0},{5,1},{6,2},{7,3},{8,12},{9,13},{10,... | collective-permute-start | bytes 196616 | tf_op jit(solution)/shard_map/ppermute | solution.py:29
  57.7 1.5 %collective-permute-start.21 = (bf16[512,256]{1,0:T(8,128)(2,1)S(1)}, bf16[512,256]{1,0:T(8,128)(2,1)S(1)}, u32[]{:S(2)}, u32[]{:S(2)}) collective-permute-start(bf16[512,256]{1,0:T(8,128)(2,1)S(1)} %get-tuple-element.23), channel_id=1, source_target_pairs={{0,16},{1,17},{2,18},{3,19},{4,20},{5,21},{6,22},{7,23},{8,24},{9,... | collective-permute-start | bytes 786440 | tf_op jit(solution)/shard_map/ppermute | solution.py:29
  59.2 0.9 %collective-permute-start.22 = (bf16[512,256]{1,0:T(8,128)(2,1)S(1)}, bf16[512,256]{1,0:T(8,128)(2,1)S(1)}, u32[]{:S(2)}, u32[]{:S(2)}) collective-permute-start(bf16[512,256]{1,0:T(8,128)(2,1)S(1)} %get-tuple-element.24), channel_id=1, source_target_pairs={{0,24},{1,25},{2,26},{3,27},{4,28},{5,29},{6,30},{7,31},{8,16},{9,... | collective-permute-start | bytes 786440 | tf_op jit(solution)/shard_map/ppermute | solution.py:29
  60.1 1.4 %collective-permute-start.10 = (bf16[512,256]{1,0:T(8,128)(2,1)S(1)}, bf16[512,256]{1,0:T(8,128)(2,1)S(1)}, u32[]{:S(2)}, u32[]{:S(2)}) collective-permute-start(bf16[512,256]{1,0:T(8,128)(2,1)S(1)} %get-tuple-element.18.rest_1_), channel_id=1, source_target_pairs={{0,2},{1,3},{2,0},{3,1},{4,6},{5,7},{6,4},{7,5},{8,10},{9,11},{10,... | collective-permute-start | bytes 786440 | tf_op jit(solution)/shard_map/ppermute | solution.py:29
  61.5 0.1 add.18
  61.6 1.9 %collective-permute-start.12 = (bf16[512,256]{1,0:T(8,128)(2,1)S(1)}, bf16[512,256]{1,0:T(8,128)(2,1)S(1)}, u32[]{:S(2)}, u32[]{:S(2)}) collective-permute-start(bf16[512,256]{1,0:T(8,128)(2,1)S(1)} %add.18), channel_id=1, source_target_pairs={{0,4},{1,5},{2,6},{3,7},{4,0},{5,1},{6,2},{7,3},{8,12},{9,13},{10,... | collective-permute-start | bytes 786440 | tf_op jit(solution)/shard_map/ppermute | solution.py:29
  63.6 0.1 collective-permute-start.28
  63.7 4.3 %collective-permute-done.21.rest_2_ = bf16[512,256]{1,0:T(8,128)(2,1)S(1)} collective-permute-done((bf16[512,256]{1,0:T(8,128)(2,1)S(1)}, bf16[512,256]{1,0:T(8,128)(2,1)S(1)}, u32[]{:S(2)}, u32[]{:S(2)}) %collective-permute-start.21) | collective-permute-done | bytes 262176 | tf_op jit(solution)/shard_map/ppermute | solution.py:29
  67.9 1.1 %input_grad.1 = bf16[512,256]{1,0:T(8,128)(2,1)} custom-call(bf16[256,256]{1,0:T(8,128)(2,1)S(1)} %copy-done.1, bf16[512,256]{1,0:T(8,128)(2,1)S(1)} %get-tuple-element.21.rest_0_, bf16[512,256]{1,0:T(8,128)(2,1)S(1)} %collective-permute-done.20.rest_1_, bf16[512,256]{1,0:T(8,128)(2,1)S(1)} %collective-permute-done.21.rest_2_, ...), custom_call_target="tpu_custom_call" | custom-call | tf_op jit(solution)/shard_map/input_grad/pallas_call | solution.py:329
  69.0 0.7 weight_grad.1
  69.8 2.8 %collective-permute-done.12.rest_2_ = bf16[512,256]{1,0:T(8,128)(2,1)S(1)} collective-permute-done((bf16[512,256]{1,0:T(8,128)(2,1)S(1)}, bf16[512,256]{1,0:T(8,128)(2,1)S(1)}, u32[]{:S(2)}, u32[]{:S(2)}) %collective-permute-start.12) | collective-permute-done | bytes 262176 | tf_op jit(solution)/shard_map/ppermute | solution.py:29
  72.6 1.0 %hidden.1 = bf16[512,256]{1,0:T(8,128)(2,1)} custom-call(bf16[256,256]{1,0:T(8,128)(2,1)S(1)} %copy-done.1, bf16[512,256]{1,0:T(8,128)(2,1)S(1)} %get-tuple-element.17.rest_0_, bf16[512,256]{1,0:T(8,128)(2,1)S(1)} %collective-permute-done.10.rest_1_, bf16[512,256]{1,0:T(8,128)(2,1)S(1)} %collective-permute-done.12.rest_2_), custom_call_target="tpu_custom_call" | custom-call | tf_op jit(solution)/shard_map/hidden/pallas_call | solution.py:303
  (31 shorter events, 0.2 us)
Async XLA Ops:
  0.6 23.0 %collective-permute-start.2 = (bf16[32,128,128]{2,1,0:T(8,128)(2,1)}, bf16[32,128,128]{2,1,0:T(8,128)(2,1)S(1)}, u32[]{:S(2)}, u32[]{:S(2)}) collective-permute-start(bf16[32,128,128]{2,1,0:T(8,128)(2,1)} %bitcast.8), channel_id=1, source_target_pairs={{0,1},{1,0},{2,3},{3,2},{4,5},{5,4},{6,7},{7,6},{8,9},{9,8},{10,11... | collective-permute-start | bytes 3145736 | tf_op jit(solution)/shard_map/ppermute | solution.py:29
  1.2 7.2 %collective-permute-start.3 = (bf16[512,256]{1,0:T(8,128)(2,1)}, bf16[512,256]{1,0:T(8,128)(2,1)S(1)}, u32[]{:S(2)}, u32[]{:S(2)}) collective-permute-start(bf16[512,256]{1,0:T(8,128)(2,1)} %shard0.1), channel_id=1, source_target_pairs={{0,1},{1,0},{2,3},{3,2},{4,5},{5,4},{6,7},{7,6},{8,9},{9,8},{10,11... | collective-permute-start | bytes 786440 | tf_op jit(solution)/shard_map/ppermute | solution.py:29
  1.3 10.3 %collective-permute-start.4 = (bf16[512,256]{1,0:T(8,128)(2,1)}, bf16[512,256]{1,0:T(8,128)(2,1)S(1)}, u32[]{:S(2)}, u32[]{:S(2)}) collective-permute-start(bf16[512,256]{1,0:T(8,128)(2,1)} %shard0.1), channel_id=1, source_target_pairs={{0,8},{1,9},{2,10},{3,11},{4,12},{5,13},{6,14},{7,15},{8,0},{9,1},... | collective-permute-start | bytes 786440 | tf_op jit(solution)/shard_map/ppermute | solution.py:29
  4.2 3.0 %collective-permute-start = (s32[32]{0:T(128)}, s32[32]{0:T(128)S(1)}, u32[]{:S(2)}, u32[]{:S(2)}) collective-permute-start(s32[32]{0:T(128)} %bitcast.5), channel_id=1, source_target_pairs={{0,1},{1,0},{2,3},{3,2},{4,5},{5,4},{6,7},{7,6},{8,9},{9,8},{10,11... | collective-permute-start | bytes 392 | tf_op jit(solution)/shard_map/ppermute | solution.py:29
  4.2 1.5 %collective-permute-start.1 = (s32[1]{0:T(128)}, s32[1]{0:T(128)}, u32[]{:S(2)}, u32[]{:S(2)}) collective-permute-start(s32[1]{0:T(128)} %bitcast.1), channel_id=1, source_target_pairs={{0,1},{1,0},{2,3},{3,2},{4,5},{5,4},{6,7},{7,6},{8,9},{9,8},{10,11... | collective-permute-start | bytes 20 | tf_op jit(solution)/shard_map/ppermute | solution.py:29
  5.6 14.4 %collective-permute-start.5 = (bf16[512,256]{1,0:T(8,128)(2,1)}, bf16[512,256]{1,0:T(8,128)(2,1)S(1)}, u32[]{:S(2)}, u32[]{:S(2)}) collective-permute-start(bf16[512,256]{1,0:T(8,128)(2,1)} %shard0.1), channel_id=1, source_target_pairs={{0,16},{1,17},{2,18},{3,19},{4,20},{5,21},{6,22},{7,23},{8,24},{9,... | collective-permute-start | bytes 786440 | tf_op jit(solution)/shard_map/ppermute | solution.py:29
  7.2 12.8 %collective-permute-start.6 = (bf16[512,256]{1,0:T(8,128)(2,1)}, bf16[512,256]{1,0:T(8,128)(2,1)S(1)}, u32[]{:S(2)}, u32[]{:S(2)}) collective-permute-start(bf16[512,256]{1,0:T(8,128)(2,1)} %shard0.1), channel_id=1, source_target_pairs={{0,24},{1,25},{2,26},{3,27},{4,28},{5,29},{6,30},{7,31},{8,16},{9,... | collective-permute-start | bytes 786440 | tf_op jit(solution)/shard_map/ppermute | solution.py:29
  8.4 14.5 %collective-permute-start.16 = (bf16[512,256]{1,0:T(8,128)(2,1)}, bf16[512,256]{1,0:T(8,128)(2,1)S(1)}, u32[]{:S(2)}, u32[]{:S(2)}) collective-permute-start(bf16[512,256]{1,0:T(8,128)(2,1)} %rest_4_.1), channel_id=1, source_target_pairs={{0,4},{1,5},{2,6},{3,7},{4,0},{5,1},{6,2},{7,3},{8,12},{9,13},{10,... | collective-permute-start | bytes 786440 | tf_op jit(solution)/shard_map/ppermute | solution.py:29
  11.5 18.5 %collective-permute-start.7 = (bf16[512,256]{1,0:T(8,128)(2,1)S(1)}, bf16[512,256]{1,0:T(8,128)(2,1)S(1)}, u32[]{:S(2)}, u32[]{:S(2)}) collective-permute-start(bf16[512,256]{1,0:T(8,128)(2,1)S(1)} %collective-permute-done.4.rest_0_), channel_id=1, source_target_pairs={{0,1},{1,0},{2,3},{3,2},{4,5},{5,4},{6,7},{7,6},{8,9},{9,8},{10,11... | collective-permute-start | bytes 786440 | tf_op jit(solution)/shard_map/ppermute | solution.py:29
  20.0 10.0 %collective-permute-start.8 = (bf16[512,256]{1,0:T(8,128)(2,1)S(1)}, bf16[512,256]{1,0:T(8,128)(2,1)S(1)}, u32[]{:S(2)}, u32[]{:S(2)}) collective-permute-start(bf16[512,256]{1,0:T(8,128)(2,1)S(1)} %collective-permute-done.5.rest_1_), channel_id=1, source_target_pairs={{0,1},{1,0},{2,3},{3,2},{4,5},{5,4},{6,7},{7,6},{8,9},{9,8},{10,11... | collective-permute-start | bytes 786440 | tf_op jit(solution)/shard_map/ppermute | solution.py:29
  20.0 10.0 %collective-permute-start.9 = (bf16[512,256]{1,0:T(8,128)(2,1)S(1)}, bf16[512,256]{1,0:T(8,128)(2,1)S(1)}, u32[]{:S(2)}, u32[]{:S(2)}) collective-permute-start(bf16[512,256]{1,0:T(8,128)(2,1)S(1)} %collective-permute-done.6.rest_2_), channel_id=1, source_target_pairs={{0,1},{1,0},{2,3},{3,2},{4,5},{5,4},{6,7},{7,6},{8,9},{9,8},{10,11... | collective-permute-start | bytes 786440 | tf_op jit(solution)/shard_map/ppermute | solution.py:29
  22.9 9.6 %collective-permute-start.14 = (bf16[512,256]{1,0:T(8,128)(2,1)}, bf16[512,256]{1,0:T(8,128)(2,1)S(1)}, u32[]{:S(2)}, u32[]{:S(2)}) collective-permute-start(bf16[512,256]{1,0:T(8,128)(2,1)} %rest_4_.1), channel_id=1, source_target_pairs={{0,2},{1,3},{2,0},{3,1},{4,6},{5,7},{6,4},{7,5},{8,10},{9,11},{10,... | collective-permute-start | bytes 786440 | tf_op jit(solution)/shard_map/ppermute | solution.py:29
  23.7 12.3 %collective-permute-start.18 = (bf16[512,256]{1,0:T(8,128)(2,1)S(1)}, bf16[512,256]{1,0:T(8,128)(2,1)S(1)}, u32[]{:S(2)}, u32[]{:S(2)}) collective-permute-start(bf16[512,256]{1,0:T(8,128)(2,1)S(1)} %collective-permute-done.16.rest_4_.rest_6_), channel_id=1, source_target_pairs={{0,2},{1,3},{2,0},{3,1},{4,6},{5,7},{6,4},{7,5},{8,10},{9,11},{10,... | collective-permute-start | bytes 786440 | tf_op jit(solution)/shard_map/ppermute | solution.py:29
  25.6 0.7 copy-start.2
  30.1 5.9 %copy-start = (bf16[512,256]{1,0:T(8,128)(2,1)S(1)}, bf16[512,256]{1,0:T(8,128)(2,1)}, u32[]{:S(2)}) copy-start(bf16[512,256]{1,0:T(8,128)(2,1)} %rest_4_.1) | copy-start | bytes 786436
  32.5 16.2 %copy-start.3 = (s32[1,1,32]{2,1,0:T(1,128)S(1)}, s32[1,1,32]{2,1,0:T(1,128)}, u32[]{:S(2)}) copy-start(s32[1,1,32]{2,1,0:T(1,128)} %param.9) | copy-start | bytes 388
  36.5 1.3 %collective-permute-start.23 = (bf16[128,256]{1,0:T(8,128)(2,1)S(1)}, bf16[128,256]{1,0:T(8,128)(2,1)S(1)}, u32[]{:S(2)}, u32[]{:S(2)}) collective-permute-start(bf16[128,256]{1,0:T(8,128)(2,1)S(1)} %get-tuple-element.26), channel_id=1, source_target_pairs={{0,1},{1,0},{2,3},{3,2},{4,5},{5,4},{6,7},{7,6},{8,9},{9,8},{10,11... | collective-permute-start | bytes 196616 | tf_op jit(solution)/shard_map/ppermute | solution.py:29
  37.9 4.3 %collective-permute-start.24 = (bf16[128,256]{1,0:T(8,128)(2,1)S(1)}, bf16[128,256]{1,0:T(8,128)(2,1)S(1)}, u32[]{:S(2)}, u32[]{:S(2)}) collective-permute-start(bf16[128,256]{1,0:T(8,128)(2,1)S(1)} %add.19), channel_id=1, source_target_pairs={{0,8},{1,9},{2,10},{3,11},{4,12},{5,13},{6,14},{7,15},{8,0},{9,1},... | collective-permute-start | bytes 196616 | tf_op jit(solution)/shard_map/ppermute | solution.py:29
  38.9 9.5 %collective-permute-start.13 = (bf16[512,256]{1,0:T(8,128)(2,1)S(1)}, bf16[512,256]{1,0:T(8,128)(2,1)S(1)}, u32[]{:S(2)}, u32[]{:S(2)}) collective-permute-start(bf16[512,256]{1,0:T(8,128)(2,1)S(1)} %copy-done), channel_id=1, source_target_pairs={{0,1},{1,0},{2,3},{3,2},{4,5},{5,4},{6,7},{7,6},{8,9},{9,8},{10,11... | collective-permute-start | bytes 786440 | tf_op jit(solution)/shard_map/ppermute | solution.py:29
  38.9 9.8 %collective-permute-start.17 = (bf16[512,256]{1,0:T(8,128)(2,1)S(1)}, bf16[512,256]{1,0:T(8,128)(2,1)S(1)}, u32[]{:S(2)}, u32[]{:S(2)}) collective-permute-start(bf16[512,256]{1,0:T(8,128)(2,1)S(1)} %collective-permute-done.16.rest_4_.rest_6_), channel_id=1, source_target_pairs={{0,1},{1,0},{2,3},{3,2},{4,5},{5,4},{6,7},{7,6},{8,9},{9,8},{10,11... | collective-permute-start | bytes 786440 | tf_op jit(solution)/shard_map/ppermute | solution.py:29
  39.4 9.3 %collective-permute-start.15 = (bf16[512,256]{1,0:T(8,128)(2,1)S(1)}, bf16[512,256]{1,0:T(8,128)(2,1)S(1)}, u32[]{:S(2)}, u32[]{:S(2)}) collective-permute-start(bf16[512,256]{1,0:T(8,128)(2,1)S(1)} %collective-permute-done.14.rest_2_.rest_5_), channel_id=1, source_target_pairs={{0,1},{1,0},{2,3},{3,2},{4,5},{5,4},{6,7},{7,6},{8,9},{9,8},{10,11... | collective-permute-start | bytes 786440 | tf_op jit(solution)/shard_map/ppermute | solution.py:29
  39.4 9.3 %collective-permute-start.19 = (bf16[512,256]{1,0:T(8,128)(2,1)S(1)}, bf16[512,256]{1,0:T(8,128)(2,1)S(1)}, u32[]{:S(2)}, u32[]{:S(2)}) collective-permute-start(bf16[512,256]{1,0:T(8,128)(2,1)S(1)} %collective-permute-done.18.rest_6_.rest_7_), channel_id=1, source_target_pairs={{0,1},{1,0},{2,3},{3,2},{4,5},{5,4},{6,7},{7,6},{8,9},{9,8},{10,11... | collective-permute-start | bytes 786440 | tf_op jit(solution)/shard_map/ppermute | solution.py:29
  42.2 25.7 %copy-start.1 = (bf16[256,256]{1,0:T(8,128)(2,1)S(1)}, bf16[256,256]{1,0:T(8,128)(2,1)}, u32[]{:S(2)}) copy-start(bf16[256,256]{1,0:T(8,128)(2,1)} %w.3) | copy-start | bytes 393220
  42.2 4.3 %collective-permute-start.25 = (bf16[128,256]{1,0:T(8,128)(2,1)S(1)}, bf16[128,256]{1,0:T(8,128)(2,1)S(1)}, u32[]{:S(2)}, u32[]{:S(2)}) collective-permute-start(bf16[128,256]{1,0:T(8,128)(2,1)S(1)} %add.20), channel_id=1, source_target_pairs={{0,16},{1,17},{2,18},{3,19},{4,20},{5,21},{6,22},{7,23},{8,24},{9,... | collective-permute-start | bytes 196616 | tf_op jit(solution)/shard_map/ppermute | solution.py:29
  46.5 13.6 %collective-permute-start.11 = (bf16[512,256]{1,0:T(8,128)(2,1)S(1)}, bf16[512,256]{1,0:T(8,128)(2,1)S(1)}, u32[]{:S(2)}, u32[]{:S(2)}) collective-permute-start(bf16[512,256]{1,0:T(8,128)(2,1)S(1)} %get-tuple-element.20.rest_3_), channel_id=1, source_target_pairs={{0,2},{1,3},{2,0},{3,1},{4,6},{5,7},{6,4},{7,5},{8,10},{9,11},{10,... | collective-permute-start | bytes 786440 | tf_op jit(solution)/shard_map/ppermute | solution.py:29
  48.3 5.7 %collective-permute-start.26 = (bf16[128,256]{1,0:T(8,128)(2,1)S(1)}, bf16[128,256]{1,0:T(8,128)(2,1)S(1)}, u32[]{:S(2)}, u32[]{:S(2)}) collective-permute-start(bf16[128,256]{1,0:T(8,128)(2,1)S(1)} %add.21), channel_id=1, source_target_pairs={{0,2},{1,3},{2,0},{3,1},{4,6},{5,7},{6,4},{7,5},{8,10},{9,11},{10,... | collective-permute-start | bytes 196616 | tf_op jit(solution)/shard_map/ppermute | solution.py:29
  52.3 11.3 %collective-permute-start.20 = (bf16[512,256]{1,0:T(8,128)(2,1)S(1)}, bf16[512,256]{1,0:T(8,128)(2,1)S(1)}, u32[]{:S(2)}, u32[]{:S(2)}) collective-permute-start(bf16[512,256]{1,0:T(8,128)(2,1)S(1)} %get-tuple-element.22), channel_id=1, source_target_pairs={{0,8},{1,9},{2,10},{3,11},{4,12},{5,13},{6,14},{7,15},{8,0},{9,1},... | collective-permute-start | bytes 786440 | tf_op jit(solution)/shard_map/ppermute | solution.py:29
  54.0 7.6 %collective-permute-start.27 = (bf16[128,256]{1,0:T(8,128)(2,1)S(1)}, bf16[128,256]{1,0:T(8,128)(2,1)S(1)}, u32[]{:S(2)}, u32[]{:S(2)}) collective-permute-start(bf16[128,256]{1,0:T(8,128)(2,1)S(1)} %add.22), channel_id=1, source_target_pairs={{0,4},{1,5},{2,6},{3,7},{4,0},{5,1},{6,2},{7,3},{8,12},{9,13},{10,... | collective-permute-start | bytes 196616 | tf_op jit(solution)/shard_map/ppermute | solution.py:29
  57.7 10.2 %collective-permute-start.21 = (bf16[512,256]{1,0:T(8,128)(2,1)S(1)}, bf16[512,256]{1,0:T(8,128)(2,1)S(1)}, u32[]{:S(2)}, u32[]{:S(2)}) collective-permute-start(bf16[512,256]{1,0:T(8,128)(2,1)S(1)} %get-tuple-element.23), channel_id=1, source_target_pairs={{0,16},{1,17},{2,18},{3,19},{4,20},{5,21},{6,22},{7,23},{8,24},{9,... | collective-permute-start | bytes 786440 | tf_op jit(solution)/shard_map/ppermute | solution.py:29
  59.2 8.7 %collective-permute-start.22 = (bf16[512,256]{1,0:T(8,128)(2,1)S(1)}, bf16[512,256]{1,0:T(8,128)(2,1)S(1)}, u32[]{:S(2)}, u32[]{:S(2)}) collective-permute-start(bf16[512,256]{1,0:T(8,128)(2,1)S(1)} %get-tuple-element.24), channel_id=1, source_target_pairs={{0,24},{1,25},{2,26},{3,27},{4,28},{5,29},{6,30},{7,31},{8,16},{9,... | collective-permute-start | bytes 786440 | tf_op jit(solution)/shard_map/ppermute | solution.py:29
  60.1 9.7 %collective-permute-start.10 = (bf16[512,256]{1,0:T(8,128)(2,1)S(1)}, bf16[512,256]{1,0:T(8,128)(2,1)S(1)}, u32[]{:S(2)}, u32[]{:S(2)}) collective-permute-start(bf16[512,256]{1,0:T(8,128)(2,1)S(1)} %get-tuple-element.18.rest_1_), channel_id=1, source_target_pairs={{0,2},{1,3},{2,0},{3,1},{4,6},{5,7},{6,4},{7,5},{8,10},{9,11},{10,... | collective-permute-start | bytes 786440 | tf_op jit(solution)/shard_map/ppermute | solution.py:29
  61.6 10.9 %collective-permute-start.12 = (bf16[512,256]{1,0:T(8,128)(2,1)S(1)}, bf16[512,256]{1,0:T(8,128)(2,1)S(1)}, u32[]{:S(2)}, u32[]{:S(2)}) collective-permute-start(bf16[512,256]{1,0:T(8,128)(2,1)S(1)} %add.18), channel_id=1, source_target_pairs={{0,4},{1,5},{2,6},{3,7},{4,0},{5,1},{6,2},{7,3},{8,12},{9,13},{10,... | collective-permute-start | bytes 786440 | tf_op jit(solution)/shard_map/ppermute | solution.py:29
  63.6 5.4 %collective-permute-start.28 = (bf16[128,256]{1,0:T(8,128)(2,1)S(1)}, bf16[128,256]{1,0:T(8,128)(2,1)S(1)}, u32[]{:S(2)}, u32[]{:S(2)}) collective-permute-start(bf16[128,256]{1,0:T(8,128)(2,1)S(1)} %add.23.mine), channel_id=1, source_target_pairs={{0,1},{1,0},{2,3},{3,2},{4,5},{5,4},{6,7},{7,6},{8,9},{9,8},{10,11... | collective-permute-start | bytes 196616 | tf_op jit(solution)/shard_map/ppermute | solution.py:29

commit v5 on v3

--- a/solution.py
+++ b/solution.py
@@ -12,7 +12,7 @@
 AXES = ("row", "col")
 F32 = jnp.float32
 BF16 = jnp.bfloat16
-UNROLL = 4
+UNROLL = 16
 ANY = pl.BlockSpec(memory_space=pl.ANY)
 HBM = pl.BlockSpec(memory_space=pltpu.HBM)
 VMEM = pl.BlockSpec(memory_space=pltpu.VMEM)
@@ -95,25 +95,21 @@
 
 
 def bwd_kernel(nrow, ncol, idx_hbm, cnt_hbm, vals, *rest):
-    feats = rest[:nrow]
-    cots = rest[nrow:nrow + ncol]
-    outs = rest[nrow + ncol:2 * nrow + ncol]
-    tkeep, tsend, vbuf, fbuf, cbuf, acc, tbuf, idx, cnt, sem, meta_sem = rest[2 * nrow + ncol:]
+    cots = rest[:ncol]
+    outs = rest[ncol:nrow + ncol]
+    vbuf, cbuf, acc, idx, cnt, sem = rest[nrow + ncol:]
     size = vals.shape[1]
-    rows, width = feats[0].shape
+    rows, _ = cots[0].shape
     per = rows // size
     block_cols = nrow * per
     full = nrow * rows
     me_r = lax.axis_index("row")
     me_c = lax.axis_index("col")
-    me_k = me_c % 2
-    metas = [pltpu.make_async_copy(idx_hbm, idx, meta_sem.at[0]), pltpu.make_async_copy(cnt_hbm, cnt, meta_sem.at[1])]
-    copies = metas + [pltpu.make_async_copy(vals, vbuf, sem.at[nrow + ncol])]
-    for s in range(nrow):
-        copies.append(pltpu.make_async_copy(feats[s], fbuf.at[pl.ds(s * rows, rows)], sem.at[s]))
+    pairs = ((idx_hbm, idx), (cnt_hbm, cnt), (vals, vbuf))
+    copies = [pltpu.make_async_copy(src, dst, sem.at[ncol + i]) for i, (src, dst) in enumerate(pairs)]
     for s in range(ncol):
         at = pl.multiple_of((me_c ^ s) * rows, rows)
-        copies.append(pltpu.make_async_copy(cots[s], cbuf.at[pl.ds(at, rows)], sem.at[nrow + s]))
+        copies.append(pltpu.make_async_copy(cots[s], cbuf.at[pl.ds(at, rows)], sem.at[s]))
     for copy in copies:
         copy.start()
     acc[...] = jnp.zeros_like(acc)
@@ -136,15 +132,19 @@
         return carry
 
     lax.fori_loop(0, (count + UNROLL - 1) // UNROLL, group, 0)
-    term = jnp.zeros((width, width), F32)
     for s in range(nrow):
-        back = acc[s * rows:(s + 1) * rows, :].astype(BF16)
-        outs[s][...] = back
-        term += lax.dot_general(
-            fbuf[s * rows:(s + 1) * rows, :], back, (((0,), (0,)), ((), ())), preferred_element_type=F32
+        outs[s][...] = acc[s * rows:(s + 1) * rows, :].astype(BF16)
+
+
+def term_kernel(zs, *rest):
+    tkeep, tsend, tbuf = rest[2 * zs:]
+    part = tkeep.shape[0]
+    me_k = lax.axis_index("col") % 2
+    for s in range(zs):
+        out = lax.dot_general(
+            rest[s][...], rest[zs + s][...], (((0,), (0,)), ((), ())), preferred_element_type=F32
         )
-    tbuf[...] = term
-    part = width // 2
+        tbuf[...] = out if s == 0 else tbuf[...] + out
     tkeep[...] = tbuf[pl.ds(pl.multiple_of(me_k * part, part), part), :].astype(BF16)
     tsend[...] = tbuf[pl.ds(pl.multiple_of((1 - me_k) * part, part), part), :].astype(BF16)
 
@@ -177,12 +177,6 @@
 
 def ones(s):
     return s.bit_count()
-
-
-def tree(terms):
-    while len(terms) > 1:
-        terms = [terms[i] + terms[i + 1] for i in range(0, len(terms), 2)]
-    return terms[0]
 
 
 def body(features, weight, cotangent, block_index, block_count, block_values):
@@ -238,6 +232,15 @@
         compiler_params=pltpu.CompilerParams(vmem_limit_bytes=16 << 20),
         name="fwd_tile",
     )(idx, idx1, cnt, cnt1, vals, vals1, *feats, *feats1)
+    term, send = pl.pallas_call(
+        functools.partial(term_kernel, zs),
+        out_shape=[shape((part, width), BF16)] * 2,
+        in_specs=[VMEM] * (2 * zs),
+        out_specs=[VMEM] * 2,
+        scratch_shapes=[pltpu.VMEM((width, width), F32)],
+        compiler_params=pltpu.CompilerParams(vmem_limit_bytes=8 << 20),
+        name="weight_term",
+    )(*parts, cotangent, *cots[2::2])
     parts = list(parts)
     final = [parts[0]]
     for s in sorted(range(1, zs), key=ones, reverse=True):
@@ -257,26 +260,22 @@
         name="hidden",
     )(weight, *parts)
 
-    out = pl.pallas_call(
+    backs = pl.pallas_call(
         functools.partial(bwd_kernel, nrow, ncol),
-        out_shape=[shape((rows, width), BF16)] * nrow + [shape((part, width), BF16)] * 2,
-        in_specs=[ANY, ANY, HBM, HBM] + [ANY] * (nrow - 1) + [HBM] + [ANY] * (ncol - 1),
-        out_specs=[VMEM] * (nrow + 2),
+        out_shape=[shape((rows, width), BF16)] * nrow,
+        in_specs=[ANY, ANY, HBM, HBM] + [ANY] * (ncol - 1),
+        out_specs=[VMEM] * nrow,
         scratch_shapes=[
             pltpu.VMEM((slots, size, size), BF16),
-            pltpu.VMEM((nrow * rows, width), BF16),
             pltpu.VMEM((ncol * rows, width), BF16),
             pltpu.VMEM((nrow * rows + size, width), F32),
-            pltpu.VMEM((width, width), F32),
             pltpu.SMEM((slots,), jnp.int32),
             pltpu.SMEM((1,), jnp.int32),
-            pltpu.SemaphoreType.DMA((nrow + ncol + 1,)),
-            pltpu.SemaphoreType.DMA((2,)),
+            pltpu.SemaphoreType.DMA((ncol + 3,)),
         ],
         compiler_params=pltpu.CompilerParams(vmem_limit_bytes=16 << 20),
         name="bwd_tile",
-    )(idx, cnt, vals, *feats, *cots)
-    backs, term, send = out[:nrow], out[nrow], out[nrow + 1]
+    )(idx, cnt, vals, *cots)
     backs = [backs[0]] + [over_row(backs[s], s) for s in range(1, nrow)]
     input_grad = pl.pallas_call(
         functools.partial(sum_dot_kernel, nrow, (((1,), (1,)), ((), ()))),
@@ -288,7 +287,8 @@
     )(weight, *backs)
 
     term = term + over_col(send, 1)
-    term = tree([term] + [over_row(term, s) for s in range(1, nrow)])
+    for s in bits(nrow):
+        term = term + over_row(term, s)
     for s in bits(zs):
         term = term + over_col(term, 2 * s)
     weight_grad = pl.pallas_call(

time: 74.6 us -> 76.8 us (1.029)
  starting transfers between devices: 24.3 us -> 29 us
  Pallas kernels: 10.9 us -> 9.46 us
    ppermute x30 -> x29, starting transfers between devices: 24.3 us -> 29 us  [move(): return lax.ppermute(x, AXES, pairs)]
    pallas_call x1, Pallas kernels: 4.18 us -> 2.44 us  [body(): pl.pallas_call(functools.partial(bwd_kernel, nrow, ncol), out_shape=[shap...]
    ppermute x30 -> x29, waiting for transfers between devices: 37 us -> 36.6 us  [move(): return lax.ppermute(x, AXES, pairs)]
  transfers between devices with their start and end apart: 30 -> 29, of which waited for: 12 -> 12; matrix products, arithmetic and copies ran while one was open for 0% -> 0% of each run, Pallas kernels for 13% -> 10%
where the time goes in v5:
time: 76.8 us; the launch traced here: 76.6 us
  waiting for transfers between devices  36.6 us (48%)
  starting transfers between devices  29 us (38%)
  Pallas kernels  9.46 us (12%)
  between operations  1.44 us (2%)
    ppermute x29, waiting for transfers between devices, move(): return lax.ppermute(x, AXES, pairs)  36.6 us
    ppermute x29, starting transfers between devices, move(): return lax.ppermute(x, AXES, pairs)  29 us
    pallas_call x1, Pallas kernels, body(): pl.pallas_call(functools.partial(fwd_kernel, nrow, ncol), out_shape=[shap...  3.67 us
    pallas_call x1, Pallas kernels, body(): pl.pallas_call(functools.partial(bwd_kernel, nrow, ncol), out_shape=[shap...  2.44 us
  transfers between devices with their start and end apart: 29, of which 12 were waited for; matrix products, arithmetic and copies ran while one was open for 0% of the time, Pallas kernels for 10%

profile of v5, /device:TPU:0, one launch (start us, length us, event | category | flops | bytes accessed | tf_op | source)
XLA Modules:
  0.0 76.6 jit_solution(2163430081984397395)
XLA Ops:
  0.6 0.6 collective-permute-start.2
  1.2 2.6 %collective-permute-start.3 = (bf16[512,256]{1,0:T(8,128)(2,1)}, bf16[512,256]{1,0:T(8,128)(2,1)S(1)}, u32[]{:S(2)}, u32[]{:S(2)}) collective-permute-start(bf16[512,256]{1,0:T(8,128)(2,1)} %rest_0_.2), channel_id=1, source_target_pairs={{0,8},{1,9},{2,10},{3,11},{4,12},{5,13},{6,14},{7,15},{8,0},{9,1},... | collective-permute-start | bytes 786440 | tf_op jit(solution)/shard_map/ppermute | solution.py:28
  3.8 1.5 %collective-permute-start.4 = (bf16[512,256]{1,0:T(8,128)(2,1)}, bf16[512,256]{1,0:T(8,128)(2,1)S(1)}, u32[]{:S(2)}, u32[]{:S(2)}) collective-permute-start(bf16[512,256]{1,0:T(8,128)(2,1)} %rest_0_.2), channel_id=1, source_target_pairs={{0,16},{1,17},{2,18},{3,19},{4,20},{5,21},{6,22},{7,23},{8,24},{9,... | collective-permute-start | bytes 786440 | tf_op jit(solution)/shard_map/ppermute | solution.py:28
  5.3 0.0 collective-permute-start
  5.3 0.5 collective-permute-start.1
  5.8 1.0 %collective-permute-done.1.cnt1_hbm = s32[1]{0:T(128)} collective-permute-done((s32[1]{0:T(128)}, s32[1]{0:T(128)}, u32[]{:S(2)}, u32[]{:S(2)}) %collective-permute-start.1) | collective-permute-done | bytes 36 | tf_op jit(solution)/shard_map/ppermute | solution.py:28
  6.7 0.8 collective-permute-start.5
  7.5 0.0 collective-permute-done.idx1_hbm
  7.5 0.0 collective-permute-start.6
  7.5 3.6 %collective-permute-done.3.rest_1_ = bf16[512,256]{1,0:T(8,128)(2,1)S(1)} collective-permute-done((bf16[512,256]{1,0:T(8,128)(2,1)}, bf16[512,256]{1,0:T(8,128)(2,1)S(1)}, u32[]{:S(2)}, u32[]{:S(2)}) %collective-permute-start.3) | collective-permute-done | bytes 262176 | tf_op jit(solution)/shard_map/ppermute | solution.py:28
  11.1 3.1 %collective-permute-start.16 = (bf16[512,256]{1,0:T(8,128)(2,1)}, bf16[512,256]{1,0:T(8,128)(2,1)S(1)}, u32[]{:S(2)}, u32[]{:S(2)}) collective-permute-start(bf16[512,256]{1,0:T(8,128)(2,1)} %rest_4_.1), channel_id=1, source_target_pairs={{0,4},{1,5},{2,6},{3,7},{4,0},{5,1},{6,2},{7,3},{8,12},{9,13},{10,... | collective-permute-start | bytes 786440 | tf_op jit(solution)/shard_map/ppermute | solution.py:28
  14.2 3.7 %collective-permute-done.4.rest_2_ = bf16[512,256]{1,0:T(8,128)(2,1)S(1)} collective-permute-done((bf16[512,256]{1,0:T(8,128)(2,1)}, bf16[512,256]{1,0:T(8,128)(2,1)S(1)}, u32[]{:S(2)}, u32[]{:S(2)}) %collective-permute-start.4) | collective-permute-done | bytes 262176 | tf_op jit(solution)/shard_map/ppermute | solution.py:28
  17.9 0.5 collective-permute-start.8
  18.5 0.1 collective-permute-start.9
  18.5 7.1 %collective-permute-done.16.rest_4_.rest_6_ = bf16[512,256]{1,0:T(8,128)(2,1)S(1)} collective-permute-done((bf16[512,256]{1,0:T(8,128)(2,1)}, bf16[512,256]{1,0:T(8,128)(2,1)S(1)}, u32[]{:S(2)}, u32[]{:S(2)}) %collective-permute-start.16) | collective-permute-done | bytes 262176 | tf_op jit(solution)/shard_map/ppermute | solution.py:28
  25.7 0.7 collective-permute-start.14
  26.4 1.3 %collective-permute-start.18 = (bf16[512,256]{1,0:T(8,128)(2,1)S(1)}, bf16[512,256]{1,0:T(8,128)(2,1)S(1)}, u32[]{:S(2)}, u32[]{:S(2)}) collective-permute-start(bf16[512,256]{1,0:T(8,128)(2,1)S(1)} %collective-permute-done.16.rest_4_.rest_6_), channel_id=1, source_target_pairs={{0,2},{1,3},{2,0},{3,1},{4,6},{5,7},{6,4},{7,5},{8,10},{9,11},{10,... | collective-permute-start | bytes 786440 | tf_op jit(solution)/shard_map/ppermute | solution.py:28
  28.4 0.0 copy-start
  28.4 3.7 %fwd_tile.1 = (bf16[512,256]{1,0:T(8,128)(2,1)S(1)}, bf16[512,256]{1,0:T(8,128)(2,1)S(1)}, bf16[512,256]{1,0:T(8,128)(2,1)S(1)}, bf16[512,256]{1,0:T(8,128)(2,1)S(1)}) custom-call(s32[32]{0:T(128)S(1)} %bitcast.6, s32[32]{0:T(128)S(1)} %collective-permute-done.idx1_hbm, s32[1]{0:T(128)} %bitcast.3.cnt0_hbm, s32[1]{0:T(128)} %collective-permute-done.1.cnt1_hbm, ...), custom_call_target="tpu_custom_call" | custom-call | tf_op jit(solution)/shard_map/fwd_tile/pallas_call | solution.py:215
  32.1 3.0 %collective-permute-done.14.rest_2_.rest_5_ = bf16[512,256]{1,0:T(8,128)(2,1)S(1)} collective-permute-done((bf16[512,256]{1,0:T(8,128)(2,1)}, bf16[512,256]{1,0:T(8,128)(2,1)S(1)}, u32[]{:S(2)}, u32[]{:S(2)}) %collective-permute-start.14) | collective-permute-done | bytes 262176 | tf_op jit(solution)/shard_map/ppermute | solution.py:28
  35.0 3.7 %collective-permute-done.18.rest_6_.rest_7_ = bf16[512,256]{1,0:T(8,128)(2,1)S(1)} collective-permute-done((bf16[512,256]{1,0:T(8,128)(2,1)S(1)}, bf16[512,256]{1,0:T(8,128)(2,1)S(1)}, u32[]{:S(2)}, u32[]{:S(2)}) %collective-permute-start.18) | collective-permute-done | bytes 262176 | tf_op jit(solution)/shard_map/ppermute | solution.py:28
  38.7 0.5 weight_term.1
  39.2 0.1 collective-permute-start.23
  39.3 1.2 %collective-permute-done.23 = bf16[128,256]{1,0:T(8,128)(2,1)S(1)} collective-permute-done((bf16[128,256]{1,0:T(8,128)(2,1)S(1)}, bf16[128,256]{1,0:T(8,128)(2,1)S(1)}, u32[]{:S(2)}, u32[]{:S(2)}) %collective-permute-start.23) | collective-permute-done | bytes 65568 | tf_op jit(solution)/shard_map/ppermute | solution.py:28
  40.6 1.6 %collective-permute-start.24 = (bf16[128,256]{1,0:T(8,128)(2,1)S(1)}, bf16[128,256]{1,0:T(8,128)(2,1)S(1)}, u32[]{:S(2)}, u32[]{:S(2)}) collective-permute-start(bf16[128,256]{1,0:T(8,128)(2,1)S(1)} %add.19), channel_id=1, source_target_pairs={{0,8},{1,9},{2,10},{3,11},{4,12},{5,13},{6,14},{7,15},{8,0},{9,1},... | collective-permute-start | bytes 196616 | tf_op jit(solution)/shard_map/ppermute | solution.py:28
  42.1 0.5 collective-permute-start.17
  42.7 0.5 collective-permute-start.19
  43.2 1.8 %collective-permute-done.24 = bf16[128,256]{1,0:T(8,128)(2,1)S(1)} collective-permute-done((bf16[128,256]{1,0:T(8,128)(2,1)S(1)}, bf16[128,256]{1,0:T(8,128)(2,1)S(1)}, u32[]{:S(2)}, u32[]{:S(2)}) %collective-permute-start.24) | collective-permute-done | bytes 65568 | tf_op jit(solution)/shard_map/ppermute | solution.py:28
  44.9 1.6 %collective-permute-start.25 = (bf16[128,256]{1,0:T(8,128)(2,1)S(1)}, bf16[128,256]{1,0:T(8,128)(2,1)S(1)}, u32[]{:S(2)}, u32[]{:S(2)}) collective-permute-start(bf16[128,256]{1,0:T(8,128)(2,1)S(1)} %add.20), channel_id=1, source_target_pairs={{0,16},{1,17},{2,18},{3,19},{4,20},{5,21},{6,22},{7,23},{8,24},{9,... | collective-permute-start | bytes 196616 | tf_op jit(solution)/shard_map/ppermute | solution.py:28
  46.5 2.8 %collective-permute-done.25 = bf16[128,256]{1,0:T(8,128)(2,1)S(1)} collective-permute-done((bf16[128,256]{1,0:T(8,128)(2,1)S(1)}, bf16[128,256]{1,0:T(8,128)(2,1)S(1)}, u32[]{:S(2)}, u32[]{:S(2)}) %collective-permute-start.25) | collective-permute-done | bytes 65568 | tf_op jit(solution)/shard_map/ppermute | solution.py:28
  49.3 1.7 %collective-permute-start.11 = (bf16[512,256]{1,0:T(8,128)(2,1)S(1)}, bf16[512,256]{1,0:T(8,128)(2,1)S(1)}, u32[]{:S(2)}, u32[]{:S(2)}) collective-permute-start(bf16[512,256]{1,0:T(8,128)(2,1)S(1)} %get-tuple-element.16.rest_3_), channel_id=1, source_target_pairs={{0,2},{1,3},{2,0},{3,1},{4,6},{5,7},{6,4},{7,5},{8,10},{9,11},{10,... | collective-permute-start | bytes 786440 | tf_op jit(solution)/shard_map/ppermute | solution.py:28
  51.0 0.4 collective-permute-start.26
  51.4 2.4 %bwd_tile.1 = (bf16[512,256]{1,0:T(8,128)(2,1)S(1)}, bf16[512,256]{1,0:T(8,128)(2,1)S(1)}, bf16[512,256]{1,0:T(8,128)(2,1)S(1)}, bf16[512,256]{1,0:T(8,128)(2,1)S(1)}) custom-call(s32[32]{0:T(128)S(1)} %bitcast.7, s32[1]{0:T(128)} %bitcast.4.cnt_hbm, bf16[32,128,128]{2,1,0:T(8,128)(2,1)} %bitcast.10, bf16[512,256]{1,0:T(8,128)(2,1)} %rest_4_.1, ...), custom_call_target="tpu_custom_call" | custom-call | tf_op jit(solution)/shard_map/bwd_tile/pallas_call | solution.py:263
  53.9 1.5 %collective-permute-start.20 = (bf16[512,256]{1,0:T(8,128)(2,1)S(1)}, bf16[512,256]{1,0:T(8,128)(2,1)S(1)}, u32[]{:S(2)}, u32[]{:S(2)}) collective-permute-start(bf16[512,256]{1,0:T(8,128)(2,1)S(1)} %get-tuple-element.18), channel_id=1, source_target_pairs={{0,8},{1,9},{2,10},{3,11},{4,12},{5,13},{6,14},{7,15},{8,0},{9,1},... | collective-permute-start | bytes 786440 | tf_op jit(solution)/shard_map/ppermute | solution.py:28
  55.4 1.3 %collective-permute-done.26 = bf16[128,256]{1,0:T(8,128)(2,1)S(1)} collective-permute-done((bf16[128,256]{1,0:T(8,128)(2,1)S(1)}, bf16[128,256]{1,0:T(8,128)(2,1)S(1)}, u32[]{:S(2)}, u32[]{:S(2)}) %collective-permute-start.26) | collective-permute-done | bytes 65568 | tf_op jit(solution)/shard_map/ppermute | solution.py:28
  56.8 3.7 %collective-permute-start.27 = (bf16[128,256]{1,0:T(8,128)(2,1)S(1)}, bf16[128,256]{1,0:T(8,128)(2,1)S(1)}, u32[]{:S(2)}, u32[]{:S(2)}) collective-permute-start(bf16[128,256]{1,0:T(8,128)(2,1)S(1)} %add.22), channel_id=1, source_target_pairs={{0,4},{1,5},{2,6},{3,7},{4,0},{5,1},{6,2},{7,3},{8,12},{9,13},{10,... | collective-permute-start | bytes 196616 | tf_op jit(solution)/shard_map/ppermute | solution.py:28
  60.4 1.5 %collective-permute-start.21 = (bf16[512,256]{1,0:T(8,128)(2,1)S(1)}, bf16[512,256]{1,0:T(8,128)(2,1)S(1)}, u32[]{:S(2)}, u32[]{:S(2)}) collective-permute-start(bf16[512,256]{1,0:T(8,128)(2,1)S(1)} %get-tuple-element.19), channel_id=1, source_target_pairs={{0,16},{1,17},{2,18},{3,19},{4,20},{5,21},{6,22},{7,23},{8,24},{9,... | collective-permute-start | bytes 786440 | tf_op jit(solution)/shard_map/ppermute | solution.py:28
  61.9 1.4 %collective-permute-start.22 = (bf16[512,256]{1,0:T(8,128)(2,1)S(1)}, bf16[512,256]{1,0:T(8,128)(2,1)S(1)}, u32[]{:S(2)}, u32[]{:S(2)}) collective-permute-start(bf16[512,256]{1,0:T(8,128)(2,1)S(1)} %get-tuple-element.20), channel_id=1, source_target_pairs={{0,24},{1,25},{2,26},{3,27},{4,28},{5,29},{6,30},{7,31},{8,16},{9,... | collective-permute-start | bytes 786440 | tf_op jit(solution)/shard_map/ppermute | solution.py:28
  63.4 1.4 %collective-permute-start.10 = (bf16[512,256]{1,0:T(8,128)(2,1)S(1)}, bf16[512,256]{1,0:T(8,128)(2,1)S(1)}, u32[]{:S(2)}, u32[]{:S(2)}) collective-permute-start(bf16[512,256]{1,0:T(8,128)(2,1)S(1)} %get-tuple-element.14.rest_1_), channel_id=1, source_target_pairs={{0,2},{1,3},{2,0},{3,1},{4,6},{5,7},{6,4},{7,5},{8,10},{9,11},{10,... | collective-permute-start | bytes 786440 | tf_op jit(solution)/shard_map/ppermute | solution.py:28
  64.8 0.1 add.18
  64.9 0.0 copy-start.1
  64.9 1.4 %collective-permute-start.12 = (bf16[512,256]{1,0:T(8,128)(2,1)S(1)}, bf16[512,256]{1,0:T(8,128)(2,1)S(1)}, u32[]{:S(2)}, u32[]{:S(2)}) collective-permute-start(bf16[512,256]{1,0:T(8,128)(2,1)S(1)} %add.18), channel_id=1, source_target_pairs={{0,4},{1,5},{2,6},{3,7},{4,0},{5,1},{6,2},{7,3},{8,12},{9,13},{10,... | collective-permute-start | bytes 786440 | tf_op jit(solution)/shard_map/ppermute | solution.py:28
  66.3 0.1 collective-permute-start.28
  66.4 4.3 %collective-permute-done.21.rest_2_ = bf16[512,256]{1,0:T(8,128)(2,1)S(1)} collective-permute-done((bf16[512,256]{1,0:T(8,128)(2,1)S(1)}, bf16[512,256]{1,0:T(8,128)(2,1)S(1)}, u32[]{:S(2)}, u32[]{:S(2)}) %collective-permute-start.21) | collective-permute-done | bytes 262176 | tf_op jit(solution)/shard_map/ppermute | solution.py:28
  70.7 1.1 %input_grad.1 = bf16[512,256]{1,0:T(8,128)(2,1)} custom-call(bf16[256,256]{1,0:T(8,128)(2,1)S(1)} %copy-done.1, bf16[512,256]{1,0:T(8,128)(2,1)S(1)} %get-tuple-element.17.rest_0_, bf16[512,256]{1,0:T(8,128)(2,1)S(1)} %collective-permute-done.20.rest_1_, bf16[512,256]{1,0:T(8,128)(2,1)S(1)} %collective-permute-done.21.rest_2_, ...), custom_call_target="tpu_custom_call" | custom-call | tf_op jit(solution)/shard_map/input_grad/pallas_call | solution.py:280
  71.7 0.7 weight_grad.1
  72.5 3.1 %collective-permute-done.12.rest_2_ = bf16[512,256]{1,0:T(8,128)(2,1)S(1)} collective-permute-done((bf16[512,256]{1,0:T(8,128)(2,1)S(1)}, bf16[512,256]{1,0:T(8,128)(2,1)S(1)}, u32[]{:S(2)}, u32[]{:S(2)}) %collective-permute-start.12) | collective-permute-done | bytes 262176 | tf_op jit(solution)/shard_map/ppermute | solution.py:28
  75.6 1.0 %hidden.1 = bf16[512,256]{1,0:T(8,128)(2,1)} custom-call(bf16[256,256]{1,0:T(8,128)(2,1)S(1)} %copy-done.1, bf16[512,256]{1,0:T(8,128)(2,1)S(1)} %get-tuple-element.13.rest_0_, bf16[512,256]{1,0:T(8,128)(2,1)S(1)} %collective-permute-done.10.rest_1_, bf16[512,256]{1,0:T(8,128)(2,1)S(1)} %collective-permute-done.12.rest_2_), custom_call_target="tpu_custom_call" | custom-call | tf_op jit(solution)/shard_map/hidden/pallas_call | solution.py:254
  (28 shorter events, 0.2 us)
Async XLA Ops:
  0.6 4.6 %copy-start.2 = (s32[1,1,32]{2,1,0:T(1,128)S(1)}, s32[1,1,32]{2,1,0:T(1,128)}, u32[]{:S(2)}) copy-start(s32[1,1,32]{2,1,0:T(1,128)} %param.9) | copy-start | bytes 388
  0.6 27.7 %collective-permute-start.2 = (bf16[32,128,128]{2,1,0:T(8,128)(2,1)}, bf16[32,128,128]{2,1,0:T(8,128)(2,1)S(1)}, u32[]{:S(2)}, u32[]{:S(2)}) collective-permute-start(bf16[32,128,128]{2,1,0:T(8,128)(2,1)} %bitcast.8), channel_id=1, source_target_pairs={{0,1},{1,0},{2,3},{3,2},{4,5},{5,4},{6,7},{7,6},{8,9},{9,8},{10,11... | collective-permute-start | bytes 3145736 | tf_op jit(solution)/shard_map/ppermute | solution.py:28
  1.2 9.9 %collective-permute-start.3 = (bf16[512,256]{1,0:T(8,128)(2,1)}, bf16[512,256]{1,0:T(8,128)(2,1)S(1)}, u32[]{:S(2)}, u32[]{:S(2)}) collective-permute-start(bf16[512,256]{1,0:T(8,128)(2,1)} %rest_0_.2), channel_id=1, source_target_pairs={{0,8},{1,9},{2,10},{3,11},{4,12},{5,13},{6,14},{7,15},{8,0},{9,1},... | collective-permute-start | bytes 786440 | tf_op jit(solution)/shard_map/ppermute | solution.py:28
  3.8 14.2 %collective-permute-start.4 = (bf16[512,256]{1,0:T(8,128)(2,1)}, bf16[512,256]{1,0:T(8,128)(2,1)S(1)}, u32[]{:S(2)}, u32[]{:S(2)}) collective-permute-start(bf16[512,256]{1,0:T(8,128)(2,1)} %rest_0_.2), channel_id=1, source_target_pairs={{0,16},{1,17},{2,18},{3,19},{4,20},{5,21},{6,22},{7,23},{8,24},{9,... | collective-permute-start | bytes 786440 | tf_op jit(solution)/shard_map/ppermute | solution.py:28
  5.3 2.2 %collective-permute-start = (s32[32]{0:T(128)S(1)}, s32[32]{0:T(128)S(1)}, u32[]{:S(2)}, u32[]{:S(2)}) collective-permute-start(s32[32]{0:T(128)S(1)} %bitcast.5), channel_id=1, source_target_pairs={{0,1},{1,0},{2,3},{3,2},{4,5},{5,4},{6,7},{7,6},{8,9},{9,8},{10,11... | collective-permute-start | bytes 392 | tf_op jit(solution)/shard_map/ppermute | solution.py:28
  5.3 1.5 %collective-permute-start.1 = (s32[1]{0:T(128)}, s32[1]{0:T(128)}, u32[]{:S(2)}, u32[]{:S(2)}) collective-permute-start(s32[1]{0:T(128)} %bitcast.1), channel_id=1, source_target_pairs={{0,1},{1,0},{2,3},{3,2},{4,5},{5,4},{6,7},{7,6},{8,9},{9,8},{10,11... | collective-permute-start | bytes 20 | tf_op jit(solution)/shard_map/ppermute | solution.py:28
  6.7 11.2 %collective-permute-start.5 = (bf16[512,256]{1,0:T(8,128)(2,1)}, bf16[512,256]{1,0:T(8,128)(2,1)S(1)}, u32[]{:S(2)}, u32[]{:S(2)}) collective-permute-start(bf16[512,256]{1,0:T(8,128)(2,1)} %rest_0_.2), channel_id=1, source_target_pairs={{0,24},{1,25},{2,26},{3,27},{4,28},{5,29},{6,30},{7,31},{8,16},{9,... | collective-permute-start | bytes 786440 | tf_op jit(solution)/shard_map/ppermute | solution.py:28
  7.5 11.0 %collective-permute-start.6 = (bf16[512,256]{1,0:T(8,128)(2,1)}, bf16[512,256]{1,0:T(8,128)(2,1)S(1)}, u32[]{:S(2)}, u32[]{:S(2)}) collective-permute-start(bf16[512,256]{1,0:T(8,128)(2,1)} %rest_0_.2), channel_id=1, source_target_pairs={{0,1},{1,0},{2,3},{3,2},{4,5},{5,4},{6,7},{7,6},{8,9},{9,8},{10,11... | collective-permute-start | bytes 786440 | tf_op jit(solution)/shard_map/ppermute | solution.py:28
  11.1 14.5 %collective-permute-start.16 = (bf16[512,256]{1,0:T(8,128)(2,1)}, bf16[512,256]{1,0:T(8,128)(2,1)S(1)}, u32[]{:S(2)}, u32[]{:S(2)}) collective-permute-start(bf16[512,256]{1,0:T(8,128)(2,1)} %rest_4_.1), channel_id=1, source_target_pairs={{0,4},{1,5},{2,6},{3,7},{4,0},{5,1},{6,2},{7,3},{8,12},{9,13},{10,... | collective-permute-start | bytes 786440 | tf_op jit(solution)/shard_map/ppermute | solution.py:28
  17.9 8.5 %collective-permute-start.7 = (bf16[512,256]{1,0:T(8,128)(2,1)S(1)}, bf16[512,256]{1,0:T(8,128)(2,1)S(1)}, u32[]{:S(2)}, u32[]{:S(2)}) collective-permute-start(bf16[512,256]{1,0:T(8,128)(2,1)S(1)} %collective-permute-done.3.rest_1_), channel_id=1, source_target_pairs={{0,1},{1,0},{2,3},{3,2},{4,5},{5,4},{6,7},{7,6},{8,9},{9,8},{10,11... | collective-permute-start | bytes 786440 | tf_op jit(solution)/shard_map/ppermute | solution.py:28
  17.9 10.4 %collective-permute-start.8 = (bf16[512,256]{1,0:T(8,128)(2,1)S(1)}, bf16[512,256]{1,0:T(8,128)(2,1)S(1)}, u32[]{:S(2)}, u32[]{:S(2)}) collective-permute-start(bf16[512,256]{1,0:T(8,128)(2,1)S(1)} %collective-permute-done.4.rest_2_), channel_id=1, source_target_pairs={{0,1},{1,0},{2,3},{3,2},{4,5},{5,4},{6,7},{7,6},{8,9},{9,8},{10,11... | collective-permute-start | bytes 786440 | tf_op jit(solution)/shard_map/ppermute | solution.py:28
  18.5 9.9 %collective-permute-start.9 = (bf16[512,256]{1,0:T(8,128)(2,1)S(1)}, bf16[512,256]{1,0:T(8,128)(2,1)S(1)}, u32[]{:S(2)}, u32[]{:S(2)}) collective-permute-start(bf16[512,256]{1,0:T(8,128)(2,1)S(1)} %collective-permute-done.5.rest_3_), channel_id=1, source_target_pairs={{0,1},{1,0},{2,3},{3,2},{4,5},{5,4},{6,7},{7,6},{8,9},{9,8},{10,11... | collective-permute-start | bytes 786440 | tf_op jit(solution)/shard_map/ppermute | solution.py:28
  25.7 9.4 %collective-permute-start.14 = (bf16[512,256]{1,0:T(8,128)(2,1)}, bf16[512,256]{1,0:T(8,128)(2,1)S(1)}, u32[]{:S(2)}, u32[]{:S(2)}) collective-permute-start(bf16[512,256]{1,0:T(8,128)(2,1)} %rest_4_.1), channel_id=1, source_target_pairs={{0,2},{1,3},{2,0},{3,1},{4,6},{5,7},{6,4},{7,5},{8,10},{9,11},{10,... | collective-permute-start | bytes 786440 | tf_op jit(solution)/shard_map/ppermute | solution.py:28
  26.4 12.3 %collective-permute-start.18 = (bf16[512,256]{1,0:T(8,128)(2,1)S(1)}, bf16[512,256]{1,0:T(8,128)(2,1)S(1)}, u32[]{:S(2)}, u32[]{:S(2)}) collective-permute-start(bf16[512,256]{1,0:T(8,128)(2,1)S(1)} %collective-permute-done.16.rest_4_.rest_6_), channel_id=1, source_target_pairs={{0,2},{1,3},{2,0},{3,1},{4,6},{5,7},{6,4},{7,5},{8,10},{9,11},{10,... | collective-permute-start | bytes 786440 | tf_op jit(solution)/shard_map/ppermute | solution.py:28
  28.4 10.4 %copy-start = (bf16[512,256]{1,0:T(8,128)(2,1)S(1)}, bf16[512,256]{1,0:T(8,128)(2,1)}, u32[]{:S(2)}) copy-start(bf16[512,256]{1,0:T(8,128)(2,1)} %rest_4_.1) | copy-start | bytes 786436
  39.2 1.3 %collective-permute-start.23 = (bf16[128,256]{1,0:T(8,128)(2,1)S(1)}, bf16[128,256]{1,0:T(8,128)(2,1)S(1)}, u32[]{:S(2)}, u32[]{:S(2)}) collective-permute-start(bf16[128,256]{1,0:T(8,128)(2,1)S(1)} %get-tuple-element.22), channel_id=1, source_target_pairs={{0,1},{1,0},{2,3},{3,2},{4,5},{5,4},{6,7},{7,6},{8,9},{9,8},{10,11... | collective-permute-start | bytes 196616 | tf_op jit(solution)/shard_map/ppermute | solution.py:28
  40.6 4.3 %collective-permute-start.24 = (bf16[128,256]{1,0:T(8,128)(2,1)S(1)}, bf16[128,256]{1,0:T(8,128)(2,1)S(1)}, u32[]{:S(2)}, u32[]{:S(2)}) collective-permute-start(bf16[128,256]{1,0:T(8,128)(2,1)S(1)} %add.19), channel_id=1, source_target_pairs={{0,8},{1,9},{2,10},{3,11},{4,12},{5,13},{6,14},{7,15},{8,0},{9,1},... | collective-permute-start | bytes 196616 | tf_op jit(solution)/shard_map/ppermute | solution.py:28
  42.1 8.9 %collective-permute-start.13 = (bf16[512,256]{1,0:T(8,128)(2,1)S(1)}, bf16[512,256]{1,0:T(8,128)(2,1)S(1)}, u32[]{:S(2)}, u32[]{:S(2)}) collective-permute-start(bf16[512,256]{1,0:T(8,128)(2,1)S(1)} %copy-done), channel_id=1, source_target_pairs={{0,1},{1,0},{2,3},{3,2},{4,5},{5,4},{6,7},{7,6},{8,9},{9,8},{10,11... | collective-permute-start | bytes 786440 | tf_op jit(solution)/shard_map/ppermute | solution.py:28
  42.1 9.3 %collective-permute-start.17 = (bf16[512,256]{1,0:T(8,128)(2,1)S(1)}, bf16[512,256]{1,0:T(8,128)(2,1)S(1)}, u32[]{:S(2)}, u32[]{:S(2)}) collective-permute-start(bf16[512,256]{1,0:T(8,128)(2,1)S(1)} %collective-permute-done.16.rest_4_.rest_6_), channel_id=1, source_target_pairs={{0,1},{1,0},{2,3},{3,2},{4,5},{5,4},{6,7},{7,6},{8,9},{9,8},{10,11... | collective-permute-start | bytes 786440 | tf_op jit(solution)/shard_map/ppermute | solution.py:28
  42.6 8.8 %collective-permute-start.15 = (bf16[512,256]{1,0:T(8,128)(2,1)S(1)}, bf16[512,256]{1,0:T(8,128)(2,1)S(1)}, u32[]{:S(2)}, u32[]{:S(2)}) collective-permute-start(bf16[512,256]{1,0:T(8,128)(2,1)S(1)} %collective-permute-done.14.rest_2_.rest_5_), channel_id=1, source_target_pairs={{0,1},{1,0},{2,3},{3,2},{4,5},{5,4},{6,7},{7,6},{8,9},{9,8},{10,11... | collective-permute-start | bytes 786440 | tf_op jit(solution)/shard_map/ppermute | solution.py:28
  42.7 8.8 %collective-permute-start.19 = (bf16[512,256]{1,0:T(8,128)(2,1)S(1)}, bf16[512,256]{1,0:T(8,128)(2,1)S(1)}, u32[]{:S(2)}, u32[]{:S(2)}) collective-permute-start(bf16[512,256]{1,0:T(8,128)(2,1)S(1)} %collective-permute-done.18.rest_6_.rest_7_), channel_id=1, source_target_pairs={{0,1},{1,0},{2,3},{3,2},{4,5},{5,4},{6,7},{7,6},{8,9},{9,8},{10,11... | collective-permute-start | bytes 786440 | tf_op jit(solution)/shard_map/ppermute | solution.py:28
  44.9 4.3 %collective-permute-start.25 = (bf16[128,256]{1,0:T(8,128)(2,1)S(1)}, bf16[128,256]{1,0:T(8,128)(2,1)S(1)}, u32[]{:S(2)}, u32[]{:S(2)}) collective-permute-start(bf16[128,256]{1,0:T(8,128)(2,1)S(1)} %add.20), channel_id=1, source_target_pairs={{0,16},{1,17},{2,18},{3,19},{4,20},{5,21},{6,22},{7,23},{8,24},{9,... | collective-permute-start | bytes 196616 | tf_op jit(solution)/shard_map/ppermute | solution.py:28
  49.3 14.1 %collective-permute-start.11 = (bf16[512,256]{1,0:T(8,128)(2,1)S(1)}, bf16[512,256]{1,0:T(8,128)(2,1)S(1)}, u32[]{:S(2)}, u32[]{:S(2)}) collective-permute-start(bf16[512,256]{1,0:T(8,128)(2,1)S(1)} %get-tuple-element.16.rest_3_), channel_id=1, source_target_pairs={{0,2},{1,3},{2,0},{3,1},{4,6},{5,7},{6,4},{7,5},{8,10},{9,11},{10,... | collective-permute-start | bytes 786440 | tf_op jit(solution)/shard_map/ppermute | solution.py:28
  51.0 5.7 %collective-permute-start.26 = (bf16[128,256]{1,0:T(8,128)(2,1)S(1)}, bf16[128,256]{1,0:T(8,128)(2,1)S(1)}, u32[]{:S(2)}, u32[]{:S(2)}) collective-permute-start(bf16[128,256]{1,0:T(8,128)(2,1)S(1)} %add.21), channel_id=1, source_target_pairs={{0,2},{1,3},{2,0},{3,1},{4,6},{5,7},{6,4},{7,5},{8,10},{9,11},{10,... | collective-permute-start | bytes 196616 | tf_op jit(solution)/shard_map/ppermute | solution.py:28
  53.9 12.5 %collective-permute-start.20 = (bf16[512,256]{1,0:T(8,128)(2,1)S(1)}, bf16[512,256]{1,0:T(8,128)(2,1)S(1)}, u32[]{:S(2)}, u32[]{:S(2)}) collective-permute-start(bf16[512,256]{1,0:T(8,128)(2,1)S(1)} %get-tuple-element.18), channel_id=1, source_target_pairs={{0,8},{1,9},{2,10},{3,11},{4,12},{5,13},{6,14},{7,15},{8,0},{9,1},... | collective-permute-start | bytes 786440 | tf_op jit(solution)/shard_map/ppermute | solution.py:28
  56.8 8.1 %collective-permute-start.27 = (bf16[128,256]{1,0:T(8,128)(2,1)S(1)}, bf16[128,256]{1,0:T(8,128)(2,1)S(1)}, u32[]{:S(2)}, u32[]{:S(2)}) collective-permute-start(bf16[128,256]{1,0:T(8,128)(2,1)S(1)} %add.22), channel_id=1, source_target_pairs={{0,4},{1,5},{2,6},{3,7},{4,0},{5,1},{6,2},{7,3},{8,12},{9,13},{10,... | collective-permute-start | bytes 196616 | tf_op jit(solution)/shard_map/ppermute | solution.py:28
  60.4 10.2 %collective-permute-start.21 = (bf16[512,256]{1,0:T(8,128)(2,1)S(1)}, bf16[512,256]{1,0:T(8,128)(2,1)S(1)}, u32[]{:S(2)}, u32[]{:S(2)}) collective-permute-start(bf16[512,256]{1,0:T(8,128)(2,1)S(1)} %get-tuple-element.19), channel_id=1, source_target_pairs={{0,16},{1,17},{2,18},{3,19},{4,20},{5,21},{6,22},{7,23},{8,24},{9,... | collective-permute-start | bytes 786440 | tf_op jit(solution)/shard_map/ppermute | solution.py:28
  61.9 8.7 %collective-permute-start.22 = (bf16[512,256]{1,0:T(8,128)(2,1)S(1)}, bf16[512,256]{1,0:T(8,128)(2,1)S(1)}, u32[]{:S(2)}, u32[]{:S(2)}) collective-permute-start(bf16[512,256]{1,0:T(8,128)(2,1)S(1)} %get-tuple-element.20), channel_id=1, source_target_pairs={{0,24},{1,25},{2,26},{3,27},{4,28},{5,29},{6,30},{7,31},{8,16},{9,... | collective-permute-start | bytes 786440 | tf_op jit(solution)/shard_map/ppermute | solution.py:28
  63.4 9.1 %collective-permute-start.10 = (bf16[512,256]{1,0:T(8,128)(2,1)S(1)}, bf16[512,256]{1,0:T(8,128)(2,1)S(1)}, u32[]{:S(2)}, u32[]{:S(2)}) collective-permute-start(bf16[512,256]{1,0:T(8,128)(2,1)S(1)} %get-tuple-element.14.rest_1_), channel_id=1, source_target_pairs={{0,2},{1,3},{2,0},{3,1},{4,6},{5,7},{6,4},{7,5},{8,10},{9,11},{10,... | collective-permute-start | bytes 786440 | tf_op jit(solution)/shard_map/ppermute | solution.py:28
  64.9 5.8 %copy-start.1 = (bf16[256,256]{1,0:T(8,128)(2,1)S(1)}, bf16[256,256]{1,0:T(8,128)(2,1)}, u32[]{:S(2)}) copy-start(bf16[256,256]{1,0:T(8,128)(2,1)} %w.3) | copy-start | bytes 393220
  64.9 10.7 %collective-permute-start.12 = (bf16[512,256]{1,0:T(8,128)(2,1)S(1)}, bf16[512,256]{1,0:T(8,128)(2,1)S(1)}, u32[]{:S(2)}, u32[]{:S(2)}) collective-permute-start(bf16[512,256]{1,0:T(8,128)(2,1)S(1)} %add.18), channel_id=1, source_target_pairs={{0,4},{1,5},{2,6},{3,7},{4,0},{5,1},{6,2},{7,3},{8,12},{9,13},{10,... | collective-permute-start | bytes 786440 | tf_op jit(solution)/shard_map/ppermute | solution.py:28
  66.3 5.4 %collective-permute-start.28 = (bf16[128,256]{1,0:T(8,128)(2,1)S(1)}, bf16[128,256]{1,0:T(8,128)(2,1)S(1)}, u32[]{:S(2)}, u32[]{:S(2)}) collective-permute-start(bf16[128,256]{1,0:T(8,128)(2,1)S(1)} %add.23.mine), channel_id=1, source_target_pairs={{0,1},{1,0},{2,3},{3,2},{4,5},{5,4},{6,7},{7,6},{8,9},{9,8},{10,11... | collective-permute-start | bytes 196616 | tf_op jit(solution)/shard_map/ppermute | solution.py:28
